TPU v7x, 32 devices: a whole 2x2x4 slice. The times are simulated.
32 devices in a mesh: lon: 8 (over z, y), lat: 4 (over x, core).
Axes of the slice: x: 2, y: 2, z: 4, core: 2. Of those that a mesh axis runs over, the one named last changes fastest.
Arguments:
- surface_adjoint: float32 [1024, 8192], P('lat', 'lon'), may hold values from -6 to 6
- east_adjoint: float32 [1024, 8192], P('lat', 'lon'), may hold values from -6 to 6
- north_adjoint: float32 [1024, 8192], P('lat', 'lon'), may hold values from -6 to 6
- water_depth: float32 [1024, 8192], P('lat', 'lon'), may hold values from 0.3 to 1
- wet_mask: int32 [1024, 8192], P('lat', 'lon'), may hold values 0 or 1
- control_active: int32 [64, 512], P('lat', 'lon'), may hold values 0 or 1
Outputs:
- surface_after: float32 [1024, 8192], P('lat', 'lon')
- east_after: float32 [1024, 8192], P('lat', 'lon')
- north_after: float32 [1024, 8192], P('lat', 'lon')
- uplift_grad: float32 [64, 512], P('lat', 'lon')
All inputs are finite; a program needn't handle non-finite values. No bound on the sum of `wet_mask` or of `control_active` on one device may be relied on, other than what follows from the above.
Results may differ from a plain program's by a relative error of at most 0.00021.
Values sent between devices are 32-bit elements; how exact they have to be, the bound alone decides.
No kernel may reach another device: no remote copies, remote signals or barrier semaphores. Data moves between devices by JAX's collectives and lax.ppermute only.
A program may use at most 64 MiB of HBM per device.

v0:
```python
import jax
import jax.numpy as jnp
from jax import lax
from jax.sharding import PartitionSpec as P

SPACING = 16
STEPS = 3


courant = 0.5


def with_halo(array, sides, width):
    for axis, dim in sides:
        size, length = (lax.axis_size(axis), array.shape[dim])
        up = [(i, (i + 1) % size) for i in range(size - 1)]
        down = [(j, i) for i, j in up]
        last = lax.slice_in_dim(array, length - width, length, axis=dim)
        initial = lax.slice_in_dim(array, 0, width, axis=dim)
        before = lax.ppermute(last, axis, up)
        after = lax.ppermute(initial, axis, down)
        array = jnp.concatenate([before, array, after], axis=dim)
    return array


def from_east(field):
    return jnp.pad(field[:, 1:], ((0, 0), (0, 1)))


def west_incoming(field):
    return jnp.pad(field[:, :-1], ((0, 0), (1, 0)))


def from_north(field):
    return jnp.pad(field[1:, :], ((0, 1), (0, 0)))


def from_south(field):
    return jnp.pad(field[:-1, :], ((1, 0), (0, 0)))


def march_steps(surface_height, eastward, northward, wet_depth, wet_fraction):
    for step in range(STEPS):
        eastward = wet_fraction * (
            eastward
            + courant * wet_depth * (from_east(surface_height) - west_incoming(surface_height))
        )
        northward = wet_fraction * (
            northward
            + courant * wet_depth * (from_north(surface_height) - from_south(surface_height))
        )
        surface_height = wet_fraction * (
            surface_height
            + courant
            * (
                from_east(eastward)
                - west_incoming(eastward)
                + (from_north(northward) - from_south(northward))
            )
        )
    return (surface_height, eastward, northward)


def spline_weight(arg):
    mag = jnp.abs(arg)
    inner = 2.0 / 3.0 - mag * mag + 0.5 * mag * mag * mag
    outer = (2.0 - mag) * (2.0 - mag) * (2.0 - mag) / 6.0
    return jnp.where(mag < 1.0, inner, jnp.where(mag < 2.0, outer, 0.0 * mag))


def spline_table(cells, points):
    rows = (jnp.arange(cells, dtype=jnp.float32)[:, None] + 0.5) / SPACING
    cols = jnp.arange(points + 4, dtype=jnp.float32)[None, :] - 2.0 + 0.5
    return spline_weight(rows - cols)


def fold_columns(extended):
    folded = extended[:, 4:-4]
    folded = folded.at[:, 0:2].add(extended[:, 0:2])
    folded = folded.at[:, -2:].add(extended[:, -2:])
    return folded


def fold_rows(extended):
    folded = extended[4:-4]
    folded = folded.at[0:2].add(extended[0:2])
    folded = folded.at[-2:].add(extended[-2:])
    return folded


def local(surface_adjoint, east_adjoint, north_adjoint, water_depth, wet_mask, control_active):
    wet_fraction = wet_mask.astype(jnp.float32)
    wet_depth = water_depth * wet_fraction
    surface_height, eastward, northward = (surface_adjoint, east_adjoint, north_adjoint)
    reach = 2 * STEPS
    wide_surface, wide_east, wide_north, wide_depth = (
        with_halo(surface_height, (("lon", 1), ("lat", 0)), reach),
        with_halo(eastward, (("lon", 1), ("lat", 0)), reach),
        with_halo(northward, (("lon", 1), ("lat", 0)), reach),
        with_halo(wet_depth, (("lon", 1), ("lat", 0)), reach),
    )
    wide_wet = jnp.where(wide_depth > 0.0, 1.0, 0.0).astype(jnp.float32)
    wide_surface, wide_east, wide_north = march_steps(
        wide_surface, wide_east, wide_north, wide_depth, wide_wet
    )
    surface_height = wide_surface[reach:-reach, reach:-reach]
    eastward = wide_east[reach:-reach, reach:-reach]
    northward = wide_north[reach:-reach, reach:-reach]
    lat_cells, longitude_cells = surface_height.shape
    lat_points = lat_cells // SPACING
    lon_points = longitude_cells // SPACING
    lat_table = spline_table(lat_cells, lat_points)
    lon_table = spline_table(longitude_cells, lon_points)
    reduced = jnp.dot(
        lat_table.T,
        surface_height,
        precision=lax.Precision.HIGHEST,
        preferred_element_type=jnp.float32,
    )
    partial_value = jnp.dot(
        reduced, lon_table, precision=lax.Precision.HIGHEST, preferred_element_type=jnp.float32
    )
    extended = with_halo(partial_value, (("lon", 1), ("lat", 0)), 2)
    sums = fold_columns(fold_rows(extended))
    uplift_grad = sums * control_active.astype(jnp.float32) / SPACING
    return (surface_height, eastward, northward, uplift_grad)


def solution(mesh):
    return jax.shard_map(
        local,
        mesh=mesh,
        in_specs=(
            P("lat", "lon"),
            P("lat", "lon"),
            P("lat", "lon"),
            P("lat", "lon"),
            P("lat", "lon"),
            P("lat", "lon"),
        ),
        out_specs=(P("lat", "lon"), P("lat", "lon"), P("lat", "lon"), P("lat", "lon")),
        check_vma=False,
    )
```

profile of v0, /device:TPU:5, one launch (start us, length us, event | category | flops | bytes accessed | tf_op | source)
XLA Modules:
  0.0 106.3 jit_solution(1969071307287319158)
XLA Ops:
  0.6 1.1 fusion.83
  1.7 3.1 %collective-permute-start.4 = (f32[256,6]{1,0:T(8,128)S(1)}, f32[256,6]{1,0:T(8,128)S(1)}, u32[]{:S(2)}, u32[]{:S(2)}) collective-permute-start(f32[256,6]{1,0:T(8,128)S(1)} %get-tuple-element.95), channel_id=1, source_target_pairs={{0,4},{4,8},{8,12},{12,16},{16,20},{20,24},{24,28},{1,5},{5,9},{9,... | collective-permute-start | bytes 18440 | tf_op jit(solution)/shard_map/ppermute | solution.py:20
  4.9 2.1 %collective-permute-start.5 = (f32[256,6]{1,0:T(8,128)S(1)}, f32[256,6]{1,0:T(8,128)S(1)}, u32[]{:S(2)}, u32[]{:S(2)}) collective-permute-start(f32[256,6]{1,0:T(8,128)S(1)} %get-tuple-element.94), channel_id=1, source_target_pairs={{4,0},{8,4},{12,8},{16,12},{20,16},{24,20},{28,24},{5,1},{9,5},{13... | collective-permute-start | bytes 18440 | tf_op jit(solution)/shard_map/ppermute | solution.py:21
  7.0 1.7 %convert_multiply_fusion = f32[256,1024]{1,0:T(8,128)S(1)} fusion(f32[256,1024]{1,0:T(8,128)} %param.17, s32[256,1024]{1,0:T(8,128)} %param.18), kind=kLoop, calls=%fused_computation.18 | loop fusion | flops 524288 | bytes 3145728 | tf_op jit(solution)/shard_map/mul | solution.py:93
  8.7 0.7 fusion.82
  9.5 4.0 %collective-permute-start = (f32[256,6]{1,0:T(8,128)}, f32[256,6]{1,0:T(8,128)S(1)}, u32[]{:S(2)}, u32[]{:S(2)}) collective-permute-start(f32[256,6]{1,0:T(8,128)} %get-tuple-element.93), channel_id=1, source_target_pairs={{0,4},{4,8},{8,12},{12,16},{16,20},{20,24},{24,28},{1,5},{5,9},{9,... | collective-permute-start | bytes 18440 | tf_op jit(solution)/shard_map/ppermute | solution.py:20
  13.5 1.9 %collective-permute-start.1 = (f32[256,6]{1,0:T(8,128)}, f32[256,6]{1,0:T(8,128)}, u32[]{:S(2)}, u32[]{:S(2)}) collective-permute-start(f32[256,6]{1,0:T(8,128)} %get-tuple-element.92), channel_id=1, source_target_pairs={{4,0},{8,4},{12,8},{16,12},{20,16},{24,20},{28,24},{5,1},{9,5},{13... | collective-permute-start | bytes 18440 | tf_op jit(solution)/shard_map/ppermute | solution.py:21
  15.4 1.7 %fusion.84 = (f32[256,6]{1,0:T(8,128)}, f32[256,6]{1,0:T(8,128)}) fusion(f32[256,1024]{1,0:T(8,128)} %param.15), kind=kLoop, calls=%fused_computation.112 | loop fusion | bytes 24576 | tf_op jit(solution)/shard_map/slice | solution.py:19
  17.2 4.2 %collective-permute-start.8 = (f32[256,6]{1,0:T(8,128)}, f32[256,6]{1,0:T(8,128)S(1)}, u32[]{:S(2)}, u32[]{:S(2)}) collective-permute-start(f32[256,6]{1,0:T(8,128)} %get-tuple-element.97), channel_id=1, source_target_pairs={{0,4},{4,8},{8,12},{12,16},{16,20},{20,24},{24,28},{1,5},{5,9},{9,... | collective-permute-start | bytes 18440 | tf_op jit(solution)/shard_map/ppermute | solution.py:20
  21.5 1.7 %fusion.81 = (f32[256,6]{1,0:T(8,128)}, f32[256,6]{1,0:T(8,128)}) fusion(f32[256,1024]{1,0:T(8,128)} %param.16), kind=kLoop, calls=%fused_computation.109 | loop fusion | bytes 24576 | tf_op jit(solution)/shard_map/slice | solution.py:19
  23.2 0.6 compare_reduce_fusion
  23.8 1.9 %collective-permute-start.9 = (f32[256,6]{1,0:T(8,128)}, f32[256,6]{1,0:T(8,128)}, u32[]{:S(2)}, u32[]{:S(2)}) collective-permute-start(f32[256,6]{1,0:T(8,128)} %get-tuple-element.96), channel_id=1, source_target_pairs={{4,0},{8,4},{12,8},{16,12},{20,16},{24,20},{28,24},{5,1},{9,5},{13... | collective-permute-start | bytes 18440 | tf_op jit(solution)/shard_map/ppermute | solution.py:21
  25.8 0.6 copy-done.6
  26.4 4.2 %collective-permute-start.12 = (f32[256,6]{1,0:T(8,128)}, f32[256,6]{1,0:T(8,128)}, u32[]{:S(2)}, u32[]{:S(2)}) collective-permute-start(f32[256,6]{1,0:T(8,128)} %get-tuple-element.91), channel_id=1, source_target_pairs={{0,4},{4,8},{8,12},{12,16},{16,20},{20,24},{24,28},{1,5},{5,9},{9,... | collective-permute-start | bytes 18440 | tf_op jit(solution)/shard_map/ppermute | solution.py:20
  30.7 1.6 %concatenate.37 = f32[256,1036]{1,0:T(8,128)S(1)} concatenate(f32[256,6]{1,0:T(8,128)} %copy-done.5, f32[256,1024]{1,0:T(8,128)S(1)} %copy-done.2, f32[256,6]{1,0:T(8,128)} %copy-done.6), dimensions={1} | concatenate | bytes 2121728 | tf_op jit(solution)/shard_map/concatenate | solution.py:22
  32.3 0.6 fusion.79
  32.9 1.9 %collective-permute-start.13 = (f32[256,6]{1,0:T(8,128)}, f32[256,6]{1,0:T(8,128)}, u32[]{:S(2)}, u32[]{:S(2)}) collective-permute-start(f32[256,6]{1,0:T(8,128)} %get-tuple-element.90), channel_id=1, source_target_pairs={{4,0},{8,4},{12,8},{16,12},{20,16},{24,20},{28,24},{5,1},{9,5},{13... | collective-permute-start | bytes 18440 | tf_op jit(solution)/shard_map/ppermute | solution.py:21
  34.9 5.6 %collective-permute-start.6 = (f32[6,1036]{1,0:T(8,128)}, f32[6,1036]{1,0:T(8,128)}, u32[]{:S(2)}, u32[]{:S(2)}) collective-permute-start(f32[6,1036]{1,0:T(8,128)} %get-tuple-element.86), channel_id=1, source_target_pairs={{0,1},{1,2},{2,3},{4,5},{5,6},{6,7},{8,9},{9,10},{10,11},{12,13},{... | collective-permute-start | bytes 74600 | tf_op jit(solution)/shard_map/ppermute | solution.py:20
  40.5 1.6 %concatenate.35 = f32[256,1036]{1,0:T(8,128)S(1)} concatenate(f32[256,6]{1,0:T(8,128)} %copy-done.4, f32[256,1024]{1,0:T(8,128)S(1)} %convert_multiply_fusion, f32[256,6]{1,0:T(8,128)} %collective-permute-done.1), dimensions={1} | concatenate | bytes 2121728 | tf_op jit(solution)/shard_map/concatenate | solution.py:22
  42.1 0.6 fusion.78
  42.8 1.9 %collective-permute-start.7 = (f32[6,1036]{1,0:T(8,128)}, f32[6,1036]{1,0:T(8,128)}, u32[]{:S(2)}, u32[]{:S(2)}) collective-permute-start(f32[6,1036]{1,0:T(8,128)} %get-tuple-element.87), channel_id=1, source_target_pairs={{1,0},{2,1},{3,2},{5,4},{6,5},{7,6},{9,8},{10,9},{11,10},{13,12},{... | collective-permute-start | bytes 74600 | tf_op jit(solution)/shard_map/ppermute | solution.py:21
  44.7 3.6 %collective-permute-start.2 = (f32[6,1036]{1,0:T(8,128)}, f32[6,1036]{1,0:T(8,128)}, u32[]{:S(2)}, u32[]{:S(2)}) collective-permute-start(f32[6,1036]{1,0:T(8,128)} %get-tuple-element.84), channel_id=1, source_target_pairs={{0,1},{1,2},{2,3},{4,5},{5,6},{6,7},{8,9},{9,10},{10,11},{12,13},{... | collective-permute-start | bytes 74600 | tf_op jit(solution)/shard_map/ppermute | solution.py:20
  48.3 1.7 %concatenate.39 = f32[256,1036]{1,0:T(8,128)S(1)} concatenate(f32[256,6]{1,0:T(8,128)} %copy-done.3, f32[256,1024]{1,0:T(8,128)} %param.15, f32[256,6]{1,0:T(8,128)} %collective-permute-done.9), dimensions={1} | concatenate | bytes 2121728 | tf_op jit(solution)/shard_map/concatenate | solution.py:22
  50.1 0.6 fusion.80
  50.7 1.9 %collective-permute-start.3 = (f32[6,1036]{1,0:T(8,128)}, f32[6,1036]{1,0:T(8,128)}, u32[]{:S(2)}, u32[]{:S(2)}) collective-permute-start(f32[6,1036]{1,0:T(8,128)} %get-tuple-element.85), channel_id=1, source_target_pairs={{1,0},{2,1},{3,2},{5,4},{6,5},{7,6},{9,8},{10,9},{11,10},{13,12},{... | collective-permute-start | bytes 74600 | tf_op jit(solution)/shard_map/ppermute | solution.py:21
  52.7 3.6 %collective-permute-start.10 = (f32[6,1036]{1,0:T(8,128)}, f32[6,1036]{1,0:T(8,128)}, u32[]{:S(2)}, u32[]{:S(2)}) collective-permute-start(f32[6,1036]{1,0:T(8,128)} %get-tuple-element.88), channel_id=1, source_target_pairs={{0,1},{1,2},{2,3},{4,5},{5,6},{6,7},{8,9},{9,10},{10,11},{12,13},{... | collective-permute-start | bytes 74600 | tf_op jit(solution)/shard_map/ppermute | solution.py:20
  56.3 2.4 %concatenate.41 = f32[256,1036]{1,0:T(8,128)} concatenate(f32[256,6]{1,0:T(8,128)} %collective-permute-done.12, f32[256,1024]{1,0:T(8,128)} %param.16, f32[256,6]{1,0:T(8,128)} %collective-permute-done.13), dimensions={1} | concatenate | bytes 2121728 | tf_op jit(solution)/shard_map/concatenate | solution.py:22
  58.7 0.8 fusion.77
  59.5 1.9 %collective-permute-start.11 = (f32[6,1036]{1,0:T(8,128)}, f32[6,1036]{1,0:T(8,128)S(1)}, u32[]{:S(2)}, u32[]{:S(2)}) collective-permute-start(f32[6,1036]{1,0:T(8,128)} %get-tuple-element.89), channel_id=1, source_target_pairs={{1,0},{2,1},{3,2},{5,4},{6,5},{7,6},{9,8},{10,9},{11,10},{13,12},{... | collective-permute-start | bytes 74600 | tf_op jit(solution)/shard_map/ppermute | solution.py:21
  61.4 3.6 %collective-permute-start.14 = (f32[6,1036]{1,0:T(8,128)S(1)}, f32[6,1036]{1,0:T(8,128)S(1)}, u32[]{:S(2)}, u32[]{:S(2)}) collective-permute-start(f32[6,1036]{1,0:T(8,128)S(1)} %get-tuple-element.82), channel_id=1, source_target_pairs={{0,1},{1,2},{2,3},{4,5},{5,6},{6,7},{8,9},{9,10},{10,11},{12,13},{... | collective-permute-start | bytes 74600 | tf_op jit(solution)/shard_map/ppermute | solution.py:20
  65.1 0.9 pad_maximum_fusion.1
  66.0 0.4 fusion.76
  66.4 0.2 fusion.75
  66.6 2.1 %collective-permute-start.15 = (f32[6,1036]{1,0:T(8,128)S(1)}, f32[6,1036]{1,0:T(8,128)S(1)}, u32[]{:S(2)}, u32[]{:S(2)}) collective-permute-start(f32[6,1036]{1,0:T(8,128)S(1)} %get-tuple-element.83), channel_id=1, source_target_pairs={{1,0},{2,1},{3,2},{5,4},{6,5},{7,6},{9,8},{10,9},{11,10},{13,12},{... | collective-permute-start | bytes 74600 | tf_op jit(solution)/shard_map/ppermute | solution.py:21
  68.7 1.7 %select_multiply_fusion.7 = (f32[268,1036]{1,0:T(8,128)S(1)}, pred[268,1036]{1,0:T(8,128)(4,1)S(1)}) fusion(f32[6,1036]{1,0:T(8,128)S(1)} %collective-permute-done.11, f32[256,1036]{1,0:T(8,128)S(1)} %concatenate.39, f32[6,1036]{1,0:T(8,128)} %collective-permute-done.10, f32[268,1035]{1,0:T(8,128)S(1)} %get-tuple-element.81, ...), kind=kLoop, calls=%fused_computation.7 | loop fusion | flops 3054128 | bytes 5828464 | tf_op jit(solution)/shard_map/mul | solution.py:44
  70.4 1.5 %collective-permute-done.15 = f32[6,1036]{1,0:T(8,128)S(1)} collective-permute-done((f32[6,1036]{1,0:T(8,128)S(1)}, f32[6,1036]{1,0:T(8,128)S(1)}, u32[]{:S(2)}, u32[]{:S(2)}) %collective-permute-start.15) | collective-permute-done | bytes 24896 | tf_op jit(solution)/shard_map/ppermute | solution.py:21
  71.8 1.4 %select_multiply_fusion.6 = f32[268,1036]{1,0:T(8,128)S(1)} fusion(pred[268,1036]{1,0:T(8,128)(4,1)S(1)} %get-tuple-element.53, f32[6,1036]{1,0:T(8,128)S(1)} %collective-permute-done.15, f32[256,1036]{1,0:T(8,128)S(1)} %copy-done, f32[6,1036]{1,0:T(8,128)S(1)} %collective-permute-done.14, f32[267,1036]{1,0:T(8,128)S(1)} %get-tuple-element.79, ...), kind=kLoop, calls=%fused_computation.6 | loop fusion | flops 2776480 | bytes 5822320 | tf_op jit(solution)/shard_map/mul | solution.py:48
  73.3 0.2 fusion.74
  73.5 0.4 fusion.73
  73.9 1.6 %select_multiply_fusion.5 = f32[268,1036]{1,0:T(8,128)S(1)} fusion(pred[268,1036]{1,0:T(8,128)(4,1)S(1)} %get-tuple-element.53, f32[267,1036]{1,0:T(8,128)S(1)} %get-tuple-element.77, f32[267,1036]{1,0:T(8,128)S(1)} %get-tuple-element.76, f32[268,1035]{1,0:T(8,128)S(1)} %get-tuple-element.75, f32[268,1035]{1,0:T(8,128)S(1)} %get-tuple-element.74, ...), kind=kLoop, calls=%fused_computation.5 | loop fusion | flops 2498832 | bytes 6930768 | tf_op jit(solution)/shard_map/mul | solution.py:52
  75.4 0.4 fusion.70
  76.0 1.7 %select_multiply_fusion.4 = (f32[268,1036]{1,0:T(8,128)S(1)}, f32[268,1036]{1,0:T(8,128)S(1)}) fusion(pred[268,1036]{1,0:T(8,128)(4,1)S(1)} %get-tuple-element.53, f32[268,1036]{1,0:T(8,128)S(1)} %get-tuple-element.52, f32[268,1035]{1,0:T(8,128)S(1)} %get-tuple-element.69, f32[268,1035]{1,0:T(8,128)S(1)} %get-tuple-element.68, ...), kind=kLoop, calls=%fused_computation.4 | loop fusion | flops 3331776 | bytes 10262544 | tf_op jit(solution)/shard_map/mul | solution.py:44
  77.7 0.4 fusion.69
  78.1 0.2 fusion.71
  78.3 0.7 select_multiply_fusion.2
  79.0 0.4 fusion.66
  79.4 0.2 fusion.68
  79.6 1.7 %select_multiply_fusion.1 = (f32[268,1036]{1,0:T(8,128)S(1)}, f32[268,1036]{1,0:T(8,128)S(1)}, f32[268,1036]{1,0:T(8,128)S(1)}) fusion(pred[268,1036]{1,0:T(8,128)(4,1)S(1)} %get-tuple-element.53, f32[268,1036]{1,0:T(8,128)S(1)} %get-tuple-element.56, f32[268,1035]{1,0:T(8,128)S(1)} %get-tuple-element.61, f32[268,1035]{1,0:T(8,128)S(1)} %get-tuple-element.60, ...), kind=kLoop, calls=%fused_computation.1 | loop fusion | flops 3331776 | bytes 11373136 | tf_op jit(solution)/shard_map/mul | solution.py:44
  81.3 0.4 fusion.65
  81.7 0.2 fusion.67
  81.9 2.5 %slice_multiply_fusion = f32[256,1024]{1,0:T(8,128)S(1)} fusion(f32[268,1036]{1,0:T(8,128)S(1)} %get-tuple-element.98, f32[268,1036]{1,0:T(8,128)S(1)} %select_multiply_fusion.2, f32[267,1036]{1,0:T(8,128)S(1)} %get-tuple-element.63, f32[267,1036]{1,0:T(8,128)S(1)} %get-tuple-element.62, f32[268,1035]{1,0:T(8,128)S(1)} %get-tuple-element.59, ...), kind=kLoop, calls=%fused_computation.12 | loop fusion | flops 1572864 | bytes 7577664 | tf_op jit(solution)/shard_map/mul | solution.py:52
  84.4 0.6 fusion.33
  85.0 0.7 fusion.10
  85.8 4.5 %collective-permute-start.16 = (f32[20,2]{1,0:T(8,128)S(1)}, f32[20,2]{1,0:T(8,128)S(1)}, u32[]{:S(2)}, u32[]{:S(2)}) collective-permute-start(f32[20,2]{1,0:T(8,128)S(1)} %get-tuple-element.101), channel_id=1, source_target_pairs={{0,4},{4,8},{8,12},{12,16},{16,20},{20,24},{24,28},{1,5},{5,9},{9,... | collective-permute-start | bytes 488 | tf_op jit(solution)/shard_map/ppermute | solution.py:20
  90.4 1.9 %collective-permute-start.17 = (f32[20,2]{1,0:T(8,128)S(1)}, f32[20,2]{1,0:T(8,128)S(1)}, u32[]{:S(2)}, u32[]{:S(2)}) collective-permute-start(f32[20,2]{1,0:T(8,128)S(1)} %get-tuple-element.102), channel_id=1, source_target_pairs={{4,0},{8,4},{12,8},{16,12},{20,16},{24,20},{28,24},{5,1},{9,5},{13... | collective-permute-start | bytes 488 | tf_op jit(solution)/shard_map/ppermute | solution.py:21
  92.3 1.3 %slice.322 = f32[256,1024]{1,0:T(8,128)} slice(f32[268,1036]{1,0:T(8,128)S(1)} %get-tuple-element.54), slice={[6:262], [6:1030]} | slice | bytes 2097152 | tf_op jit(solution)/shard_map/slice | solution.py:107
  93.6 1.3 %slice.323 = f32[256,1024]{1,0:T(8,128)} slice(f32[268,1036]{1,0:T(8,128)S(1)} %get-tuple-element.55), slice={[6:262], [6:1030]} | slice | bytes 2097152 | tf_op jit(solution)/shard_map/slice | solution.py:108
  94.9 0.8 collective-permute-done.17
  95.8 3.6 %collective-permute-start.18 = (f32[2,72]{1,0:T(2,128)S(1)}, f32[2,72]{1,0:T(2,128)S(1)}, u32[]{:S(2)}, u32[]{:S(2)}) collective-permute-start(f32[2,72]{1,0:T(2,128)S(1)} %get-tuple-element.100), channel_id=1, source_target_pairs={{0,1},{1,2},{2,3},{4,5},{5,6},{6,7},{8,9},{9,10},{10,11},{12,13},{... | collective-permute-start | bytes 1736 | tf_op jit(solution)/shard_map/ppermute | solution.py:20
  99.5 1.9 %collective-permute-start.19 = (f32[2,72]{1,0:T(2,128)S(1)}, f32[2,72]{1,0:T(2,128)S(1)}, u32[]{:S(2)}, u32[]{:S(2)}) collective-permute-start(f32[2,72]{1,0:T(2,128)S(1)} %get-tuple-element.99), channel_id=1, source_target_pairs={{1,0},{2,1},{3,2},{5,4},{6,5},{7,6},{9,8},{10,9},{11,10},{13,12},{... | collective-permute-start | bytes 1736 | tf_op jit(solution)/shard_map/ppermute | solution.py:21
  101.5 2.9 %collective-permute-done.19 = f32[2,72]{1,0:T(2,128)S(1)} collective-permute-done((f32[2,72]{1,0:T(2,128)S(1)}, f32[2,72]{1,0:T(2,128)S(1)}, u32[]{:S(2)}, u32[]{:S(2)}) %collective-permute-start.19) | collective-permute-done | bytes 608 | tf_op jit(solution)/shard_map/ppermute | solution.py:21
  104.5 0.7 add_select_fusion
  105.4 0.2 scatter-add.19
  105.7 0.6 multiply_multiply_fusion.6
  (46 shorter events, 0.9 us)
Async XLA Ops:
  1.7 22.1 %collective-permute-start.4 = (f32[256,6]{1,0:T(8,128)S(1)}, f32[256,6]{1,0:T(8,128)S(1)}, u32[]{:S(2)}, u32[]{:S(2)}) collective-permute-start(f32[256,6]{1,0:T(8,128)S(1)} %get-tuple-element.95), channel_id=1, source_target_pairs={{0,4},{4,8},{8,12},{12,16},{16,20},{20,24},{24,28},{1,5},{5,9},{9,... | collective-permute-start | bytes 18440 | tf_op jit(solution)/shard_map/ppermute | solution.py:20
  4.9 20.9 %collective-permute-start.5 = (f32[256,6]{1,0:T(8,128)S(1)}, f32[256,6]{1,0:T(8,128)S(1)}, u32[]{:S(2)}, u32[]{:S(2)}) collective-permute-start(f32[256,6]{1,0:T(8,128)S(1)} %get-tuple-element.94), channel_id=1, source_target_pairs={{4,0},{8,4},{12,8},{16,12},{20,16},{24,20},{28,24},{5,1},{9,5},{13... | collective-permute-start | bytes 18440 | tf_op jit(solution)/shard_map/ppermute | solution.py:21
  8.7 22.0 %copy-start.2 = (f32[256,1024]{1,0:T(8,128)S(1)}, f32[256,1024]{1,0:T(8,128)}, u32[]{:S(2)}) copy-start(f32[256,1024]{1,0:T(8,128)} %param.14) | copy-start | bytes 3145732
  9.5 23.5 %collective-permute-start = (f32[256,6]{1,0:T(8,128)}, f32[256,6]{1,0:T(8,128)S(1)}, u32[]{:S(2)}, u32[]{:S(2)}) collective-permute-start(f32[256,6]{1,0:T(8,128)} %get-tuple-element.93), channel_id=1, source_target_pairs={{0,4},{4,8},{8,12},{12,16},{16,20},{20,24},{24,28},{1,5},{5,9},{9,... | collective-permute-start | bytes 18440 | tf_op jit(solution)/shard_map/ppermute | solution.py:20
  13.5 21.4 %collective-permute-start.1 = (f32[256,6]{1,0:T(8,128)}, f32[256,6]{1,0:T(8,128)}, u32[]{:S(2)}, u32[]{:S(2)}) collective-permute-start(f32[256,6]{1,0:T(8,128)} %get-tuple-element.92), channel_id=1, source_target_pairs={{4,0},{8,4},{12,8},{16,12},{20,16},{24,20},{28,24},{5,1},{9,5},{13... | collective-permute-start | bytes 18440 | tf_op jit(solution)/shard_map/ppermute | solution.py:21
  17.2 25.6 %collective-permute-start.8 = (f32[256,6]{1,0:T(8,128)}, f32[256,6]{1,0:T(8,128)S(1)}, u32[]{:S(2)}, u32[]{:S(2)}) collective-permute-start(f32[256,6]{1,0:T(8,128)} %get-tuple-element.97), channel_id=1, source_target_pairs={{0,4},{4,8},{8,12},{12,16},{16,20},{20,24},{24,28},{1,5},{5,9},{9,... | collective-permute-start | bytes 18440 | tf_op jit(solution)/shard_map/ppermute | solution.py:20
  23.8 1.9 %copy-start.5 = (f32[256,6]{1,0:T(8,128)}, f32[256,6]{1,0:T(8,128)S(1)}, u32[]{:S(2)}) copy-start(f32[256,6]{1,0:T(8,128)S(1)} %collective-permute-done.4) | copy-start | bytes 18436
  23.8 20.8 %collective-permute-start.9 = (f32[256,6]{1,0:T(8,128)}, f32[256,6]{1,0:T(8,128)}, u32[]{:S(2)}, u32[]{:S(2)}) collective-permute-start(f32[256,6]{1,0:T(8,128)} %get-tuple-element.96), channel_id=1, source_target_pairs={{4,0},{8,4},{12,8},{16,12},{20,16},{24,20},{28,24},{5,1},{9,5},{13... | collective-permute-start | bytes 18440 | tf_op jit(solution)/shard_map/ppermute | solution.py:21
  25.8 0.7 copy-start.6
  26.4 24.3 %collective-permute-start.12 = (f32[256,6]{1,0:T(8,128)}, f32[256,6]{1,0:T(8,128)}, u32[]{:S(2)}, u32[]{:S(2)}) collective-permute-start(f32[256,6]{1,0:T(8,128)} %get-tuple-element.91), channel_id=1, source_target_pairs={{0,4},{4,8},{8,12},{12,16},{16,20},{20,24},{24,28},{1,5},{5,9},{9,... | collective-permute-start | bytes 18440 | tf_op jit(solution)/shard_map/ppermute | solution.py:20
  32.9 1.9 %copy-start.4 = (f32[256,6]{1,0:T(8,128)}, f32[256,6]{1,0:T(8,128)S(1)}, u32[]{:S(2)}) copy-start(f32[256,6]{1,0:T(8,128)S(1)} %collective-permute-done) | copy-start | bytes 18436
  32.9 19.7 %collective-permute-start.13 = (f32[256,6]{1,0:T(8,128)}, f32[256,6]{1,0:T(8,128)}, u32[]{:S(2)}, u32[]{:S(2)}) collective-permute-start(f32[256,6]{1,0:T(8,128)} %get-tuple-element.90), channel_id=1, source_target_pairs={{4,0},{8,4},{12,8},{16,12},{20,16},{24,20},{28,24},{5,1},{9,5},{13... | collective-permute-start | bytes 18440 | tf_op jit(solution)/shard_map/ppermute | solution.py:21
  34.9 24.6 %collective-permute-start.6 = (f32[6,1036]{1,0:T(8,128)}, f32[6,1036]{1,0:T(8,128)}, u32[]{:S(2)}, u32[]{:S(2)}) collective-permute-start(f32[6,1036]{1,0:T(8,128)} %get-tuple-element.86), channel_id=1, source_target_pairs={{0,1},{1,2},{2,3},{4,5},{5,6},{6,7},{8,9},{9,10},{10,11},{12,13},{... | collective-permute-start | bytes 74600 | tf_op jit(solution)/shard_map/ppermute | solution.py:20
  42.7 1.9 %copy-start.3 = (f32[256,6]{1,0:T(8,128)}, f32[256,6]{1,0:T(8,128)S(1)}, u32[]{:S(2)}) copy-start(f32[256,6]{1,0:T(8,128)S(1)} %collective-permute-done.8) | copy-start | bytes 18436
  42.8 18.7 %collective-permute-start.7 = (f32[6,1036]{1,0:T(8,128)}, f32[6,1036]{1,0:T(8,128)}, u32[]{:S(2)}, u32[]{:S(2)}) collective-permute-start(f32[6,1036]{1,0:T(8,128)} %get-tuple-element.87), channel_id=1, source_target_pairs={{1,0},{2,1},{3,2},{5,4},{6,5},{7,6},{9,8},{10,9},{11,10},{13,12},{... | collective-permute-start | bytes 74600 | tf_op jit(solution)/shard_map/ppermute | solution.py:21
  44.7 21.9 %collective-permute-start.2 = (f32[6,1036]{1,0:T(8,128)}, f32[6,1036]{1,0:T(8,128)}, u32[]{:S(2)}, u32[]{:S(2)}) collective-permute-start(f32[6,1036]{1,0:T(8,128)} %get-tuple-element.84), channel_id=1, source_target_pairs={{0,1},{1,2},{2,3},{4,5},{5,6},{6,7},{8,9},{9,10},{10,11},{12,13},{... | collective-permute-start | bytes 74600 | tf_op jit(solution)/shard_map/ppermute | solution.py:20
  50.7 17.9 %collective-permute-start.3 = (f32[6,1036]{1,0:T(8,128)}, f32[6,1036]{1,0:T(8,128)}, u32[]{:S(2)}, u32[]{:S(2)}) collective-permute-start(f32[6,1036]{1,0:T(8,128)} %get-tuple-element.85), channel_id=1, source_target_pairs={{1,0},{2,1},{3,2},{5,4},{6,5},{7,6},{9,8},{10,9},{11,10},{13,12},{... | collective-permute-start | bytes 74600 | tf_op jit(solution)/shard_map/ppermute | solution.py:21
  52.7 16.0 %collective-permute-start.10 = (f32[6,1036]{1,0:T(8,128)}, f32[6,1036]{1,0:T(8,128)}, u32[]{:S(2)}, u32[]{:S(2)}) collective-permute-start(f32[6,1036]{1,0:T(8,128)} %get-tuple-element.88), channel_id=1, source_target_pairs={{0,1},{1,2},{2,3},{4,5},{5,6},{6,7},{8,9},{9,10},{10,11},{12,13},{... | collective-permute-start | bytes 74600 | tf_op jit(solution)/shard_map/ppermute | solution.py:20
  59.5 9.2 %collective-permute-start.11 = (f32[6,1036]{1,0:T(8,128)}, f32[6,1036]{1,0:T(8,128)S(1)}, u32[]{:S(2)}, u32[]{:S(2)}) collective-permute-start(f32[6,1036]{1,0:T(8,128)} %get-tuple-element.89), channel_id=1, source_target_pairs={{1,0},{2,1},{3,2},{5,4},{6,5},{7,6},{9,8},{10,9},{11,10},{13,12},{... | collective-permute-start | bytes 74600 | tf_op jit(solution)/shard_map/ppermute | solution.py:21
  61.4 9.0 %collective-permute-start.14 = (f32[6,1036]{1,0:T(8,128)S(1)}, f32[6,1036]{1,0:T(8,128)S(1)}, u32[]{:S(2)}, u32[]{:S(2)}) collective-permute-start(f32[6,1036]{1,0:T(8,128)S(1)} %get-tuple-element.82), channel_id=1, source_target_pairs={{0,1},{1,2},{2,3},{4,5},{5,6},{6,7},{8,9},{9,10},{10,11},{12,13},{... | collective-permute-start | bytes 74600 | tf_op jit(solution)/shard_map/ppermute | solution.py:20
  66.6 5.3 %collective-permute-start.15 = (f32[6,1036]{1,0:T(8,128)S(1)}, f32[6,1036]{1,0:T(8,128)S(1)}, u32[]{:S(2)}, u32[]{:S(2)}) collective-permute-start(f32[6,1036]{1,0:T(8,128)S(1)} %get-tuple-element.83), channel_id=1, source_target_pairs={{1,0},{2,1},{3,2},{5,4},{6,5},{7,6},{9,8},{10,9},{11,10},{13,12},{... | collective-permute-start | bytes 74600 | tf_op jit(solution)/shard_map/ppermute | solution.py:21
  68.7 3.1 %copy-start = (f32[256,1036]{1,0:T(8,128)S(1)}, f32[256,1036]{1,0:T(8,128)}, u32[]{:S(2)}) copy-start(f32[256,1036]{1,0:T(8,128)} %concatenate.41) | copy-start | bytes 3182596
  84.4 1.4 %copy-start.1 = (f32[256,1024]{1,0:T(8,128)}, f32[256,1024]{1,0:T(8,128)S(1)}, u32[]{:S(2)}) copy-start(f32[256,1024]{1,0:T(8,128)S(1)} %slice_multiply_fusion) | copy-start | bytes 3145732
  85.8 9.1 %collective-permute-start.16 = (f32[20,2]{1,0:T(8,128)S(1)}, f32[20,2]{1,0:T(8,128)S(1)}, u32[]{:S(2)}, u32[]{:S(2)}) collective-permute-start(f32[20,2]{1,0:T(8,128)S(1)} %get-tuple-element.101), channel_id=1, source_target_pairs={{0,4},{4,8},{8,12},{12,16},{16,20},{20,24},{24,28},{1,5},{5,9},{9,... | collective-permute-start | bytes 488 | tf_op jit(solution)/shard_map/ppermute | solution.py:20
  90.4 5.3 %collective-permute-start.17 = (f32[20,2]{1,0:T(8,128)S(1)}, f32[20,2]{1,0:T(8,128)S(1)}, u32[]{:S(2)}, u32[]{:S(2)}) collective-permute-start(f32[20,2]{1,0:T(8,128)S(1)} %get-tuple-element.102), channel_id=1, source_target_pairs={{4,0},{8,4},{12,8},{16,12},{20,16},{24,20},{28,24},{5,1},{9,5},{13... | collective-permute-start | bytes 488 | tf_op jit(solution)/shard_map/ppermute | solution.py:21
  93.6 12.1 %copy-start.7 = (s32[16,64]{1,0:T(8,128)S(1)}, s32[16,64]{1,0:T(8,128)}, u32[]{:S(2)}) copy-start(s32[16,64]{1,0:T(8,128)} %param.19) | copy-start | bytes 12292
  95.8 5.6 %collective-permute-start.18 = (f32[2,72]{1,0:T(2,128)S(1)}, f32[2,72]{1,0:T(2,128)S(1)}, u32[]{:S(2)}, u32[]{:S(2)}) collective-permute-start(f32[2,72]{1,0:T(2,128)S(1)} %get-tuple-element.100), channel_id=1, source_target_pairs={{0,1},{1,2},{2,3},{4,5},{5,6},{6,7},{8,9},{9,10},{10,11},{12,13},{... | collective-permute-start | bytes 1736 | tf_op jit(solution)/shard_map/ppermute | solution.py:20
  99.5 4.9 %collective-permute-start.19 = (f32[2,72]{1,0:T(2,128)S(1)}, f32[2,72]{1,0:T(2,128)S(1)}, u32[]{:S(2)}, u32[]{:S(2)}) collective-permute-start(f32[2,72]{1,0:T(2,128)S(1)} %get-tuple-element.99), channel_id=1, source_target_pairs={{1,0},{2,1},{3,2},{5,4},{6,5},{7,6},{9,8},{10,9},{11,10},{13,12},{... | collective-permute-start | bytes 1736 | tf_op jit(solution)/shard_map/ppermute | solution.py:21
where the time goes:
time: 108 us; the launch traced here: 106 us
  starting transfers between devices  60 us (56%)
  local copies, waits for them, and re-layouts  22.6 us (21%)
  other arithmetic  16.1 us (15%)
  waiting for transfers between devices  5.16 us (5%)
  matrix products  1.36 us (1%)
  between operations  1.14 us (1%)
    ppermute x10, starting transfers between devices, with_halo(): before = lax.ppermute(last, axis, up)  40.4 us
    ppermute x10, starting transfers between devices, with_halo(): after = lax.ppermute(initial, axis, down)  19.6 us
    concatenate x4, local copies, waits for them, and re-layouts, with_halo(): array = jnp.concatenate([before, array, after], axis=dim)  7.27 us
    slice x4, local copies, waits for them, and re-layouts, with_halo(): initial = lax.slice_in_dim(array, 0, width, axis=dim)  5.27 us
    ppermute x10, waiting for transfers between devices, with_halo(): after = lax.ppermute(initial, axis, down)  5.13 us
    mul x3, other arithmetic, march_steps(): wet_fraction * (eastward + courant * wet_depth * (from_east(surface_heigh...  5.03 us
    mul x3, other arithmetic, march_steps(): wet_fraction * (surface_height + courant * (from_east(eastward) - west_in...  4.71 us
    slice x5, local copies, waits for them, and re-layouts, with_halo(): last = lax.slice_in_dim(array, length - width, length, axis=dim)  2.78 us
  transfers between devices with their start and end apart: 20, of which 3 were waited for; matrix products, arithmetic and copies ran while one was open for 21% of the time, Pallas kernels for 0%

commit v1 on v0

v1 whole, which is shorter than its diff:
```python
import functools

import jax
import jax.numpy as jnp
from jax import lax
from jax.experimental import pallas as pl
from jax.experimental.pallas import tpu as pltpu
from jax.sharding import PartitionSpec as P

SPACING = 16
STEPS = 3
COURANT = 0.5
LANES = 128
SUB = 8
HALO = 32
EDGE = 2 * STEPS
STRIP = HALO + 16
CHUNK = 64
F32 = jnp.float32
ANY = pl.BlockSpec(memory_space=pl.ANY)
VMEM = pl.BlockSpec(memory_space=pltpu.VMEM)


def lane_index():
    return lax.broadcasted_iota(jnp.int32, (SUB, LANES), 1)


def east_minus_west(tiles):
    n = len(tiles)
    up = [pltpu.roll(t, LANES - 1, 1) for t in tiles]
    down = [pltpu.roll(t, 1, 1) for t in tiles]
    if n == 1:
        return [up[0] - down[0]]
    lane = lane_index()
    return [
        jnp.where(lane == LANES - 1, up[(c + 1) % n], up[c])
        - jnp.where(lane == 0, down[(c - 1) % n], down[c])
        for c in range(n)
    ]


def rows_at(ref, c, r):
    return ref[c, pl.ds(r, SUB), :]


def flux_rows(refs, r, tiles):
    S, E, N, Q, W = refs
    ds = east_minus_west([rows_at(S, c, r) for c in range(tiles)])
    for c in range(tiles):
        q = rows_at(Q, c, r)
        E[c, pl.ds(r, SUB), :] = rows_at(E, c, r) + q * ds[c]
        N[c, pl.ds(r, SUB), :] = rows_at(N, c, r) + q * (rows_at(S, c, r + 1) - rows_at(S, c, r - 1))


def surface_rows(refs, r, tiles, first):
    S, E, N, Q, W = refs
    de = east_minus_west([rows_at(E, c, r) for c in range(tiles)])
    for c in range(tiles):
        hw = rows_at(W, c, r)
        s = rows_at(S, c, r)
        if first:
            s = s * (hw + hw)
        S[c, pl.ds(r, SUB), :] = s + hw * (de[c] + (rows_at(N, c, r + 1) - rows_at(N, c, r - 1)))


def loop_rows(count, body, unroll=8):
    while count % unroll:
        unroll -= 1

    def step(i, carry):
        base = pl.multiple_of(i * (unroll * SUB), unroll * SUB) + SUB
        for u in range(unroll):
            body(base + u * SUB)
        return carry

    lax.fori_loop(0, count // unroll, step, 0)


def spline_weight(arg):
    mag = jnp.abs(arg)
    inner = 2.0 / 3.0 - mag * mag + 0.5 * mag * mag * mag
    outer = (2.0 - mag) * (2.0 - mag) * (2.0 - mag) / 6.0
    return jnp.where(mag < 1.0, inner, jnp.where(mag < 2.0, outer, 0.0 * mag))


def spline_of(cell, point):
    return spline_weight((cell.astype(F32) + 0.5) / SPACING - (point.astype(F32) + 0.5))


def dot(a, b):
    return jnp.dot(a, b, precision=lax.Precision.HIGHEST, preferred_element_type=F32)


def zero_borders(refs, rows, tiles):
    z = jnp.zeros((SUB, LANES), F32)
    for ref in refs:
        for c in range(tiles):
            ref[c, 0:SUB, :] = z
            ref[c, SUB + rows : SUB + rows + SUB, :] = z


def wait_all(copies):
    for copy in copies:
        copy.wait()


def is_even(axis):
    return lax.rem(lax.axis_index(axis), 2) == 0


def pack_rows_kernel(s, e, n, d, m, pa, pb, depth, mask, sem):
    rows = s.shape[0]
    even = is_even("lat")
    top = rows - HALO
    starts = (jnp.where(even, top, 0), jnp.where(even, 0, top))
    copies = []
    for side, (out, row) in enumerate(zip((pa, pb), starts)):
        at = pl.ds(pl.multiple_of(row, SUB), HALO)
        for f, (src, dst) in enumerate(
            (
                (s, out.at[0:HALO]),
                (e, out.at[HALO : 2 * HALO]),
                (n, out.at[2 * HALO : 3 * HALO]),
                (d, depth.at[side]),
                (m, mask.at[side]),
            )
        ):
            copy = pltpu.make_async_copy(src.at[at, :], dst, sem.at[side, f])
            copy.start()
            copies.append(copy)
    wait_all(copies)
    for side, out in enumerate((pa, pb)):
        wet = mask[side].astype(F32)
        out[HALO : 2 * HALO] = out[HALO : 2 * HALO] * wet
        out[2 * HALO : 3 * HALO] = out[2 * HALO : 3 * HALO] * wet
        out[3 * HALO : 4 * HALO] = depth[side] * (COURANT * wet)


def pack_rows(s, e, n, d, m):
    rows, cols = s.shape
    return pl.pallas_call(
        pack_rows_kernel,
        out_shape=[jax.ShapeDtypeStruct((4 * HALO, cols), F32)] * 2,
        in_specs=[ANY] * 5,
        out_specs=[VMEM] * 2,
        scratch_shapes=[
            pltpu.VMEM((2, HALO, cols), F32),
            pltpu.VMEM((2, HALO, cols), jnp.int32),
            pltpu.SemaphoreType.DMA((2, 5)),
        ],
        name="pack_rows",
    )(s, e, n, d, m)


def own_columns(first, last):
    lane = lane_index()
    both = jnp.where(lane < HALO, first, pltpu.roll(last, LANES // 2, 1))
    return jnp.where(lane < 2 * HALO, both, 0.0)


def pack_columns(own, even):
    group = lax.div(lane_index(), HALO)
    shift = jnp.where(even, 1, 0)
    pc = pd = None
    for f, tile in enumerate(own):
        turn = (f + 2) % 4
        moved = pltpu.roll(tile, turn * HALO, 1) if turn else tile
        if pc is None:
            pc = pd = moved
        else:
            pc = jnp.where(group == lax.rem(turn + shift, 4), moved, pc)
            pd = jnp.where(group == lax.rem(turn + 1 - shift, 4), moved, pd)
    return pc, pd


def interior_kernel(
    s, e, n, d, m, so, eo, no, u, pc, pd, own, S, E, N, Q, W, M, PC, PD, OWN, isem, osem, psem
):
    rows, cols = s.shape
    tiles = cols // LANES
    chunks = rows // CHUNK
    refs = (S, E, N, Q, W)
    even = is_even("lon")
    loads = []
    for k in range(chunks):
        copies = []
        for src, dst in ((s, S), (d, Q), (m, M), (e, E), (n, N)):
            for c in range(tiles):
                copy = pltpu.make_async_copy(
                    src.at[k * CHUNK : (k + 1) * CHUNK, c * LANES : (c + 1) * LANES],
                    dst.at[c, SUB + k * CHUNK : SUB + (k + 1) * CHUNK, :],
                    isem.at[k],
                )
                copy.start()
                copies.append(copy)
        loads.append(copies)
    zero_borders((S, N), rows, tiles)

    def first_flux(r):
        ds = east_minus_west([rows_at(S, c, r) for c in range(tiles)])
        ends = {}
        for c in range(tiles):
            wet = rows_at(M, c, r).astype(F32)
            hw = COURANT * wet
            q = rows_at(Q, c, r) * hw
            e0 = rows_at(E, c, r) * wet
            n0 = rows_at(N, c, r) * wet
            if c in (0, tiles - 1):
                ends[c] = (rows_at(S, c, r), e0, n0, q)
            W[c, pl.ds(r, SUB), :] = hw
            Q[c, pl.ds(r, SUB), :] = q
            E[c, pl.ds(r, SUB), :] = e0 + q * ds[c]
            N[c, pl.ds(r, SUB), :] = n0 + q * (rows_at(S, c, r + 1) - rows_at(S, c, r - 1))
        mine = [own_columns(a, b) for a, b in zip(ends[0], ends[tiles - 1])]
        for f in range(4):
            OWN[f, pl.ds(r - SUB, SUB), :] = mine[f]
        tc, td = pack_columns(mine, even)
        PC[pl.ds(r - SUB, SUB), :] = tc
        PD[pl.ds(r - SUB, SUB), :] = td

    def over_chunk(k, body):
        def shifted(r):
            body(r + k * CHUNK)

        loop_rows(CHUNK // SUB, shifted)

    wait_all(loads[0])
    for k in range(chunks):
        if k + 1 < chunks:
            wait_all(loads[k + 1])
        over_chunk(k, first_flux)
    sends = [
        pltpu.make_async_copy(PC, pc.at[HALO : HALO + rows], psem.at[0]),
        pltpu.make_async_copy(PD, pd.at[HALO : HALO + rows], psem.at[1]),
        pltpu.make_async_copy(OWN, own.at[:, HALO : HALO + rows], psem.at[2]),
    ]
    for copy in sends:
        copy.start()
    loop_rows(rows // SUB, lambda r: surface_rows(refs, r, tiles, True))
    for step in range(1, STEPS):
        last = step == STEPS - 1
        for k in range(chunks):
            over_chunk(k, lambda r: flux_rows(refs, r, tiles))
            if last:
                sends += store_rows(((E, eo), (N, no)), k, tiles, osem)
        for k in range(chunks):
            over_chunk(k, lambda r: surface_rows(refs, r, tiles, False))
            if last:
                sends += store_rows(((S, so),), k, tiles, osem)
    points = rows // SPACING
    cell = lax.broadcasted_iota(jnp.int32, (points, rows), 1)
    table = spline_of(cell, lax.broadcasted_iota(jnp.int32, (points, rows), 0))
    table = jnp.where((cell >= EDGE) & (cell < rows - EDGE), table, 0.0)
    for c in range(tiles):
        u[:, c * LANES : (c + 1) * LANES] = dot(table, S[c, SUB : SUB + rows, :])
    wait_all(sends)


def store_rows(pairs, k, tiles, sem):
    copies = []
    for src, dst in pairs:
        for c in range(tiles):
            copy = pltpu.make_async_copy(
                src.at[c, SUB + k * CHUNK : SUB + (k + 1) * CHUNK, :],
                dst.at[k * CHUNK : (k + 1) * CHUNK, c * LANES : (c + 1) * LANES],
                sem.at[0],
            )
            copy.start()
            copies.append(copy)
    return copies


def interior(s, e, n, d, m):
    rows, cols = s.shape
    tiles = cols // LANES
    field = jax.ShapeDtypeStruct((rows, cols), F32)
    wide = jax.ShapeDtypeStruct((rows + 2 * HALO, LANES), F32)
    return pl.pallas_call(
        interior_kernel,
        out_shape=[field] * 3
        + [
            jax.ShapeDtypeStruct((rows // SPACING, cols), F32),
            wide,
            wide,
            jax.ShapeDtypeStruct((4, rows + 2 * HALO, LANES), F32),
        ],
        in_specs=[ANY] * 5,
        out_specs=[ANY] * 3 + [VMEM] + [ANY] * 3,
        scratch_shapes=[pltpu.VMEM((tiles, rows + 2 * SUB, LANES), F32)] * 5
        + [
            pltpu.VMEM((tiles, rows + 2 * SUB, LANES), jnp.int32),
            pltpu.VMEM((rows, LANES), F32),
            pltpu.VMEM((rows, LANES), F32),
            pltpu.VMEM((4, rows, LANES), F32),
            pltpu.SemaphoreType.DMA((rows // CHUNK,)),
            pltpu.SemaphoreType.DMA((1,)),
            pltpu.SemaphoreType.DMA((3,)),
        ],
        cost_estimate=pl.CostEstimate(flops=40 * rows * cols, bytes_accessed=32 * rows * cols, transcendentals=0),
        name="interior",
    )(s, e, n, d, m)


def corner_kernel(ra, rb, pc_in, pd_in, own_in, pc, pd, own, X, PC, PD, OWN, sem, psem):
    del pc_in, pd_in, own_in
    height = pc.shape[0]
    cols = ra.shape[1]
    even, lon_even = is_even("lat"), is_even("lon")
    copies = []
    for side, src in enumerate((ra, rb)):
        for end, col in enumerate((0, cols - LANES)):
            copy = pltpu.make_async_copy(src.at[:, col : col + LANES], X.at[side, end], sem.at[side, end])
            copy.start()
            copies.append(copy)
    wait_all(copies)
    top = height - HALO
    starts = (jnp.where(even, top, 0), jnp.where(even, 0, top))
    sends = []
    for side, row in enumerate(starts):
        for r in range(0, HALO, SUB):
            mine = [
                own_columns(X[side, 0, f * HALO + r : f * HALO + r + SUB, :], X[side, 1, f * HALO + r : f * HALO + r + SUB, :])
                for f in range(4)
            ]
            for f in range(4):
                OWN[side, f, r : r + SUB, :] = mine[f]
            tc, td = pack_columns(mine, lon_even)
            PC[side, r : r + SUB, :] = tc
            PD[side, r : r + SUB, :] = td
        at = pl.ds(pl.multiple_of(row, SUB), HALO)
        for f, (src, dst) in enumerate(
            ((PC.at[side], pc.at[at, :]), (PD.at[side], pd.at[at, :]), (OWN.at[side], own.at[:, at, :]))
        ):
            copy = pltpu.make_async_copy(src, dst, psem.at[side, f])
            copy.start()
            sends.append(copy)
    wait_all(sends)


def corners(ra, rb, pc, pd, own):
    return pl.pallas_call(
        corner_kernel,
        out_shape=[jax.ShapeDtypeStruct(x.shape, F32) for x in (pc, pd, own)],
        in_specs=[ANY] * 5,
        out_specs=[ANY] * 3,
        scratch_shapes=[
            pltpu.VMEM((2, 2, 4 * HALO, LANES), F32),
            pltpu.VMEM((2, HALO, LANES), F32),
            pltpu.VMEM((2, HALO, LANES), F32),
            pltpu.VMEM((2, 4, HALO, LANES), F32),
            pltpu.SemaphoreType.DMA((2, 2)),
            pltpu.SemaphoreType.DMA((2, 3)),
        ],
        input_output_aliases={2: 0, 3: 1, 4: 2},
        name="corners",
    )(ra, rb, pc, pd, own)


def strip_kernel(s, e, n, d, m, ra, rb, u, so_in, eo_in, no_in, so, eo, no, v, S, E, N, Q, W, M, sem, osem):
    del so_in, eo_in, no_in
    rows, cols = s.shape
    tiles = cols // LANES
    refs = (S, E, N, Q, W)
    even = is_even("lat")
    keep = STRIP - HALO
    count = 2 * STRIP
    loads = []
    for src, dst in ((s, S), (e, E), (n, N), (d, Q), (m, M)):
        for row, to in ((0, HALO), (rows - keep, STRIP)):
            for c in range(tiles):
                copy = pltpu.make_async_copy(
                    src.at[row : row + keep, c * LANES : (c + 1) * LANES],
                    dst.at[c, SUB + to : SUB + to + keep, :],
                    sem.at[0],
                )
                copy.start()
                loads.append(copy)
    high = SUB + STRIP + keep
    for src, to in ((ra, jnp.where(even, high, SUB)), (rb, jnp.where(even, SUB, high))):
        at = pl.ds(pl.multiple_of(to, SUB), HALO)
        for f, dst in enumerate((S, E, N, Q)):
            for c in range(tiles):
                copy = pltpu.make_async_copy(
                    src.at[f * HALO : (f + 1) * HALO, c * LANES : (c + 1) * LANES],
                    dst.at[c, at, :],
                    sem.at[0],
                )
                copy.start()
                loads.append(copy)
    zero_borders((S, N), count, tiles)
    wait_all(loads)
    for c in range(tiles):
        for r in range(SUB + HALO, SUB + HALO + 2 * keep, SUB):
            wet = M[c, r : r + SUB, :].astype(F32)
            hw = COURANT * wet
            W[c, r : r + SUB, :] = hw
            Q[c, r : r + SUB, :] = Q[c, r : r + SUB, :] * hw
            E[c, r : r + SUB, :] = E[c, r : r + SUB, :] * wet
            N[c, r : r + SUB, :] = N[c, r : r + SUB, :] * wet
        for first in (SUB, high):
            for r in range(first, first + HALO, SUB):
                W[c, r : r + SUB, :] = jnp.where(Q[c, r : r + SUB, :] > 0.0, COURANT, 0.0)
    for step in range(STEPS):
        loop_rows(count // SUB, lambda r: flux_rows(refs, r, tiles), 12)
        loop_rows(count // SUB, lambda r: surface_rows(refs, r, tiles, step == 0), 12)
    sends = []
    for src, dst in ((S, so), (E, eo), (N, no)):
        for frm, to in ((SUB + HALO, 0), (SUB + STRIP + keep - SUB, rows - SUB)):
            for c in range(tiles):
                copy = pltpu.make_async_copy(
                    src.at[c, frm : frm + SUB, :],
                    dst.at[to : to + SUB, c * LANES : (c + 1) * LANES],
                    osem.at[0],
                )
                copy.start()
                sends.append(copy)
    points = rows // SPACING
    index = lax.broadcasted_iota(jnp.int32, (points, count), 1)
    cell = jnp.where(index < STRIP, index - HALO, index + (rows - keep - STRIP))
    table = spline_of(cell, lax.broadcasted_iota(jnp.int32, (points, count), 0))
    table = jnp.where((cell < EDGE) | (cell >= rows - EDGE), table, 0.0)
    across = cols // SPACING
    total = jnp.zeros((points, across), F32)
    for c in range(tiles):
        part = u[:, c * LANES : (c + 1) * LANES] + dot(table, S[c, SUB : SUB + count, :])
        col = lax.broadcasted_iota(jnp.int32, (LANES, across), 0) + c * LANES
        weights = spline_of(col, lax.broadcasted_iota(jnp.int32, (LANES, across), 1))
        weights = jnp.where((col >= EDGE) & (col < cols - EDGE), weights, 0.0)
        total = total + dot(part, weights)
    v[...] = total
    wait_all(sends)


def strips(s, e, n, d, m, ra, rb, u, so, eo, no):
    rows, cols = s.shape
    tiles = cols // LANES
    field = jax.ShapeDtypeStruct((rows, cols), F32)
    return pl.pallas_call(
        strip_kernel,
        out_shape=[field] * 3 + [jax.ShapeDtypeStruct((rows // SPACING, cols // SPACING), F32)],
        in_specs=[ANY] * 7 + [VMEM] + [ANY] * 3,
        out_specs=[ANY] * 3 + [VMEM],
        scratch_shapes=[pltpu.VMEM((tiles, 2 * STRIP + 2 * SUB, LANES), F32)] * 5
        + [
            pltpu.VMEM((tiles, 2 * STRIP + 2 * SUB, LANES), jnp.int32),
            pltpu.SemaphoreType.DMA((1,)),
            pltpu.SemaphoreType.DMA((1,)),
        ],
        input_output_aliases={8: 0, 9: 1, 10: 2},
        cost_estimate=pl.CostEstimate(flops=20 * rows * cols, bytes_accessed=16 * rows * cols, transcendentals=0),
        name="strips",
    )(s, e, n, d, m, ra, rb, u, so, eo, no)


def column_kernel(rc, rd, own, v, active, so_in, eo_in, no_in, so, eo, no, grad, S, E, N, Q, W, X, sem, osem):
    rows, cols = so.shape
    height = rows + 2 * HALO
    refs = (S, E, N, Q, W)
    even = is_even("lon")
    loads = []
    for f, src in enumerate((so_in, eo_in, no_in)):
        for end, col in enumerate((0, cols - LANES)):
            copy = pltpu.make_async_copy(src.at[:, col : col + LANES], X.at[f, end], sem.at[f, end])
            copy.start()
            loads.append(copy)
    zero_borders((S, N), height, 1)
    group = lax.div(lane_index(), HALO)

    def unpack(r):
        at = pl.ds(r - SUB, SUB)
        c, d = rc[at, :], rd[at, :]
        right, left = jnp.where(even, c, d), jnp.where(even, d, c)
        for f, dst in enumerate((S, E, N, Q)):
            a, b = right, left
            if f:
                a, b = pltpu.roll(a, LANES - f * HALO, 1), pltpu.roll(b, LANES - f * HALO, 1)
            tile = jnp.where(group == 2, a, jnp.where(group == 3, b, own[f, at, :]))
            dst[0, pl.ds(r, SUB), :] = tile
            if f == 3:
                W[0, pl.ds(r, SUB), :] = jnp.where(tile > 0.0, COURANT, 0.0)

    loop_rows(height // SUB, unpack, 20)
    for step in range(STEPS):
        loop_rows(height // SUB, lambda r: flux_rows(refs, r, 1), 20)
        loop_rows(height // SUB, lambda r: surface_rows(refs, r, 1, step == 0), 20)
    wait_all(loads)
    lane = lane_index()

    def merge(r):
        at = pl.ds(r - SUB, SUB)
        for f, src in enumerate((S, E, N)):
            tile = src[0, pl.ds(r + HALO, SUB), :]
            X[f, 0, at, :] = jnp.where(lane < EDGE, tile, X[f, 0, at, :])
            X[f, 1, at, :] = jnp.where(lane >= LANES - EDGE, pltpu.roll(tile, LANES // 2, 1), X[f, 1, at, :])

    loop_rows(rows // SUB, merge, 8)
    sends = []
    for f, dst in enumerate((so, eo, no)):
        for end, col in enumerate((0, cols - LANES)):
            copy = pltpu.make_async_copy(X.at[f, end], dst.at[:, col : col + LANES], osem.at[f, end])
            copy.start()
            sends.append(copy)
    points, across = grad.shape
    cell = lax.broadcasted_iota(jnp.int32, (points, height), 1) - HALO
    table = spline_of(cell, lax.broadcasted_iota(jnp.int32, (points, height), 0))
    part = dot(table, S[0, SUB : SUB + height, :])
    index = lax.broadcasted_iota(jnp.int32, (LANES, across), 0)
    col = jnp.where(index < HALO, index, jnp.where(index < 3 * HALO, index + (cols - 2 * HALO), index - LANES))
    weights = spline_of(col, lax.broadcasted_iota(jnp.int32, (LANES, across), 1))
    weights = jnp.where((col < EDGE) | (col >= cols - EDGE), weights, 0.0)
    sums = v[...] + dot(part, weights)
    grad[...] = sums * active[...].astype(F32) / SPACING
    wait_all(sends)


def columns(rc, rd, own, v, active, so, eo, no):
    rows, cols = so.shape
    height = rows + 2 * HALO
    field = jax.ShapeDtypeStruct((rows, cols), F32)
    return pl.pallas_call(
        column_kernel,
        out_shape=[field] * 3 + [jax.ShapeDtypeStruct(v.shape, F32)],
        in_specs=[VMEM] * 5 + [ANY] * 3,
        out_specs=[ANY] * 3 + [VMEM],
        scratch_shapes=[pltpu.VMEM((1, height + 2 * SUB, LANES), F32)] * 5
        + [
            pltpu.VMEM((3, 2, rows, LANES), F32),
            pltpu.SemaphoreType.DMA((3, 2)),
            pltpu.SemaphoreType.DMA((3, 2)),
        ],
        input_output_aliases={5: 0, 6: 1, 7: 2},
        name="columns",
    )(rc, rd, own, v, active, so, eo, no)


def swap(array, axis, offset):
    size = lax.axis_size(axis)
    pairs = []
    for i in range(offset, size):
        j = ((i - offset) ^ 1) + offset
        if j < size:
            pairs.append((i, j))
    return lax.ppermute(array, axis, pairs)


def local(surface_adjoint, east_adjoint, north_adjoint, water_depth, wet_mask, control_active):
    fields = (surface_adjoint, east_adjoint, north_adjoint, water_depth, wet_mask)
    pa, pb = pack_rows(*fields)
    rb = swap(pb, "lat", 1)
    ra = swap(pa, "lat", 0)
    so, eo, no, u, pc, pd, own = interior(*fields)
    pc, pd, own = corners(ra, rb, pc, pd, own)
    rc = swap(pc, "lon", 0)
    rd = swap(pd, "lon", 1)
    so, eo, no, v = strips(*fields, ra, rb, u, so, eo, no)
    return columns(rc, rd, own, v, control_active, so, eo, no)


def solution(mesh):
    spec = P("lat", "lon")
    return jax.shard_map(
        lambda *args: tuple(local(*args)),
        mesh=mesh,
        in_specs=(spec,) * 6,
        out_specs=(spec,) * 4,
        check_vma=False,
    )
```

time: 108 us -> 34.3 us (0.32); the launches traced: 106 us -> 33.9 us
  starting transfers between devices: 60 us -> 8.2 us
  Pallas kernels: 0 us -> 23.3 us
  local copies, waits for them, and re-layouts: 22.6 us -> 1.65 us
  other arithmetic: 16.1 us -> 0 us
  waiting for transfers between devices: 5.16 us -> 0.01 us
  matrix products: 1.36 us -> 0 us
    ppermute x20 -> x4, starting transfers between devices: 60 us -> 8.2 us  [swap(): return lax.ppermute(array, axis, pairs)]
    pallas_call x0 -> x5, Pallas kernels: none -> 23.3 us  [the longest x1 8.49 us: interior(): pl.pallas_call(interior_kernel, out_shape=[field] * 3 + [jax.ShapeDtypeSt...]
    slice x25 -> x0, local copies, waits for them, and re-layouts: 14.2 us -> none  [the longest x4 5.27 us: with_halo(): initial = lax.slice_in_dim(array, 0, width, axis=dim)]
    mul x8 -> x0, other arithmetic: 12.9 us -> none  [the longest x3 5.03 us: march_steps(): wet_fraction * (eastward + courant * wet_depth * (from_east(surface_heigh...]
    concatenate x4 -> x0, local copies, waits for them, and re-layouts: 7.27 us -> none  [with_halo(): array = jnp.concatenate([before, array, after], axis=dim)]
    ppermute x20 -> x4, waiting for transfers between devices: 5.16 us -> 0.01 us  [swap(): return lax.ppermute(array, axis, pairs)]
    another operation x2 -> x0, other arithmetic: 1.36 us -> none
    dot_general x2 -> x0, matrix products: 1.36 us -> none  [the longest x1 0.73 us: local(): jnp.dot(reduced, lon_table, precision=lax.Precision.HIGHEST, preferred_el...]
  transfers between devices with their start and end apart: 20 -> 4, of which waited for: 3 -> 0; matrix products, arithmetic and copies ran while one was open for 21% -> 0% of each run, Pallas kernels for 0% -> 41%
where the time goes in v1:
time: 34.3 us; the launch traced here: 33.9 us
  Pallas kernels  23.3 us (68%)
  starting transfers between devices  8.2 us (24%)
  local copies, waits for them, and re-layouts  1.65 us (5%)
  between operations  0.74 us (2%)
    pallas_call x1, Pallas kernels, interior(): pl.pallas_call(interior_kernel, out_shape=[field] * 3 + [jax.ShapeDtypeSt...  8.49 us
    ppermute x4, starting transfers between devices, swap(): return lax.ppermute(array, axis, pairs)  8.2 us
    pallas_call x1, Pallas kernels, strips(): pl.pallas_call(strip_kernel, out_shape=[field] * 3 + [jax.ShapeDtypeStruc...  5.43 us
    pallas_call x1, Pallas kernels, columns(): pl.pallas_call(column_kernel, out_shape=[field] * 3 + [jax.ShapeDtypeStru...  5.03 us
    pallas_call x1, Pallas kernels, pack_rows(): pl.pallas_call(pack_rows_kernel, out_shape=[jax.ShapeDtypeStruct((4 * HAL...  2.48 us
    pallas_call x1, Pallas kernels, corners(): pl.pallas_call(corner_kernel, out_shape=[jax.ShapeDtypeStruct(x.shape, F3...  1.88 us
    unnamed x8, local copies, waits for them, and re-layouts  1.65 us
  transfers between devices with their start and end apart: 4, of which 0 were waited for; matrix products, arithmetic and copies ran while one was open for 0% of the time, Pallas kernels for 41%

profile of v1, /device:TPU:5, one launch (start us, length us, event | category | flops | bytes accessed | tf_op | source)
XLA Modules:
  0.0 33.9 jit_solution(17287794612657479337)
XLA Ops:
  0.6 2.5 %pack_rows.1 = (f32[128,1024]{1,0:T(8,128)}, f32[128,1024]{1,0:T(8,128)}) custom-call(f32[256,1024]{1,0:T(8,128)} %s.5, f32[256,1024]{1,0:T(8,128)} %e.5, f32[256,1024]{1,0:T(8,128)} %n.5, f32[256,1024]{1,0:T(8,128)} %d.5, s32[256,1024]{1,0:T(8,128)} %m.5), custom_call_target="tpu_custom_call" | custom-call | tf_op jit(solution)/shard_map/pack_rows/pallas_call | solution.py:141
  3.1 0.7 %collective-permute-start = (f32[128,1024]{1,0:T(8,128)}, f32[128,1024]{1,0:T(8,128)S(1)}, u32[]{:S(2)}, u32[]{:S(2)}) collective-permute-start(f32[128,1024]{1,0:T(8,128)} %get-tuple-element.20), channel_id=1, source_target_pairs={{0,1},{1,0},{2,3},{3,2},{4,5},{5,4},{6,7},{7,6},{8,9},{9,8},{10,11... | collective-permute-start | bytes 1572872 | tf_op jit(solution)/shard_map/ppermute | solution.py:543
  3.9 3.0 %collective-permute-start.1 = (f32[128,1024]{1,0:T(8,128)}, f32[128,1024]{1,0:T(8,128)S(1)}, u32[]{:S(2)}, u32[]{:S(2)}) collective-permute-start(f32[128,1024]{1,0:T(8,128)} %get-tuple-element.21), channel_id=1, source_target_pairs={{1,2},{2,1},{5,6},{6,5},{9,10},{10,9},{13,14},{14,13},{17,18},{18,... | collective-permute-start | bytes 1572872 | tf_op jit(solution)/shard_map/ppermute | solution.py:543
  6.9 8.5 %interior.1 = (f32[256,1024]{1,0:T(8,128)}, f32[256,1024]{1,0:T(8,128)}, f32[256,1024]{1,0:T(8,128)}, f32[16,1024]{1,0:T(8,128)}, f32[320,128]{1,0:T(8,128)}, /*...) custom-call(f32[256,1024]{1,0:T(8,128)} %s.5, f32[256,1024]{1,0:T(8,128)} %e.5, f32[256,1024]{1,0:T(8,128)} %n.5, f32[256,1024]{1,0:T(8,128)} %d.5, ...), custom_call_target="tpu_custom_call" | custom-call | flops 10485760 | bytes 8388608 | tf_op jit(solution)/shard_map/interior/pallas_call | solution.py:278
  15.4 0.0 collective-permute-done.ra
  15.4 0.0 copy-start
  15.4 0.0 collective-permute-done.1.rb
  15.4 0.0 copy-start.1
  15.4 0.8 %copy-done = f32[128,1024]{1,0:T(8,128)} copy-done((f32[128,1024]{1,0:T(8,128)}, f32[128,1024]{1,0:T(8,128)S(1)}, u32[]{:S(2)}) %copy-start) | copy-done | bytes 524312
  16.2 0.2 copy-done.1
  16.4 1.9 %corners.1 = (f32[320,128]{1,0:T(8,128)}, f32[320,128]{1,0:T(8,128)}, f32[4,320,128]{2,1,0:T(8,128)}) custom-call(f32[128,1024]{1,0:T(8,128)} %copy-done, f32[128,1024]{1,0:T(8,128)} %copy-done.1, f32[320,128]{1,0:T(8,128)} %get-tuple-element.22.pc_in, ...), custom_call_target="tpu_custom_call", output_to_operand_aliasing={{0}: (2, {}), {1}: (3, {}), {2}: (4, {})} | custom-call | tf_op jit(solution)/shard_map/corners/pallas_call | solution.py:341
  18.3 0.3 collective-permute-start.2
  18.6 4.1 %collective-permute-start.3 = (f32[320,128]{1,0:T(8,128)}, f32[320,128]{1,0:T(8,128)S(1)}, u32[]{:S(2)}, u32[]{:S(2)}) collective-permute-start(f32[320,128]{1,0:T(8,128)} %get-tuple-element.26), channel_id=1, source_target_pairs={{4,8},{8,4},{12,16},{16,12},{20,24},{24,20},{5,9},{9,5},{13,17},{1... | collective-permute-start | bytes 491528 | tf_op jit(solution)/shard_map/ppermute | solution.py:543
  22.7 5.4 %strips.1 = (f32[256,1024]{1,0:T(8,128)}, f32[256,1024]{1,0:T(8,128)}, f32[256,1024]{1,0:T(8,128)}, f32[16,64]{1,0:T(8,128)}) custom-call(f32[256,1024]{1,0:T(8,128)} %s.5, f32[256,1024]{1,0:T(8,128)} %e.5, f32[256,1024]{1,0:T(8,128)} %n.5, f32[256,1024]{1,0:T(8,128)} %d.5, ...), custom_call_target="tpu_custom_call", output_to_operand_aliasing={{0}: (8, {}), {1}: (9, {}), {2}: (10, {})} | custom-call | flops 5242880 | bytes 4194304 | tf_op jit(solution)/shard_map/strips/pallas_call | solution.py:438
  28.2 0.0 collective-permute-done.2.rc
  28.2 0.0 copy-start.2
  28.2 0.0 collective-permute-done.3.rd
  28.2 0.0 copy-start.3
  28.2 0.6 %copy-done.2 = f32[320,128]{1,0:T(8,128)} copy-done((f32[320,128]{1,0:T(8,128)}, f32[320,128]{1,0:T(8,128)S(1)}, u32[]{:S(2)}) %copy-start.2) | copy-done | bytes 163864
  28.8 0.0 copy-done.3
  28.9 5.0 %columns.1 = (f32[256,1024]{1,0:T(8,128)}, f32[256,1024]{1,0:T(8,128)}, f32[256,1024]{1,0:T(8,128)}, f32[16,64]{1,0:T(8,128)}) custom-call(f32[320,128]{1,0:T(8,128)} %copy-done.2, f32[320,128]{1,0:T(8,128)} %copy-done.3, f32[4,320,128]{2,1,0:T(8,128)} %get-tuple-element.27.own, ...), custom_call_target="tpu_custom_call", output_to_operand_aliasing={{0}: (5, {}), {1}: (6, {}), {2}: (7, {})} | custom-call | tf_op jit(solution)/shard_map/columns/pallas_call | solution.py:520
Async XLA Ops:
  3.1 12.3 %collective-permute-start = (f32[128,1024]{1,0:T(8,128)}, f32[128,1024]{1,0:T(8,128)S(1)}, u32[]{:S(2)}, u32[]{:S(2)}) collective-permute-start(f32[128,1024]{1,0:T(8,128)} %get-tuple-element.20), channel_id=1, source_target_pairs={{0,1},{1,0},{2,3},{3,2},{4,5},{5,4},{6,7},{7,6},{8,9},{9,8},{10,11... | collective-permute-start | bytes 1572872 | tf_op jit(solution)/shard_map/ppermute | solution.py:543
  3.9 11.5 %collective-permute-start.1 = (f32[128,1024]{1,0:T(8,128)}, f32[128,1024]{1,0:T(8,128)S(1)}, u32[]{:S(2)}, u32[]{:S(2)}) collective-permute-start(f32[128,1024]{1,0:T(8,128)} %get-tuple-element.21), channel_id=1, source_target_pairs={{1,2},{2,1},{5,6},{6,5},{9,10},{10,9},{13,14},{14,13},{17,18},{18,... | collective-permute-start | bytes 1572872 | tf_op jit(solution)/shard_map/ppermute | solution.py:543
  15.4 0.8 %copy-start = (f32[128,1024]{1,0:T(8,128)}, f32[128,1024]{1,0:T(8,128)S(1)}, u32[]{:S(2)}) copy-start(f32[128,1024]{1,0:T(8,128)S(1)} %collective-permute-done.ra) | copy-start | bytes 1572868
  15.4 1.0 %copy-start.1 = (f32[128,1024]{1,0:T(8,128)}, f32[128,1024]{1,0:T(8,128)S(1)}, u32[]{:S(2)}) copy-start(f32[128,1024]{1,0:T(8,128)S(1)} %collective-permute-done.1.rb) | copy-start | bytes 1572868
  18.3 9.9 %collective-permute-start.2 = (f32[320,128]{1,0:T(8,128)}, f32[320,128]{1,0:T(8,128)S(1)}, u32[]{:S(2)}, u32[]{:S(2)}) collective-permute-start(f32[320,128]{1,0:T(8,128)} %get-tuple-element.25), channel_id=1, source_target_pairs={{0,4},{4,0},{8,12},{12,8},{16,20},{20,16},{24,28},{28,24},{1,5},{5... | collective-permute-start | bytes 491528 | tf_op jit(solution)/shard_map/ppermute | solution.py:543
  18.6 9.6 %collective-permute-start.3 = (f32[320,128]{1,0:T(8,128)}, f32[320,128]{1,0:T(8,128)S(1)}, u32[]{:S(2)}, u32[]{:S(2)}) collective-permute-start(f32[320,128]{1,0:T(8,128)} %get-tuple-element.26), channel_id=1, source_target_pairs={{4,8},{8,4},{12,16},{16,12},{20,24},{24,20},{5,9},{9,5},{13,17},{1... | collective-permute-start | bytes 491528 | tf_op jit(solution)/shard_map/ppermute | solution.py:543
  28.2 0.7 %copy-start.2 = (f32[320,128]{1,0:T(8,128)}, f32[320,128]{1,0:T(8,128)S(1)}, u32[]{:S(2)}) copy-start(f32[320,128]{1,0:T(8,128)S(1)} %collective-permute-done.2.rc) | copy-start | bytes 491524
  28.2 0.7 %copy-start.3 = (f32[320,128]{1,0:T(8,128)}, f32[320,128]{1,0:T(8,128)S(1)}, u32[]{:S(2)}) copy-start(f32[320,128]{1,0:T(8,128)S(1)} %collective-permute-done.3.rd) | copy-start | bytes 491524

commit v2 on v1

--- a/solution.py
+++ b/solution.py
@@ -18,7 +18,9 @@
 CHUNK = 64
 F32 = jnp.float32
 ANY = pl.BlockSpec(memory_space=pl.ANY)
+HBM = pl.BlockSpec(memory_space=pltpu.HBM)
 VMEM = pl.BlockSpec(memory_space=pltpu.VMEM)
+PARAMS = pltpu.CompilerParams(vmem_limit_bytes=16 * 2**20)
 
 
 def lane_index():
@@ -141,15 +143,16 @@
     return pl.pallas_call(
         pack_rows_kernel,
         out_shape=[jax.ShapeDtypeStruct((4 * HALO, cols), F32)] * 2,
-        in_specs=[ANY] * 5,
+        in_specs=[HBM] * 5,
         out_specs=[VMEM] * 2,
         scratch_shapes=[
             pltpu.VMEM((2, HALO, cols), F32),
             pltpu.VMEM((2, HALO, cols), jnp.int32),
             pltpu.SemaphoreType.DMA((2, 5)),
         ],
+        compiler_params=PARAMS,
         name="pack_rows",
-    )(s, e, n, d, m)
+    )(*(pltpu.with_memory_space_constraint(x, pltpu.HBM) for x in (s, e, n, d, m)))
 
 
 def own_columns(first, last):
@@ -297,6 +300,7 @@
             pltpu.SemaphoreType.DMA((3,)),
         ],
         cost_estimate=pl.CostEstimate(flops=40 * rows * cols, bytes_accessed=32 * rows * cols, transcendentals=0),
+        compiler_params=PARAMS,
         name="interior",
     )(s, e, n, d, m)
 
@@ -352,6 +356,7 @@
             pltpu.SemaphoreType.DMA((2, 3)),
         ],
         input_output_aliases={2: 0, 3: 1, 4: 2},
+        compiler_params=PARAMS,
         name="corners",
     )(ra, rb, pc, pd, own)
 
@@ -448,6 +453,7 @@
         ],
         input_output_aliases={8: 0, 9: 1, 10: 2},
         cost_estimate=pl.CostEstimate(flops=20 * rows * cols, bytes_accessed=16 * rows * cols, transcendentals=0),
+        compiler_params=PARAMS,
         name="strips",
     )(s, e, n, d, m, ra, rb, u, so, eo, no)
 
@@ -529,6 +535,7 @@
             pltpu.SemaphoreType.DMA((3, 2)),
         ],
         input_output_aliases={5: 0, 6: 1, 7: 2},
+        compiler_params=PARAMS,
         name="columns",
     )(rc, rd, own, v, active, so, eo, no)
 

time: 34.3 us -> 27.4 us (0.80)
  Pallas kernels: 23.3 us -> 17.4 us
  local copies, waits for them, and re-layouts: 1.65 us -> 0.69 us
    pallas_call x1, Pallas kernels: 5.43 us -> 3.79 us  [strips(): pl.pallas_call(strip_kernel, out_shape=[field] * 3 + [jax.ShapeDtypeStruc...]
    pallas_call x1, Pallas kernels: 1.88 us -> 0.57 us  [corners(): pl.pallas_call(corner_kernel, out_shape=[jax.ShapeDtypeStruct(x.shape, F3...]
    pallas_call x1, Pallas kernels: 5.03 us -> 3.76 us  [columns(): pl.pallas_call(column_kernel, out_shape=[field] * 3 + [jax.ShapeDtypeStru...]
    unnamed x8 -> x12, local copies, waits for them, and re-layouts: 1.65 us -> 0.69 us
    pallas_call x1, Pallas kernels: 8.49 us -> 7.6 us  [interior(): pl.pallas_call(interior_kernel, out_shape=[field] * 3 + [jax.ShapeDtypeSt...]
    pallas_call x1, Pallas kernels: 2.48 us -> 1.66 us  [pack_rows(): pl.pallas_call(pack_rows_kernel, out_shape=[jax.ShapeDtypeStruct((4 * HAL...]
  transfers between devices with their start and end apart: 4 -> 4, of which waited for: 0 -> 0; matrix products, arithmetic and copies ran while one was open for 0% -> 0% of each run, Pallas kernels for 41% -> 42%
where the time goes in v2:
time: 27.4 us; the launch traced here: 27.2 us
  Pallas kernels  17.4 us (64%)
  starting transfers between devices  8.33 us (30%)
  between operations  0.8 us (3%)
  local copies, waits for them, and re-layouts  0.69 us (3%)
    ppermute x4, starting transfers between devices, swap(): return lax.ppermute(array, axis, pairs)  8.33 us
    pallas_call x1, Pallas kernels, interior(): pl.pallas_call(interior_kernel, out_shape=[field] * 3 + [jax.ShapeDtypeSt...  7.6 us
    pallas_call x1, Pallas kernels, strips(): pl.pallas_call(strip_kernel, out_shape=[field] * 3 + [jax.ShapeDtypeStruc...  3.79 us
    pallas_call x1, Pallas kernels, columns(): pl.pallas_call(column_kernel, out_shape=[field] * 3 + [jax.ShapeDtypeStru...  3.76 us
    pallas_call x1, Pallas kernels, pack_rows(): pl.pallas_call(pack_rows_kernel, out_shape=[jax.ShapeDtypeStruct((4 * HAL...  1.66 us
    unnamed x12, local copies, waits for them, and re-layouts  0.69 us
    pallas_call x1, Pallas kernels, corners(): pl.pallas_call(corner_kernel, out_shape=[jax.ShapeDtypeStruct(x.shape, F3...  0.57 us
  transfers between devices with their start and end apart: 4, of which 0 were waited for; matrix products, arithmetic and copies ran while one was open for 0% of the time, Pallas kernels for 42%

profile of v2, /device:TPU:5, one launch (start us, length us, event | category | flops | bytes accessed | tf_op | source)
XLA Modules:
  0.0 27.2 jit_solution(10085058203129766846)
XLA Ops:
  0.6 0.0 copy-start
  0.6 0.0 copy-start.1
  0.7 0.0 copy-start.2
  0.7 0.0 copy-start.3
  0.7 0.0 copy-start.4
  0.7 1.7 %pack_rows.1 = (f32[128,1024]{1,0:T(8,128)S(1)}, f32[128,1024]{1,0:T(8,128)S(1)}) custom-call(f32[256,1024]{1,0:T(8,128)} %s.5, f32[256,1024]{1,0:T(8,128)} %e.5, f32[256,1024]{1,0:T(8,128)} %n.5, f32[256,1024]{1,0:T(8,128)} %d.5, s32[256,1024]{1,0:T(8,128)} %m.5), custom_call_target="tpu_custom_call" | custom-call | tf_op jit(solution)/shard_map/pack_rows/pallas_call | solution.py:143
  2.4 0.7 %collective-permute-start = (f32[128,1024]{1,0:T(8,128)S(1)}, f32[128,1024]{1,0:T(8,128)S(1)}, u32[]{:S(2)}, u32[]{:S(2)}) collective-permute-start(f32[128,1024]{1,0:T(8,128)S(1)} %get-tuple-element.20), channel_id=1, source_target_pairs={{0,1},{1,0},{2,3},{3,2},{4,5},{5,4},{6,7},{7,6},{8,9},{9,8},{10,11... | collective-permute-start | bytes 1572872 | tf_op jit(solution)/shard_map/ppermute | solution.py:550
  3.1 3.1 %collective-permute-start.1 = (f32[128,1024]{1,0:T(8,128)S(1)}, f32[128,1024]{1,0:T(8,128)S(1)}, u32[]{:S(2)}, u32[]{:S(2)}) collective-permute-start(f32[128,1024]{1,0:T(8,128)S(1)} %get-tuple-element.21), channel_id=1, source_target_pairs={{1,2},{2,1},{5,6},{6,5},{9,10},{10,9},{13,14},{14,13},{17,18},{18,... | collective-permute-start | bytes 1572872 | tf_op jit(solution)/shard_map/ppermute | solution.py:550
  6.3 0.0 copy-done
  6.3 0.0 copy-done.1
  6.3 0.0 copy-done.2
  6.3 0.0 copy-done.3
  6.3 0.0 copy-done.4
  6.3 7.6 %interior.1 = (f32[256,1024]{1,0:T(8,128)}, f32[256,1024]{1,0:T(8,128)}, f32[256,1024]{1,0:T(8,128)}, f32[16,1024]{1,0:T(8,128)S(1)}, f32[320,128]{1,0:T(8,128)S...) custom-call(f32[256,1024]{1,0:T(8,128)S(1)} %copy-done, f32[256,1024]{1,0:T(8,128)S(1)} %copy-done.1, ...), custom_call_target="tpu_custom_call" | custom-call | flops 10485760 | bytes 8388608 | tf_op jit(solution)/shard_map/interior/pallas_call | solution.py:281
  13.9 0.0 collective-permute-done.ra
  13.9 0.0 collective-permute-done.1.rb
  13.9 0.6 %corners.1 = (f32[320,128]{1,0:T(8,128)S(1)}, f32[320,128]{1,0:T(8,128)S(1)}, f32[4,320,128]{2,1,0:T(8,128)S(1)}) custom-call(f32[128,1024]{1,0:T(8,128)S(1)} %collective-permute-done.ra, f32[128,1024]{1,0:T(8,128)S(1)} %collective-permute-done.1.rb, ...), custom_call_target="tpu_custom_call", output_to_operand_aliasing={{0}: (2, {}), {1}: (3, {}), {2}: (4, {})} | custom-call | tf_op jit(solution)/shard_map/corners/pallas_call | solution.py:345
  14.5 0.3 %collective-permute-start.2 = (f32[320,128]{1,0:T(8,128)S(1)}, f32[320,128]{1,0:T(8,128)S(1)}, u32[]{:S(2)}, u32[]{:S(2)}) collective-permute-start(f32[320,128]{1,0:T(8,128)S(1)} %get-tuple-element.25), channel_id=1, source_target_pairs={{0,4},{4,0},{8,12},{12,8},{16,20},{20,16},{24,28},{28,24},{1,5},{5... | collective-permute-start | bytes 491528 | tf_op jit(solution)/shard_map/ppermute | solution.py:550
  14.8 4.1 %collective-permute-start.3 = (f32[320,128]{1,0:T(8,128)S(1)}, f32[320,128]{1,0:T(8,128)S(1)}, u32[]{:S(2)}, u32[]{:S(2)}) collective-permute-start(f32[320,128]{1,0:T(8,128)S(1)} %get-tuple-element.26), channel_id=1, source_target_pairs={{4,8},{8,4},{12,16},{16,12},{20,24},{24,20},{5,9},{9,5},{13,17},{1... | collective-permute-start | bytes 491528 | tf_op jit(solution)/shard_map/ppermute | solution.py:550
  19.0 3.8 %strips.1 = (f32[256,1024]{1,0:T(8,128)}, f32[256,1024]{1,0:T(8,128)}, f32[256,1024]{1,0:T(8,128)}, f32[16,64]{1,0:T(8,128)S(1)}) custom-call(f32[256,1024]{1,0:T(8,128)S(1)} %copy-done, f32[256,1024]{1,0:T(8,128)S(1)} %copy-done.1, f32[256,1024]{1,0:T(8,128)S(1)} %copy-done.2, ...), custom_call_target="tpu_custom_call", output_to_operand_aliasing={{0}: (8, {}), {1}: (9, {}), {2}: (10, {})} | custom-call | flops 5242880 | bytes 4194304 | tf_op jit(solution)/shard_map/strips/pallas_call | solution.py:443
  22.8 0.0 copy-start.5
  22.8 0.0 collective-permute-done.2.rc
  22.8 0.0 collective-permute-done.3.rd
  22.8 0.7 %copy-done.5 = s32[16,64]{1,0:T(8,128)S(1)} copy-done((s32[16,64]{1,0:T(8,128)S(1)}, s32[16,64]{1,0:T(8,128)}, u32[]{:S(2)}) %copy-start.5) | copy-done | bytes 4120
  23.5 3.8 %columns.1 = (f32[256,1024]{1,0:T(8,128)}, f32[256,1024]{1,0:T(8,128)}, f32[256,1024]{1,0:T(8,128)}, f32[16,64]{1,0:T(8,128)}) custom-call(f32[320,128]{1,0:T(8,128)S(1)} %collective-permute-done.2.rc, f32[320,128]{1,0:T(8,128)S(1)} %collective-permute-done.3.rd, ...), custom_call_target="tpu_custom_call", output_to_operand_aliasing={{0}: (5, {}), {1}: (6, {}), {2}: (7, {})} | custom-call | tf_op jit(solution)/shard_map/columns/pallas_call | solution.py:526
Async XLA Ops:
  0.6 5.6 %copy-start = (f32[256,1024]{1,0:T(8,128)S(1)}, f32[256,1024]{1,0:T(8,128)}, u32[]{:S(2)}) copy-start(f32[256,1024]{1,0:T(8,128)} %s.5) | copy-start | bytes 3145732
  0.6 5.6 %copy-start.1 = (f32[256,1024]{1,0:T(8,128)S(1)}, f32[256,1024]{1,0:T(8,128)}, u32[]{:S(2)}) copy-start(f32[256,1024]{1,0:T(8,128)} %e.5) | copy-start | bytes 3145732
  0.7 5.6 %copy-start.2 = (f32[256,1024]{1,0:T(8,128)S(1)}, f32[256,1024]{1,0:T(8,128)}, u32[]{:S(2)}) copy-start(f32[256,1024]{1,0:T(8,128)} %n.5) | copy-start | bytes 3145732
  0.7 5.6 %copy-start.3 = (f32[256,1024]{1,0:T(8,128)S(1)}, f32[256,1024]{1,0:T(8,128)}, u32[]{:S(2)}) copy-start(f32[256,1024]{1,0:T(8,128)} %d.5) | copy-start | bytes 3145732
  0.7 5.6 %copy-start.4 = (s32[256,1024]{1,0:T(8,128)S(1)}, s32[256,1024]{1,0:T(8,128)}, u32[]{:S(2)}) copy-start(s32[256,1024]{1,0:T(8,128)} %m.5) | copy-start | bytes 3145732
  2.4 11.6 %collective-permute-start = (f32[128,1024]{1,0:T(8,128)S(1)}, f32[128,1024]{1,0:T(8,128)S(1)}, u32[]{:S(2)}, u32[]{:S(2)}) collective-permute-start(f32[128,1024]{1,0:T(8,128)S(1)} %get-tuple-element.20), channel_id=1, source_target_pairs={{0,1},{1,0},{2,3},{3,2},{4,5},{5,4},{6,7},{7,6},{8,9},{9,8},{10,11... | collective-permute-start | bytes 1572872 | tf_op jit(solution)/shard_map/ppermute | solution.py:550
  3.1 10.8 %collective-permute-start.1 = (f32[128,1024]{1,0:T(8,128)S(1)}, f32[128,1024]{1,0:T(8,128)S(1)}, u32[]{:S(2)}, u32[]{:S(2)}) collective-permute-start(f32[128,1024]{1,0:T(8,128)S(1)} %get-tuple-element.21), channel_id=1, source_target_pairs={{1,2},{2,1},{5,6},{6,5},{9,10},{10,9},{13,14},{14,13},{17,18},{18,... | collective-permute-start | bytes 1572872 | tf_op jit(solution)/shard_map/ppermute | solution.py:550
  14.5 8.3 %collective-permute-start.2 = (f32[320,128]{1,0:T(8,128)S(1)}, f32[320,128]{1,0:T(8,128)S(1)}, u32[]{:S(2)}, u32[]{:S(2)}) collective-permute-start(f32[320,128]{1,0:T(8,128)S(1)} %get-tuple-element.25), channel_id=1, source_target_pairs={{0,4},{4,0},{8,12},{12,8},{16,20},{20,16},{24,28},{28,24},{1,5},{5... | collective-permute-start | bytes 491528 | tf_op jit(solution)/shard_map/ppermute | solution.py:550
  14.8 8.0 %collective-permute-start.3 = (f32[320,128]{1,0:T(8,128)S(1)}, f32[320,128]{1,0:T(8,128)S(1)}, u32[]{:S(2)}, u32[]{:S(2)}) collective-permute-start(f32[320,128]{1,0:T(8,128)S(1)} %get-tuple-element.26), channel_id=1, source_target_pairs={{4,8},{8,4},{12,16},{16,12},{20,24},{24,20},{5,9},{9,5},{13,17},{1... | collective-permute-start | bytes 491528 | tf_op jit(solution)/shard_map/ppermute | solution.py:550
  22.8 0.7 %copy-start.5 = (s32[16,64]{1,0:T(8,128)S(1)}, s32[16,64]{1,0:T(8,128)}, u32[]{:S(2)}) copy-start(s32[16,64]{1,0:T(8,128)} %active.1) | copy-start | bytes 12292

commit v3 on v2

v3 whole, which is shorter than its diff:
```python
import functools

import jax
import jax.numpy as jnp
from jax import lax
from jax.experimental import pallas as pl
from jax.experimental.pallas import tpu as pltpu
from jax.sharding import PartitionSpec as P

SPACING = 16
STEPS = 3
COURANT = 0.5
LANES = 128
SUB = 8
HALO = 32
EDGE = 2 * STEPS
STRIP = HALO + 16
CHUNK = 64
F32 = jnp.float32
ANY = pl.BlockSpec(memory_space=pl.ANY)
HBM = pl.BlockSpec(memory_space=pltpu.HBM)
VMEM = pl.BlockSpec(memory_space=pltpu.VMEM)
PARAMS = pltpu.CompilerParams(vmem_limit_bytes=16 * 2**20)


def lane_index():
    return lax.broadcasted_iota(jnp.int32, (SUB, LANES), 1)


def east_minus_west(tiles):
    n = len(tiles)
    up = [pltpu.roll(t, LANES - 1, 1) for t in tiles]
    down = [pltpu.roll(t, 1, 1) for t in tiles]
    if n == 1:
        return [up[0] - down[0]]
    lane = lane_index()
    return [
        jnp.where(lane == LANES - 1, up[(c + 1) % n], up[c])
        - jnp.where(lane == 0, down[(c - 1) % n], down[c])
        for c in range(n)
    ]


def rows_at(ref, c, r):
    return ref[c, pl.ds(r, SUB), :]


def flux_rows(refs, r, tiles):
    S, E, N, Q, W = refs
    ds = east_minus_west([rows_at(S, c, r) for c in range(tiles)])
    for c in range(tiles):
        q = rows_at(Q, c, r)
        E[c, pl.ds(r, SUB), :] = rows_at(E, c, r) + q * ds[c]
        N[c, pl.ds(r, SUB), :] = rows_at(N, c, r) + q * (rows_at(S, c, r + 1) - rows_at(S, c, r - 1))


def surface_rows(refs, r, tiles, first):
    S, E, N, Q, W = refs
    de = east_minus_west([rows_at(E, c, r) for c in range(tiles)])
    for c in range(tiles):
        hw = rows_at(W, c, r)
        s = rows_at(S, c, r)
        if first:
            s = s * (hw + hw)
        S[c, pl.ds(r, SUB), :] = s + hw * (de[c] + (rows_at(N, c, r + 1) - rows_at(N, c, r - 1)))


def loop_rows(count, body, unroll=64):
    if unroll >= count:
        for i in range(count):
            body(SUB + i * SUB)
        return
    while count % unroll:
        unroll -= 1

    def step(i, carry):
        base = pl.multiple_of(i * (unroll * SUB), unroll * SUB) + SUB
        for u in range(unroll):
            body(base + u * SUB)
        return carry

    lax.fori_loop(0, count // unroll, step, 0)


def spline_weight(arg):
    mag = jnp.abs(arg)
    inner = 2.0 / 3.0 - mag * mag + 0.5 * mag * mag * mag
    outer = (2.0 - mag) * (2.0 - mag) * (2.0 - mag) / 6.0
    return jnp.where(mag < 1.0, inner, jnp.where(mag < 2.0, outer, 0.0 * mag))


def spline_of(cell, point):
    return spline_weight((cell.astype(F32) + 0.5) / SPACING - (point.astype(F32) + 0.5))


def dot(a, b):
    return jnp.dot(a, b, precision=lax.Precision.HIGHEST, preferred_element_type=F32)


def zero_borders(refs, rows, tiles):
    z = jnp.zeros((SUB, LANES), F32)
    for ref in refs:
        for c in range(tiles):
            ref[c, 0:SUB, :] = z
            ref[c, SUB + rows : SUB + rows + SUB, :] = z


def wait_all(copies):
    for copy in copies:
        copy.wait()


def is_even(axis):
    return lax.rem(lax.axis_index(axis), 2) == 0


def own_columns(first, last):
    lane = lane_index()
    both = jnp.where(lane < HALO, first, pltpu.roll(last, LANES // 2, 1))
    return jnp.where(lane < 2 * HALO, both, 0.0)


def masked(s, e, n, d, wet):
    return s, e * wet, n * wet, d * (COURANT * wet)


def pack_first_kernel(s, e, n, d, m, pa, pc, depth, mask, C, M, sem):
    rows, cols = s.shape
    even = is_even("lat")
    top = rows - HALO
    near, far = jnp.where(even, top, 0), jnp.where(even, 0, top)
    far = pl.ds(pl.multiple_of(far, SUB), HALO)
    near = pl.ds(pl.multiple_of(near, SUB), HALO)
    copies = []
    for f, src in enumerate((s, e, n, d, m)):
        for end, col in enumerate((0, cols - LANES)):
            dst = M.at[end] if f == 4 else C.at[f, end]
            copies.append(pltpu.make_async_copy(src.at[far, col : col + LANES], dst, sem.at[0]))
    for src, dst in (
        (s, pa.at[0:HALO]),
        (e, pa.at[HALO : 2 * HALO]),
        (n, pa.at[2 * HALO : 3 * HALO]),
        (d, depth),
        (m, mask),
    ):
        copies.append(pltpu.make_async_copy(src.at[near, :], dst, sem.at[1]))
    for copy in copies:
        copy.start()
    wait_all(copies[:10])
    for r in range(0, HALO, SUB):
        ends = [
            masked(*(C[f, end, r : r + SUB, :] for f in range(4)), M[end, r : r + SUB, :].astype(F32))
            for end in range(2)
        ]
        mine = [own_columns(a, b) for a, b in zip(*ends)]
        for half in range(2):
            pair = mine[2 * half] + pltpu.roll(mine[2 * half + 1], LANES // 2, 1)
            pc[half * HALO + r : half * HALO + r + SUB, :] = pair
    wait_all(copies[10:])
    wet = mask[...].astype(F32)
    pa[HALO : 2 * HALO] = pa[HALO : 2 * HALO] * wet
    pa[2 * HALO : 3 * HALO] = pa[2 * HALO : 3 * HALO] * wet
    pa[3 * HALO : 4 * HALO] = depth[...] * (COURANT * wet)


def pack_first(s, e, n, d, m):
    rows, cols = s.shape
    return pl.pallas_call(
        pack_first_kernel,
        out_shape=[jax.ShapeDtypeStruct((4 * HALO, cols), F32), jax.ShapeDtypeStruct((2 * HALO, LANES), F32)],
        in_specs=[ANY] * 5,
        out_specs=[VMEM] * 2,
        scratch_shapes=[
            pltpu.VMEM((HALO, cols), F32),
            pltpu.VMEM((HALO, cols), jnp.int32),
            pltpu.VMEM((4, 2, HALO, LANES), F32),
            pltpu.VMEM((2, HALO, LANES), jnp.int32),
            pltpu.SemaphoreType.DMA((2,)),
        ],
        compiler_params=PARAMS,
        name="pack_first",
    )(*(in_hbm(x) for x in (s, e, n, d, m)))


def in_hbm(x):
    return pltpu.with_memory_space_constraint(x, pltpu.HBM)


def pack_columns(own, even):
    group = lax.div(lane_index(), HALO)
    shift = jnp.where(even, 1, 0)
    pc = pd = None
    for f, tile in enumerate(own):
        turn = (f + 2) % 4
        moved = pltpu.roll(tile, turn * HALO, 1) if turn else tile
        if pc is None:
            pc = pd = moved
        else:
            pc = jnp.where(group == lax.rem(turn + shift, 4), moved, pc)
            pd = jnp.where(group == lax.rem(turn + 1 - shift, 4), moved, pd)
    return pc, pd


def edge_kernel(s, e, n, d, m, pb, pc, pd, own, PC, PD, OWN, sem):
    rows, cols = s.shape
    lat_even, lon_even = is_even("lat"), is_even("lon")
    far = pl.multiple_of(jnp.where(lat_even, 0, rows - HALO), SUB)
    for r in range(0, HALO, SUB):
        at = pl.ds(far + r, SUB)
        wet = m[at, :].astype(F32)
        for f, value in enumerate(masked(s[at, :], e[at, :], n[at, :], d[at, :], wet)):
            pb[f * HALO + r : f * HALO + r + SUB, :] = value

    def pack(r):
        at = pl.ds(r - SUB, SUB)
        ends = []
        for col in (0, cols - LANES):
            to = slice(col, col + LANES)
            ends.append(masked(s[at, to], e[at, to], n[at, to], d[at, to], m[at, to].astype(F32)))
        mine = [own_columns(a, b) for a, b in zip(*ends)]
        for f in range(4):
            OWN[f, at, :] = mine[f]
        PC[at, :], PD[at, :] = pack_columns(mine, lon_even)

    loop_rows(rows // SUB, pack, 8)
    sends = [
        pltpu.make_async_copy(PC, pc.at[HALO : HALO + rows], sem.at[0]),
        pltpu.make_async_copy(PD, pd.at[HALO : HALO + rows], sem.at[1]),
        pltpu.make_async_copy(OWN, own.at[:, HALO : HALO + rows], sem.at[2]),
    ]
    for copy in sends:
        copy.start()
    wait_all(sends)


def edges(s, e, n, d, m):
    rows, cols = s.shape
    wide = jax.ShapeDtypeStruct((rows + 2 * HALO, LANES), F32)
    return pl.pallas_call(
        edge_kernel,
        out_shape=[
            jax.ShapeDtypeStruct((4 * HALO, cols), F32),
            wide,
            wide,
            jax.ShapeDtypeStruct((4, rows + 2 * HALO, LANES), F32),
        ],
        in_specs=[VMEM] * 5,
        out_specs=[VMEM] + [ANY] * 3,
        scratch_shapes=[
            pltpu.VMEM((rows, LANES), F32),
            pltpu.VMEM((rows, LANES), F32),
            pltpu.VMEM((4, rows, LANES), F32),
            pltpu.SemaphoreType.DMA((3,)),
        ],
        compiler_params=PARAMS,
        name="edges",
    )(s, e, n, d, m)


def corner_kernel(ra, rbc, pc_in, pd_in, own_in, pc, pd, own, PC, PD, OWN, sem):
    del pc_in, pd_in, own_in
    height = pc.shape[0]
    cols = ra.shape[1]
    even, lon_even = is_even("lat"), is_even("lon")
    top = height - HALO
    starts = (jnp.where(even, top, 0), jnp.where(even, 0, top))
    sends = []
    lane = lane_index()
    for side, row in enumerate(starts):
        for r in range(0, HALO, SUB):
            if side == 0:
                mine = [
                    own_columns(
                        ra[f * HALO + r : f * HALO + r + SUB, 0:LANES],
                        ra[f * HALO + r : f * HALO + r + SUB, cols - LANES : cols],
                    )
                    for f in range(4)
                ]
            else:
                mine = []
                for half in range(2):
                    pair = rbc[half * HALO + r : half * HALO + r + SUB, :]
                    for tile in (pair, pltpu.roll(pair, LANES // 2, 1)):
                        mine.append(jnp.where(lane < 2 * HALO, tile, 0.0))
            for f in range(4):
                OWN[side, f, r : r + SUB, :] = mine[f]
            PC[side, r : r + SUB, :], PD[side, r : r + SUB, :] = pack_columns(mine, lon_even)
        at = pl.ds(pl.multiple_of(row, SUB), HALO)
        for f, (src, dst) in enumerate(
            ((PC.at[side], pc.at[at, :]), (PD.at[side], pd.at[at, :]), (OWN.at[side], own.at[:, at, :]))
        ):
            copy = pltpu.make_async_copy(src, dst, sem.at[side, f])
            copy.start()
            sends.append(copy)
    wait_all(sends)


def corners(ra, rbc, pc, pd, own):
    return pl.pallas_call(
        corner_kernel,
        out_shape=[jax.ShapeDtypeStruct(x.shape, F32) for x in (pc, pd, own)],
        in_specs=[VMEM] * 2 + [ANY] * 3,
        out_specs=[ANY] * 3,
        scratch_shapes=[
            pltpu.VMEM((2, HALO, LANES), F32),
            pltpu.VMEM((2, HALO, LANES), F32),
            pltpu.VMEM((2, 4, HALO, LANES), F32),
            pltpu.SemaphoreType.DMA((2, 3)),
        ],
        input_output_aliases={2: 0, 3: 1, 4: 2},
        compiler_params=PARAMS,
        name="corners",
    )(ra, rbc, pc, pd, own)


def interior_kernel(s, e, n, d, m, S, E, N, u, Q, W, isem):
    rows, cols = e.shape
    tiles = cols // LANES
    chunks = rows // CHUNK
    refs = (S, E, N, Q, W)
    loads = []
    for k in range(chunks):
        loads.append([])
        for c in range(tiles):
            copy = pltpu.make_async_copy(
                s.at[k * CHUNK : (k + 1) * CHUNK, c * LANES : (c + 1) * LANES],
                S.at[c, SUB + k * CHUNK : SUB + (k + 1) * CHUNK, :],
                isem.at[k],
            )
            copy.start()
            loads[-1].append(copy)
    zero_borders((S, N), rows, tiles)

    def first_flux(r):
        ds = east_minus_west([rows_at(S, c, r) for c in range(tiles)])
        at = pl.ds(r - SUB, SUB)
        for c in range(tiles):
            to = slice(c * LANES, (c + 1) * LANES)
            wet = m[at, to].astype(F32)
            hw = COURANT * wet
            q = d[at, to] * hw
            W[c, pl.ds(r, SUB), :] = hw
            Q[c, pl.ds(r, SUB), :] = q
            E[c, pl.ds(r, SUB), :] = e[at, to] * wet + q * ds[c]
            N[c, pl.ds(r, SUB), :] = n[at, to] * wet + q * (rows_at(S, c, r + 1) - rows_at(S, c, r - 1))

    def over_chunk(k, body):
        def shifted(r):
            body(pl.multiple_of(r + k * CHUNK, SUB))

        loop_rows(CHUNK // SUB, shifted)

    wait_all(loads[0])
    for k in range(chunks):
        if k + 1 < chunks:
            wait_all(loads[k + 1])
        over_chunk(k, first_flux)
    loop_rows(rows // SUB, lambda r: surface_rows(refs, r, tiles, True))
    for step in range(1, STEPS):
        loop_rows(rows // SUB, lambda r: flux_rows(refs, r, tiles))
        loop_rows(rows // SUB, lambda r: surface_rows(refs, r, tiles, False))
    points = rows // SPACING
    cell = lax.broadcasted_iota(jnp.int32, (points, rows), 1)
    table = spline_of(cell, lax.broadcasted_iota(jnp.int32, (points, rows), 0))
    table = jnp.where((cell >= EDGE) & (cell < rows - EDGE), table, 0.0)
    for c in range(tiles):
        u[:, c * LANES : (c + 1) * LANES] = dot(table, S[c, SUB : SUB + rows, :])


def interior(s, e, n, d, m):
    rows, cols = s.shape
    tiles = cols // LANES
    field = (tiles, rows + 2 * SUB, LANES)
    return pl.pallas_call(
        interior_kernel,
        out_shape=[jax.ShapeDtypeStruct(field, F32)] * 3 + [jax.ShapeDtypeStruct((rows // SPACING, cols), F32)],
        in_specs=[ANY] + [VMEM] * 4,
        out_specs=[VMEM] * 4,
        scratch_shapes=[pltpu.VMEM(field, F32)] * 2 + [pltpu.SemaphoreType.DMA((rows // CHUNK,))],
        cost_estimate=pl.CostEstimate(flops=40 * rows * cols, bytes_accessed=32 * rows * cols, transcendentals=0),
        compiler_params=PARAMS,
        name="interior",
    )(s, e, n, d, m)


def strip_kernel(s, e, n, d, m, ra, rb, u, si, ei, ni, so, eo, no, v, x, S, E, N, Q, W, osem):
    rows, cols = s.shape
    tiles = cols // LANES
    refs = (S, E, N, Q, W)
    even = is_even("lat")
    keep = STRIP - HALO
    count = 2 * STRIP
    sends = []
    for src, dst in ((ei, eo), (ni, no), (si, so)):
        for c in range(1, tiles - 1):
            copy = pltpu.make_async_copy(
                src.at[c, 2 * SUB : rows, :], dst.at[SUB : rows - SUB, c * LANES : (c + 1) * LANES], osem.at[0]
            )
            copy.start()
            sends.append(copy)
    zero_borders((S, N), count, tiles)
    for row, to in ((0, SUB + HALO), (rows - keep, SUB + STRIP)):
        for r in range(0, keep, SUB):
            for c in range(tiles):
                at, lanes = slice(row + r, row + r + SUB), slice(c * LANES, (c + 1) * LANES)
                wet = m[at, lanes].astype(F32)
                hw = COURANT * wet
                here = slice(to + r, to + r + SUB)
                S[c, here, :] = s[at, lanes]
                E[c, here, :] = e[at, lanes] * wet
                N[c, here, :] = n[at, lanes] * wet
                Q[c, here, :] = d[at, lanes] * hw
                W[c, here, :] = hw
    high = SUB + STRIP + keep
    for src, to in ((ra, jnp.where(even, high, SUB)), (rb, jnp.where(even, SUB, high))):
        for r in range(0, HALO, SUB):
            here = pl.ds(pl.multiple_of(to + r, SUB), SUB)
            for c in range(tiles):
                for f, dst in enumerate((S, E, N, Q)):
                    value = src[f * HALO + r : f * HALO + r + SUB, c * LANES : (c + 1) * LANES]
                    dst[c, here, :] = value
                W[c, here, :] = jnp.where(value > 0.0, COURANT, 0.0)
    for step in range(STEPS):
        loop_rows(count // SUB, lambda r: flux_rows(refs, r, tiles), 12)
        loop_rows(count // SUB, lambda r: surface_rows(refs, r, tiles, step == 0), 12)
    for f, (src, dst) in enumerate(((S, so), (E, eo), (N, no))):
        for side, (frm, to) in enumerate(((SUB + HALO, 0), (SUB + STRIP + keep - SUB, rows - SUB))):
            for c in range(tiles):
                if c in (0, tiles - 1):
                    x[f, min(c, 1), side] = src[c, frm : frm + SUB, :]
                    continue
                copy = pltpu.make_async_copy(
                    src.at[c, frm : frm + SUB, :],
                    dst.at[to : to + SUB, c * LANES : (c + 1) * LANES],
                    osem.at[0],
                )
                copy.start()
                sends.append(copy)
    points = rows // SPACING
    index = lax.broadcasted_iota(jnp.int32, (points, count), 1)
    cell = jnp.where(index < STRIP, index - HALO, index + (rows - keep - STRIP))
    table = spline_of(cell, lax.broadcasted_iota(jnp.int32, (points, count), 0))
    table = jnp.where((cell < EDGE) | (cell >= rows - EDGE), table, 0.0)
    lane = lax.broadcasted_iota(jnp.int32, (points, LANES), 1)
    parts = []
    for c in range(tiles):
        part = u[:, c * LANES : (c + 1) * LANES] + dot(table, S[c, SUB : SUB + count, :])
        if c == 0:
            part = jnp.where(lane < EDGE, 0.0, part)
        if c == tiles - 1:
            part = jnp.where(lane >= LANES - EDGE, 0.0, part)
        parts.append(part)
    weights = spline_of(
        lax.broadcasted_iota(jnp.int32, (LANES, LANES), 0),
        lax.broadcasted_iota(jnp.int32, (LANES, LANES), 1) - 2,
    )
    product = dot(jnp.concatenate(parts, axis=0), weights)
    total = jnp.zeros((points, LANES), F32)
    reach = LANES // SPACING + 4
    for c in range(tiles):
        piece = jnp.where(lane < reach, product[c * points : (c + 1) * points], 0.0)
        total = total + pltpu.roll(piece, (c * (LANES // SPACING) - 2) % LANES, 1)
    v[...] = total
    wait_all(sends)


def strips(s, e, n, d, m, ra, rb, u, si, ei, ni):
    rows, cols = s.shape
    tiles = cols // LANES
    field = jax.ShapeDtypeStruct((rows, cols), F32)
    return pl.pallas_call(
        strip_kernel,
        out_shape=[field] * 3
        + [
            jax.ShapeDtypeStruct((rows // SPACING, LANES), F32),
            jax.ShapeDtypeStruct((3, 2, 2, SUB, LANES), F32),
        ],
        in_specs=[VMEM] * 8 + [ANY] * 3,
        out_specs=[ANY] * 3 + [VMEM] * 2,
        scratch_shapes=[pltpu.VMEM((tiles, 2 * STRIP + 2 * SUB, LANES), F32)] * 5
        + [pltpu.SemaphoreType.DMA((1,))],
        cost_estimate=pl.CostEstimate(flops=20 * rows * cols, bytes_accessed=16 * rows * cols, transcendentals=0),
        compiler_params=PARAMS,
        name="strips",
    )(s, e, n, d, m, ra, rb, u, si, ei, ni)


def column_kernel(
    rc, rd, own, v, si, ei, ni, xs, active, so_in, eo_in, no_in, so, eo, no, grad, S, E, N, Q, W, X, A, sem, osem
):
    del so_in, eo_in, no_in
    rows, cols = so.shape
    height = rows + 2 * HALO
    refs = (S, E, N, Q, W)
    even = is_even("lon")
    fetch = pltpu.make_async_copy(active, A, sem.at[0])
    fetch.start()
    zero_borders((S, N), height, 1)
    group = lax.div(lane_index(), HALO)

    def unpack(r):
        at = pl.ds(r - SUB, SUB)
        c, d = rc[at, :], rd[at, :]
        right, left = jnp.where(even, c, d), jnp.where(even, d, c)
        for f, dst in enumerate((S, E, N, Q)):
            a, b = right, left
            if f:
                a, b = pltpu.roll(a, LANES - f * HALO, 1), pltpu.roll(b, LANES - f * HALO, 1)
            tile = jnp.where(group == 2, a, jnp.where(group == 3, b, own[f, at, :]))
            dst[0, pl.ds(r, SUB), :] = tile
            if f == 3:
                W[0, pl.ds(r, SUB), :] = jnp.where(tile > 0.0, COURANT, 0.0)

    loop_rows(height // SUB, unpack, 40)
    lane = lane_index()
    sends = []

    def merge(fields):
        def body(r, i=None):
            at = pl.ds(r - SUB, SUB)
            for f in fields:
                tile = (S, E, N)[f][0, pl.ds(r + HALO, SUB), :]
                xi, tiles = (si, ei, ni)[f], cols // LANES
                first, last = (
                    xi[end * (tiles - 1), pl.ds(r, SUB), :] if i is None else xs[f, end, i] for end in range(2)
                )
                X[f, 0, at, :] = jnp.where(lane < EDGE, tile, first)
                X[f, 1, at, :] = jnp.where(lane >= LANES - EDGE, pltpu.roll(tile, LANES // 2, 1), last)

        loop_rows(rows // SUB, body, 32)
        body(SUB, 0)
        body(rows, 1)
        for f in fields:
            for end, col in enumerate((0, cols - LANES)):
                copy = pltpu.make_async_copy(X.at[f, end], (so, eo, no)[f].at[:, col : col + LANES], osem.at[f, end])
                copy.start()
                sends.append(copy)

    for step in range(STEPS):
        loop_rows(height // SUB, lambda r: flux_rows(refs, r, 1), 40)
        if step == STEPS - 1:
            merge((1, 2))
        loop_rows(height // SUB, lambda r: surface_rows(refs, r, 1, step == 0), 40)
    merge((0,))
    points, across = grad.shape
    cell = lax.broadcasted_iota(jnp.int32, (points, height), 1) - HALO
    table = spline_of(cell, lax.broadcasted_iota(jnp.int32, (points, height), 0))
    part = dot(table, S[0, SUB : SUB + height, :])
    index = lax.broadcasted_iota(jnp.int32, (LANES, across), 0)
    col = jnp.where(index < HALO, index, jnp.where(index < 3 * HALO, index + (cols - 2 * HALO), index - LANES))
    weights = spline_of(col, lax.broadcasted_iota(jnp.int32, (LANES, across), 1))
    weights = jnp.where((col < EDGE) | (col >= cols - EDGE), weights, 0.0)
    sums = v[:, 0:across] + dot(part, weights)
    fetch.wait()
    grad[...] = sums * A[...].astype(F32) / SPACING
    wait_all(sends)


def columns(rc, rd, own, v, si, ei, ni, xs, active, so, eo, no):
    rows, cols = so.shape
    height = rows + 2 * HALO
    field = jax.ShapeDtypeStruct((rows, cols), F32)
    return pl.pallas_call(
        column_kernel,
        out_shape=[field] * 3 + [jax.ShapeDtypeStruct(active.shape, F32)],
        in_specs=[VMEM] * 8 + [ANY] * 4,
        out_specs=[ANY] * 3 + [VMEM],
        scratch_shapes=[pltpu.VMEM((1, height + 2 * SUB, LANES), F32)] * 5
        + [
            pltpu.VMEM((3, 2, rows, LANES), F32),
            pltpu.VMEM(active.shape, jnp.int32),
            pltpu.SemaphoreType.DMA((1,)),
            pltpu.SemaphoreType.DMA((3, 2)),
        ],
        input_output_aliases={9: 0, 10: 1, 11: 2},
        compiler_params=PARAMS,
        name="columns",
    )(rc, rd, own, v, si, ei, ni, xs, in_hbm(active), so, eo, no)


def swap(array, axis, offset):
    size = lax.axis_size(axis)
    pairs = []
    for i in range(offset, size):
        j = ((i - offset) ^ 1) + offset
        if j < size:
            pairs.append((i, j))
    return lax.ppermute(array, axis, pairs)


def local(surface_adjoint, east_adjoint, north_adjoint, water_depth, wet_mask, control_active):
    fields = (surface_adjoint, east_adjoint, north_adjoint, water_depth, wet_mask)
    pa, pbc = pack_first(*fields)
    ra = swap(pa, "lat", 0)
    rbc = swap(pbc, "lat", 1)
    pb, pc, pd, own = edges(*fields)
    rb = swap(pb, "lat", 1)
    pc, pd, own = corners(ra, rbc, pc, pd, own)
    rc = swap(pc, "lon", 0)
    rd = swap(pd, "lon", 1)
    si, ei, ni, u = interior(*fields)
    so, eo, no, v, xs = strips(*fields, ra, rb, u, si, ei, ni)
    return columns(rc, rd, own, v, si, ei, ni, xs, control_active, so, eo, no)


def solution(mesh):
    spec = P("lat", "lon")
    return jax.shard_map(
        lambda *args: tuple(local(*args)),
        mesh=mesh,
        in_specs=(spec,) * 6,
        out_specs=(spec,) * 4,
        check_vma=False,
    )
```

time: 27.4 us -> 31.6 us (1.15)
  the two profiles are of different devices: /device:TPU:5 before, /device:TPU:6 now
where the time goes in v3:
time: 31.6 us; the launch traced here: 31.4 us
  Pallas kernels  13.4 us (42%)
  starting transfers between devices  10.6 us (34%)
  waiting for transfers between devices  5.28 us (17%)
  local copies, waits for them, and re-layouts  1.29 us (4%)
  between operations  0.77 us (2%)
    ppermute x5, starting transfers between devices, swap(): return lax.ppermute(array, axis, pairs)  10.6 us
    ppermute x5, waiting for transfers between devices, swap(): return lax.ppermute(array, axis, pairs)  5.28 us
    pallas_call x1, Pallas kernels, interior(): pl.pallas_call(interior_kernel, out_shape=[jax.ShapeDtypeStruct(field, F3...  4.95 us
    pallas_call x1, Pallas kernels, strips(): pl.pallas_call(strip_kernel, out_shape=[field] * 3 + [jax.ShapeDtypeStruc...  2.8 us
    pallas_call x1, Pallas kernels, columns(): pl.pallas_call(column_kernel, out_shape=[field] * 3 + [jax.ShapeDtypeStru...  2.58 us
    pallas_call x1, Pallas kernels, pack_first(): pl.pallas_call(pack_first_kernel, out_shape=[jax.ShapeDtypeStruct((4 * HA...  1.43 us
    unnamed x10, local copies, waits for them, and re-layouts  1.29 us
    pallas_call x1, Pallas kernels, edges(): pl.pallas_call(edge_kernel, out_shape=[jax.ShapeDtypeStruct((4 * HALO, co...  1.18 us
  transfers between devices with their start and end apart: 5, of which 1 were waited for; matrix products, arithmetic and copies ran while one was open for 0% of the time, Pallas kernels for 30%

profile of v3, /device:TPU:6, one launch (start us, length us, event | category | flops | bytes accessed | tf_op | source)
XLA Modules:
  0.0 31.4 jit_solution(16269505430648193052)
XLA Ops:
  0.6 0.0 copy-start.4
  0.6 0.0 copy-start.3
  0.7 0.0 copy-start.2
  0.7 0.0 copy-start.1
  0.7 0.0 copy-start
  0.7 1.4 %pack_first.1 = (f32[128,1024]{1,0:T(8,128)S(1)}, f32[64,128]{1,0:T(8,128)S(1)}) custom-call(f32[256,1024]{1,0:T(8,128)} %s.7, f32[256,1024]{1,0:T(8,128)} %e.7, f32[256,1024]{1,0:T(8,128)} %n.7, f32[256,1024]{1,0:T(8,128)} %d.7, s32[256,1024]{1,0:T(8,128)} %m.7), custom_call_target="tpu_custom_call" | custom-call | tf_op jit(solution)/shard_map/pack_first/pallas_call | solution.py:168
  2.1 0.1 collective-permute-start
  2.2 0.0 copy-done.4
  2.2 0.3 %copy-done.3 = f32[256,1024]{1,0:T(8,128)S(1)} copy-done((f32[256,1024]{1,0:T(8,128)S(1)}, f32[256,1024]{1,0:T(8,128)}, u32[]{:S(2)}) %copy-start.3) | copy-done | bytes 1048600
  2.5 0.3 %copy-done.2 = f32[256,1024]{1,0:T(8,128)S(1)} copy-done((f32[256,1024]{1,0:T(8,128)S(1)}, f32[256,1024]{1,0:T(8,128)}, u32[]{:S(2)}) %copy-start.2) | copy-done | bytes 1048600
  2.8 0.3 %copy-done.1 = f32[256,1024]{1,0:T(8,128)S(1)} copy-done((f32[256,1024]{1,0:T(8,128)S(1)}, f32[256,1024]{1,0:T(8,128)}, u32[]{:S(2)}) %copy-start.1) | copy-done | bytes 1048600
  3.2 0.3 %copy-done = f32[256,1024]{1,0:T(8,128)S(1)} copy-done((f32[256,1024]{1,0:T(8,128)S(1)}, f32[256,1024]{1,0:T(8,128)}, u32[]{:S(2)}) %copy-start) | copy-done | bytes 1048600
  3.5 1.2 %edges.1 = (f32[128,1024]{1,0:T(8,128)S(1)}, f32[320,128]{1,0:T(8,128)S(1)}, f32[320,128]{1,0:T(8,128)S(1)}, f32[4,320,128]{2,1,0:T(8,128)S(1)}) custom-call(f32[256,1024]{1,0:T(8,128)S(1)} %copy-done, f32[256,1024]{1,0:T(8,128)S(1)} %copy-done.1, f32[256,1024]{1,0:T(8,128)S(1)} %copy-done.2, f32[256,1024]{1,0:T(8,128)S(1)} %copy-done.3, ...), custom_call_target="tpu_custom_call" | custom-call | tf_op jit(solution)/shard_map/edges/pallas_call | solution.py:239
  4.7 1.9 %collective-permute-start.4 = (f32[128,1024]{1,0:T(8,128)S(1)}, f32[128,1024]{1,0:T(8,128)S(1)}, u32[]{:S(2)}, u32[]{:S(2)}) collective-permute-start(f32[128,1024]{1,0:T(8,128)S(1)} %get-tuple-element.30), channel_id=1, source_target_pairs={{1,2},{2,1},{5,6},{6,5},{9,10},{10,9},{13,14},{14,13},{17,18},{18,... | collective-permute-start | bytes 1572872 | tf_op jit(solution)/shard_map/ppermute | solution.py:588
  6.6 3.6 %collective-permute-start.1 = (f32[64,128]{1,0:T(8,128)S(1)}, f32[64,128]{1,0:T(8,128)S(1)}, u32[]{:S(2)}, u32[]{:S(2)}) collective-permute-start(f32[64,128]{1,0:T(8,128)S(1)} %get-tuple-element.23), channel_id=1, source_target_pairs={{1,2},{2,1},{5,6},{6,5},{9,10},{10,9},{13,14},{14,13},{17,18},{18,... | collective-permute-start | bytes 98312 | tf_op jit(solution)/shard_map/ppermute | solution.py:588
  10.2 5.3 %collective-permute-done.1.rbc = f32[64,128]{1,0:T(8,128)S(1)} collective-permute-done((f32[64,128]{1,0:T(8,128)S(1)}, f32[64,128]{1,0:T(8,128)S(1)}, u32[]{:S(2)}, u32[]{:S(2)}) %collective-permute-start.1) | collective-permute-done | bytes 32800 | tf_op jit(solution)/shard_map/ppermute | solution.py:588
  15.5 0.0 collective-permute-done.ra
  15.5 0.5 %corners.1 = (f32[320,128]{1,0:T(8,128)S(1)}, f32[320,128]{1,0:T(8,128)S(1)}, f32[4,320,128]{2,1,0:T(8,128)S(1)}) custom-call(f32[128,1024]{1,0:T(8,128)S(1)} %collective-permute-done.ra, f32[64,128]{1,0:T(8,128)S(1)} %collective-permute-done.1.rbc, ...), custom_call_target="tpu_custom_call", output_to_operand_aliasing={{0}: (2, {}), {1}: (3, {}), {2}: (4, {})} | custom-call | tf_op jit(solution)/shard_map/corners/pallas_call | solution.py:299
  16.0 0.6 %collective-permute-start.2 = (f32[320,128]{1,0:T(8,128)S(1)}, f32[320,128]{1,0:T(8,128)S(1)}, u32[]{:S(2)}, u32[]{:S(2)}) collective-permute-start(f32[320,128]{1,0:T(8,128)S(1)} %get-tuple-element.27), channel_id=1, source_target_pairs={{0,4},{4,0},{8,12},{12,8},{16,20},{20,16},{24,28},{28,24},{1,5},{5... | collective-permute-start | bytes 491528 | tf_op jit(solution)/shard_map/ppermute | solution.py:588
  16.6 4.4 %collective-permute-start.3 = (f32[320,128]{1,0:T(8,128)S(1)}, f32[320,128]{1,0:T(8,128)S(1)}, u32[]{:S(2)}, u32[]{:S(2)}) collective-permute-start(f32[320,128]{1,0:T(8,128)S(1)} %get-tuple-element.28), channel_id=1, source_target_pairs={{4,8},{8,4},{12,16},{16,12},{20,24},{24,20},{5,9},{9,5},{13,17},{1... | collective-permute-start | bytes 491528 | tf_op jit(solution)/shard_map/ppermute | solution.py:588
  21.0 4.9 %interior.1 = (f32[8,272,128]{2,1,0:T(8,128)S(1)}, f32[8,272,128]{2,1,0:T(8,128)S(1)}, f32[8,272,128]{2,1,0:T(8,128)S(1)}, f32[16,1024]{1,0:T(8,128)S(1)}) custom-call(f32[256,1024]{1,0:T(8,128)S(1)} %copy-done, f32[256,1024]{1,0:T(8,128)S(1)} %copy-done.1, f32[256,1024]{1,0:T(8,128)S(1)} %copy-done.2, f32[256,1024]{1,0:T(8,128)S(1)} %copy-done.3, ...), custom_call_target="tpu_custom_call" | custom-call | flops 10485760 | bytes 8388608 | tf_op jit(solution)/shard_map/interior/pallas_call | solution.py:374
  26.0 0.0 collective-permute-done.4.rb
  26.0 2.8 %strips.1 = (f32[256,1024]{1,0:T(8,128)}, f32[256,1024]{1,0:T(8,128)}, f32[256,1024]{1,0:T(8,128)}, f32[16,128]{1,0:T(8,128)S(1)}, f32[3,2,2,8,128]{4,3,2,1,0:T(8,128)S(1)}) custom-call(f32[256,1024]{1,0:T(8,128)S(1)} %copy-done, f32[256,1024]{1,0:T(8,128)S(1)} %copy-done.1, f32[256,1024]{1,0:T(8,128)S(1)} %copy-done.2, f32[256,1024]{1,0:T(8,128)S(1)} %copy-done.3, ...), custom_call_target="tpu_custom_call" | custom-call | flops 5242880 | bytes 4194304 | tf_op jit(solution)/shard_map/strips/pallas_call | solution.py:471
  28.8 0.0 collective-permute-done.2.rc
  28.8 0.0 collective-permute-done.3.rd
  28.8 2.6 %columns.1 = (f32[256,1024]{1,0:T(8,128)}, f32[256,1024]{1,0:T(8,128)}, f32[256,1024]{1,0:T(8,128)}, f32[16,64]{1,0:T(8,128)}) custom-call(f32[320,128]{1,0:T(8,128)S(1)} %collective-permute-done.2.rc, f32[320,128]{1,0:T(8,128)S(1)} %collective-permute-done.3.rd, ...), custom_call_target="tpu_custom_call", output_to_operand_aliasing={{0}: (9, {}), {1}: (10, {}), {2}: (11, {})} | custom-call | tf_op jit(solution)/shard_map/columns/pallas_call | solution.py:563
Async XLA Ops:
  0.6 1.6 %copy-start.4 = (s32[256,1024]{1,0:T(8,128)S(1)}, s32[256,1024]{1,0:T(8,128)}, u32[]{:S(2)}) copy-start(s32[256,1024]{1,0:T(8,128)} %m.7) | copy-start | bytes 3145732
  0.6 1.9 %copy-start.3 = (f32[256,1024]{1,0:T(8,128)S(1)}, f32[256,1024]{1,0:T(8,128)}, u32[]{:S(2)}) copy-start(f32[256,1024]{1,0:T(8,128)} %d.7) | copy-start | bytes 3145732
  0.7 2.2 %copy-start.2 = (f32[256,1024]{1,0:T(8,128)S(1)}, f32[256,1024]{1,0:T(8,128)}, u32[]{:S(2)}) copy-start(f32[256,1024]{1,0:T(8,128)} %n.7) | copy-start | bytes 3145732
  0.7 2.5 %copy-start.1 = (f32[256,1024]{1,0:T(8,128)S(1)}, f32[256,1024]{1,0:T(8,128)}, u32[]{:S(2)}) copy-start(f32[256,1024]{1,0:T(8,128)} %e.7) | copy-start | bytes 3145732
  0.7 2.8 %copy-start = (f32[256,1024]{1,0:T(8,128)S(1)}, f32[256,1024]{1,0:T(8,128)}, u32[]{:S(2)}) copy-start(f32[256,1024]{1,0:T(8,128)} %s.7) | copy-start | bytes 3145732
  2.1 13.4 %collective-permute-start = (f32[128,1024]{1,0:T(8,128)S(1)}, f32[128,1024]{1,0:T(8,128)S(1)}, u32[]{:S(2)}, u32[]{:S(2)}) collective-permute-start(f32[128,1024]{1,0:T(8,128)S(1)} %get-tuple-element.22), channel_id=1, source_target_pairs={{0,1},{1,0},{2,3},{3,2},{4,5},{5,4},{6,7},{7,6},{8,9},{9,8},{10,11... | collective-permute-start | bytes 1572872 | tf_op jit(solution)/shard_map/ppermute | solution.py:588
  4.7 21.3 %collective-permute-start.4 = (f32[128,1024]{1,0:T(8,128)S(1)}, f32[128,1024]{1,0:T(8,128)S(1)}, u32[]{:S(2)}, u32[]{:S(2)}) collective-permute-start(f32[128,1024]{1,0:T(8,128)S(1)} %get-tuple-element.30), channel_id=1, source_target_pairs={{1,2},{2,1},{5,6},{6,5},{9,10},{10,9},{13,14},{14,13},{17,18},{18,... | collective-permute-start | bytes 1572872 | tf_op jit(solution)/shard_map/ppermute | solution.py:588
  6.6 8.9 %collective-permute-start.1 = (f32[64,128]{1,0:T(8,128)S(1)}, f32[64,128]{1,0:T(8,128)S(1)}, u32[]{:S(2)}, u32[]{:S(2)}) collective-permute-start(f32[64,128]{1,0:T(8,128)S(1)} %get-tuple-element.23), channel_id=1, source_target_pairs={{1,2},{2,1},{5,6},{6,5},{9,10},{10,9},{13,14},{14,13},{17,18},{18,... | collective-permute-start | bytes 98312 | tf_op jit(solution)/shard_map/ppermute | solution.py:588
  16.0 12.8 %collective-permute-start.2 = (f32[320,128]{1,0:T(8,128)S(1)}, f32[320,128]{1,0:T(8,128)S(1)}, u32[]{:S(2)}, u32[]{:S(2)}) collective-permute-start(f32[320,128]{1,0:T(8,128)S(1)} %get-tuple-element.27), channel_id=1, source_target_pairs={{0,4},{4,0},{8,12},{12,8},{16,20},{20,16},{24,28},{28,24},{1,5},{5... | collective-permute-start | bytes 491528 | tf_op jit(solution)/shard_map/ppermute | solution.py:588
  16.6 12.2 %collective-permute-start.3 = (f32[320,128]{1,0:T(8,128)S(1)}, f32[320,128]{1,0:T(8,128)S(1)}, u32[]{:S(2)}, u32[]{:S(2)}) collective-permute-start(f32[320,128]{1,0:T(8,128)S(1)} %get-tuple-element.28), channel_id=1, source_target_pairs={{4,8},{8,4},{12,16},{16,12},{20,24},{24,20},{5,9},{9,5},{13,17},{1... | collective-permute-start | bytes 491528 | tf_op jit(solution)/shard_map/ppermute | solution.py:588

commit v4 on v3

--- a/solution.py
+++ b/solution.py
@@ -1,5 +1,3 @@
-import functools
-
 import jax
 import jax.numpy as jnp
 from jax import lax
@@ -46,7 +44,7 @@
 
 
 def flux_rows(refs, r, tiles):
-    S, E, N, Q, W = refs
+    S, E, N, Q, _ = refs
     ds = east_minus_west([rows_at(S, c, r) for c in range(tiles)])
     for c in range(tiles):
         q = rows_at(Q, c, r)
@@ -55,7 +53,7 @@
 
 
 def surface_rows(refs, r, tiles, first):
-    S, E, N, Q, W = refs
+    S, E, N, _, W = refs
     de = east_minus_west([rows_at(E, c, r) for c in range(tiles)])
     for c in range(tiles):
         hw = rows_at(W, c, r)
@@ -164,7 +162,7 @@
 
 
 def pack_first(s, e, n, d, m):
-    rows, cols = s.shape
+    _, cols = s.shape
     return pl.pallas_call(
         pack_first_kernel,
         out_shape=[jax.ShapeDtypeStruct((4 * HALO, cols), F32), jax.ShapeDtypeStruct((2 * HALO, LANES), F32)],
@@ -356,7 +354,7 @@
             wait_all(loads[k + 1])
         over_chunk(k, first_flux)
     loop_rows(rows // SUB, lambda r: surface_rows(refs, r, tiles, True))
-    for step in range(1, STEPS):
+    for _ in range(1, STEPS):
         loop_rows(rows // SUB, lambda r: flux_rows(refs, r, tiles))
         loop_rows(rows // SUB, lambda r: surface_rows(refs, r, tiles, False))
     points = rows // SPACING

time: 31.6 us -> 31.6 us (level)
  no operation moved by 1% of the time
where the time goes in v4:
time: 31.6 us; the launch traced here: 31.4 us
  Pallas kernels  13.4 us (42%)
  starting transfers between devices  10.6 us (34%)
  waiting for transfers between devices  5.28 us (17%)
  local copies, waits for them, and re-layouts  1.29 us (4%)
  between operations  0.77 us (2%)
    ppermute x5, starting transfers between devices, swap(): return lax.ppermute(array, axis, pairs)  10.6 us
    ppermute x5, waiting for transfers between devices, swap(): return lax.ppermute(array, axis, pairs)  5.28 us
    pallas_call x1, Pallas kernels, interior(): pl.pallas_call(interior_kernel, out_shape=[jax.ShapeDtypeStruct(field, F3...  4.95 us
    pallas_call x1, Pallas kernels, strips(): pl.pallas_call(strip_kernel, out_shape=[field] * 3 + [jax.ShapeDtypeStruc...  2.8 us
    pallas_call x1, Pallas kernels, columns(): pl.pallas_call(column_kernel, out_shape=[field] * 3 + [jax.ShapeDtypeStru...  2.58 us
    pallas_call x1, Pallas kernels, pack_first(): pl.pallas_call(pack_first_kernel, out_shape=[jax.ShapeDtypeStruct((4 * HA...  1.43 us
    unnamed x10, local copies, waits for them, and re-layouts  1.29 us
    pallas_call x1, Pallas kernels, edges(): pl.pallas_call(edge_kernel, out_shape=[jax.ShapeDtypeStruct((4 * HALO, co...  1.18 us
  transfers between devices with their start and end apart: 5, of which 1 were waited for; matrix products, arithmetic and copies ran while one was open for 0% of the time, Pallas kernels for 30%

profile of v4, /device:TPU:6, one launch (start us, length us, event | category | flops | bytes accessed | tf_op | source)
XLA Modules:
  0.0 31.4 jit_solution(16269505430648193052)
XLA Ops:
  0.6 0.0 copy-start.4
  0.6 0.0 copy-start.3
  0.7 0.0 copy-start.2
  0.7 0.0 copy-start.1
  0.7 0.0 copy-start
  0.7 1.4 %pack_first.1 = (f32[128,1024]{1,0:T(8,128)S(1)}, f32[64,128]{1,0:T(8,128)S(1)}) custom-call(f32[256,1024]{1,0:T(8,128)} %s.7, f32[256,1024]{1,0:T(8,128)} %e.7, f32[256,1024]{1,0:T(8,128)} %n.7, f32[256,1024]{1,0:T(8,128)} %d.7, s32[256,1024]{1,0:T(8,128)} %m.7), custom_call_target="tpu_custom_call" | custom-call | tf_op jit(solution)/shard_map/pack_first/pallas_call | solution.py:166
  2.1 0.1 collective-permute-start
  2.2 0.0 copy-done.4
  2.2 0.3 %copy-done.3 = f32[256,1024]{1,0:T(8,128)S(1)} copy-done((f32[256,1024]{1,0:T(8,128)S(1)}, f32[256,1024]{1,0:T(8,128)}, u32[]{:S(2)}) %copy-start.3) | copy-done | bytes 1048600
  2.5 0.3 %copy-done.2 = f32[256,1024]{1,0:T(8,128)S(1)} copy-done((f32[256,1024]{1,0:T(8,128)S(1)}, f32[256,1024]{1,0:T(8,128)}, u32[]{:S(2)}) %copy-start.2) | copy-done | bytes 1048600
  2.8 0.3 %copy-done.1 = f32[256,1024]{1,0:T(8,128)S(1)} copy-done((f32[256,1024]{1,0:T(8,128)S(1)}, f32[256,1024]{1,0:T(8,128)}, u32[]{:S(2)}) %copy-start.1) | copy-done | bytes 1048600
  3.2 0.3 %copy-done = f32[256,1024]{1,0:T(8,128)S(1)} copy-done((f32[256,1024]{1,0:T(8,128)S(1)}, f32[256,1024]{1,0:T(8,128)}, u32[]{:S(2)}) %copy-start) | copy-done | bytes 1048600
  3.5 1.2 %edges.1 = (f32[128,1024]{1,0:T(8,128)S(1)}, f32[320,128]{1,0:T(8,128)S(1)}, f32[320,128]{1,0:T(8,128)S(1)}, f32[4,320,128]{2,1,0:T(8,128)S(1)}) custom-call(f32[256,1024]{1,0:T(8,128)S(1)} %copy-done, f32[256,1024]{1,0:T(8,128)S(1)} %copy-done.1, f32[256,1024]{1,0:T(8,128)S(1)} %copy-done.2, f32[256,1024]{1,0:T(8,128)S(1)} %copy-done.3, ...), custom_call_target="tpu_custom_call" | custom-call | tf_op jit(solution)/shard_map/edges/pallas_call | solution.py:237
  4.7 1.9 %collective-permute-start.4 = (f32[128,1024]{1,0:T(8,128)S(1)}, f32[128,1024]{1,0:T(8,128)S(1)}, u32[]{:S(2)}, u32[]{:S(2)}) collective-permute-start(f32[128,1024]{1,0:T(8,128)S(1)} %get-tuple-element.30), channel_id=1, source_target_pairs={{1,2},{2,1},{5,6},{6,5},{9,10},{10,9},{13,14},{14,13},{17,18},{18,... | collective-permute-start | bytes 1572872 | tf_op jit(solution)/shard_map/ppermute | solution.py:586
  6.6 3.6 %collective-permute-start.1 = (f32[64,128]{1,0:T(8,128)S(1)}, f32[64,128]{1,0:T(8,128)S(1)}, u32[]{:S(2)}, u32[]{:S(2)}) collective-permute-start(f32[64,128]{1,0:T(8,128)S(1)} %get-tuple-element.23), channel_id=1, source_target_pairs={{1,2},{2,1},{5,6},{6,5},{9,10},{10,9},{13,14},{14,13},{17,18},{18,... | collective-permute-start | bytes 98312 | tf_op jit(solution)/shard_map/ppermute | solution.py:586
  10.2 5.3 %collective-permute-done.1.rbc = f32[64,128]{1,0:T(8,128)S(1)} collective-permute-done((f32[64,128]{1,0:T(8,128)S(1)}, f32[64,128]{1,0:T(8,128)S(1)}, u32[]{:S(2)}, u32[]{:S(2)}) %collective-permute-start.1) | collective-permute-done | bytes 32800 | tf_op jit(solution)/shard_map/ppermute | solution.py:586
  15.5 0.0 collective-permute-done.ra
  15.5 0.5 %corners.1 = (f32[320,128]{1,0:T(8,128)S(1)}, f32[320,128]{1,0:T(8,128)S(1)}, f32[4,320,128]{2,1,0:T(8,128)S(1)}) custom-call(f32[128,1024]{1,0:T(8,128)S(1)} %collective-permute-done.ra, f32[64,128]{1,0:T(8,128)S(1)} %collective-permute-done.1.rbc, ...), custom_call_target="tpu_custom_call", output_to_operand_aliasing={{0}: (2, {}), {1}: (3, {}), {2}: (4, {})} | custom-call | tf_op jit(solution)/shard_map/corners/pallas_call | solution.py:297
  16.0 0.6 %collective-permute-start.2 = (f32[320,128]{1,0:T(8,128)S(1)}, f32[320,128]{1,0:T(8,128)S(1)}, u32[]{:S(2)}, u32[]{:S(2)}) collective-permute-start(f32[320,128]{1,0:T(8,128)S(1)} %get-tuple-element.27), channel_id=1, source_target_pairs={{0,4},{4,0},{8,12},{12,8},{16,20},{20,16},{24,28},{28,24},{1,5},{5... | collective-permute-start | bytes 491528 | tf_op jit(solution)/shard_map/ppermute | solution.py:586
  16.6 4.4 %collective-permute-start.3 = (f32[320,128]{1,0:T(8,128)S(1)}, f32[320,128]{1,0:T(8,128)S(1)}, u32[]{:S(2)}, u32[]{:S(2)}) collective-permute-start(f32[320,128]{1,0:T(8,128)S(1)} %get-tuple-element.28), channel_id=1, source_target_pairs={{4,8},{8,4},{12,16},{16,12},{20,24},{24,20},{5,9},{9,5},{13,17},{1... | collective-permute-start | bytes 491528 | tf_op jit(solution)/shard_map/ppermute | solution.py:586
  21.0 4.9 %interior.1 = (f32[8,272,128]{2,1,0:T(8,128)S(1)}, f32[8,272,128]{2,1,0:T(8,128)S(1)}, f32[8,272,128]{2,1,0:T(8,128)S(1)}, f32[16,1024]{1,0:T(8,128)S(1)}) custom-call(f32[256,1024]{1,0:T(8,128)S(1)} %copy-done, f32[256,1024]{1,0:T(8,128)S(1)} %copy-done.1, f32[256,1024]{1,0:T(8,128)S(1)} %copy-done.2, f32[256,1024]{1,0:T(8,128)S(1)} %copy-done.3, ...), custom_call_target="tpu_custom_call" | custom-call | flops 10485760 | bytes 8388608 | tf_op jit(solution)/shard_map/interior/pallas_call | solution.py:372
  26.0 0.0 collective-permute-done.4.rb
  26.0 2.8 %strips.1 = (f32[256,1024]{1,0:T(8,128)}, f32[256,1024]{1,0:T(8,128)}, f32[256,1024]{1,0:T(8,128)}, f32[16,128]{1,0:T(8,128)S(1)}, f32[3,2,2,8,128]{4,3,2,1,0:T(8,128)S(1)}) custom-call(f32[256,1024]{1,0:T(8,128)S(1)} %copy-done, f32[256,1024]{1,0:T(8,128)S(1)} %copy-done.1, f32[256,1024]{1,0:T(8,128)S(1)} %copy-done.2, f32[256,1024]{1,0:T(8,128)S(1)} %copy-done.3, ...), custom_call_target="tpu_custom_call" | custom-call | flops 5242880 | bytes 4194304 | tf_op jit(solution)/shard_map/strips/pallas_call | solution.py:469
  28.8 0.0 collective-permute-done.2.rc
  28.8 0.0 collective-permute-done.3.rd
  28.8 2.6 %columns.1 = (f32[256,1024]{1,0:T(8,128)}, f32[256,1024]{1,0:T(8,128)}, f32[256,1024]{1,0:T(8,128)}, f32[16,64]{1,0:T(8,128)}) custom-call(f32[320,128]{1,0:T(8,128)S(1)} %collective-permute-done.2.rc, f32[320,128]{1,0:T(8,128)S(1)} %collective-permute-done.3.rd, ...), custom_call_target="tpu_custom_call", output_to_operand_aliasing={{0}: (9, {}), {1}: (10, {}), {2}: (11, {})} | custom-call | tf_op jit(solution)/shard_map/columns/pallas_call | solution.py:561
Async XLA Ops:
  0.6 1.6 %copy-start.4 = (s32[256,1024]{1,0:T(8,128)S(1)}, s32[256,1024]{1,0:T(8,128)}, u32[]{:S(2)}) copy-start(s32[256,1024]{1,0:T(8,128)} %m.7) | copy-start | bytes 3145732
  0.6 1.9 %copy-start.3 = (f32[256,1024]{1,0:T(8,128)S(1)}, f32[256,1024]{1,0:T(8,128)}, u32[]{:S(2)}) copy-start(f32[256,1024]{1,0:T(8,128)} %d.7) | copy-start | bytes 3145732
  0.7 2.2 %copy-start.2 = (f32[256,1024]{1,0:T(8,128)S(1)}, f32[256,1024]{1,0:T(8,128)}, u32[]{:S(2)}) copy-start(f32[256,1024]{1,0:T(8,128)} %n.7) | copy-start | bytes 3145732
  0.7 2.5 %copy-start.1 = (f32[256,1024]{1,0:T(8,128)S(1)}, f32[256,1024]{1,0:T(8,128)}, u32[]{:S(2)}) copy-start(f32[256,1024]{1,0:T(8,128)} %e.7) | copy-start | bytes 3145732
  0.7 2.8 %copy-start = (f32[256,1024]{1,0:T(8,128)S(1)}, f32[256,1024]{1,0:T(8,128)}, u32[]{:S(2)}) copy-start(f32[256,1024]{1,0:T(8,128)} %s.7) | copy-start | bytes 3145732
  2.1 13.4 %collective-permute-start = (f32[128,1024]{1,0:T(8,128)S(1)}, f32[128,1024]{1,0:T(8,128)S(1)}, u32[]{:S(2)}, u32[]{:S(2)}) collective-permute-start(f32[128,1024]{1,0:T(8,128)S(1)} %get-tuple-element.22), channel_id=1, source_target_pairs={{0,1},{1,0},{2,3},{3,2},{4,5},{5,4},{6,7},{7,6},{8,9},{9,8},{10,11... | collective-permute-start | bytes 1572872 | tf_op jit(solution)/shard_map/ppermute | solution.py:586
  4.7 21.3 %collective-permute-start.4 = (f32[128,1024]{1,0:T(8,128)S(1)}, f32[128,1024]{1,0:T(8,128)S(1)}, u32[]{:S(2)}, u32[]{:S(2)}) collective-permute-start(f32[128,1024]{1,0:T(8,128)S(1)} %get-tuple-element.30), channel_id=1, source_target_pairs={{1,2},{2,1},{5,6},{6,5},{9,10},{10,9},{13,14},{14,13},{17,18},{18,... | collective-permute-start | bytes 1572872 | tf_op jit(solution)/shard_map/ppermute | solution.py:586
  6.6 8.9 %collective-permute-start.1 = (f32[64,128]{1,0:T(8,128)S(1)}, f32[64,128]{1,0:T(8,128)S(1)}, u32[]{:S(2)}, u32[]{:S(2)}) collective-permute-start(f32[64,128]{1,0:T(8,128)S(1)} %get-tuple-element.23), channel_id=1, source_target_pairs={{1,2},{2,1},{5,6},{6,5},{9,10},{10,9},{13,14},{14,13},{17,18},{18,... | collective-permute-start | bytes 98312 | tf_op jit(solution)/shard_map/ppermute | solution.py:586
  16.0 12.8 %collective-permute-start.2 = (f32[320,128]{1,0:T(8,128)S(1)}, f32[320,128]{1,0:T(8,128)S(1)}, u32[]{:S(2)}, u32[]{:S(2)}) collective-permute-start(f32[320,128]{1,0:T(8,128)S(1)} %get-tuple-element.27), channel_id=1, source_target_pairs={{0,4},{4,0},{8,12},{12,8},{16,20},{20,16},{24,28},{28,24},{1,5},{5... | collective-permute-start | bytes 491528 | tf_op jit(solution)/shard_map/ppermute | solution.py:586
  16.6 12.2 %collective-permute-start.3 = (f32[320,128]{1,0:T(8,128)S(1)}, f32[320,128]{1,0:T(8,128)S(1)}, u32[]{:S(2)}, u32[]{:S(2)}) collective-permute-start(f32[320,128]{1,0:T(8,128)S(1)} %get-tuple-element.28), channel_id=1, source_target_pairs={{4,8},{8,4},{12,16},{16,12},{20,24},{24,20},{5,9},{9,5},{13,17},{1... | collective-permute-start | bytes 491528 | tf_op jit(solution)/shard_map/ppermute | solution.py:586

commit v5 on v4

--- a/solution.py
+++ b/solution.py
@@ -1,3 +1,5 @@
+import functools
+
 import jax
 import jax.numpy as jnp
 from jax import lax
@@ -92,7 +94,10 @@
 
 
 def dot(a, b):
-    return jnp.dot(a, b, precision=lax.Precision.HIGHEST, preferred_element_type=F32)
+    ah, bh = a.astype(jnp.bfloat16), b.astype(jnp.bfloat16)
+    al, bl = (a - ah.astype(F32)).astype(jnp.bfloat16), (b - bh.astype(F32)).astype(jnp.bfloat16)
+    product = functools.partial(jnp.dot, preferred_element_type=F32)
+    return product(ah, bh) + (product(ah, bl) + product(al, bh))
 
 
 def zero_borders(refs, rows, tiles):
@@ -199,10 +204,9 @@
     return pc, pd
 
 
-def edge_kernel(s, e, n, d, m, pb, pc, pd, own, PC, PD, OWN, sem):
+def edge_kernel(s, e, n, d, m, pb, own):
     rows, cols = s.shape
-    lat_even, lon_even = is_even("lat"), is_even("lon")
-    far = pl.multiple_of(jnp.where(lat_even, 0, rows - HALO), SUB)
+    far = pl.multiple_of(jnp.where(is_even("lat"), 0, rows - HALO), SUB)
     for r in range(0, HALO, SUB):
         at = pl.ds(far + r, SUB)
         wet = m[at, :].astype(F32)
@@ -215,56 +219,32 @@
         for col in (0, cols - LANES):
             to = slice(col, col + LANES)
             ends.append(masked(s[at, to], e[at, to], n[at, to], d[at, to], m[at, to].astype(F32)))
-        mine = [own_columns(a, b) for a, b in zip(*ends)]
-        for f in range(4):
-            OWN[f, at, :] = mine[f]
-        PC[at, :], PD[at, :] = pack_columns(mine, lon_even)
+        for f, (a, b) in enumerate(zip(*ends)):
+            own[f, at, :] = own_columns(a, b)
 
     loop_rows(rows // SUB, pack, 8)
-    sends = [
-        pltpu.make_async_copy(PC, pc.at[HALO : HALO + rows], sem.at[0]),
-        pltpu.make_async_copy(PD, pd.at[HALO : HALO + rows], sem.at[1]),
-        pltpu.make_async_copy(OWN, own.at[:, HALO : HALO + rows], sem.at[2]),
-    ]
-    for copy in sends:
-        copy.start()
-    wait_all(sends)
 
 
 def edges(s, e, n, d, m):
     rows, cols = s.shape
-    wide = jax.ShapeDtypeStruct((rows + 2 * HALO, LANES), F32)
     return pl.pallas_call(
         edge_kernel,
         out_shape=[
             jax.ShapeDtypeStruct((4 * HALO, cols), F32),
-            wide,
-            wide,
-            jax.ShapeDtypeStruct((4, rows + 2 * HALO, LANES), F32),
+            jax.ShapeDtypeStruct((4, rows, LANES), F32),
         ],
         in_specs=[VMEM] * 5,
-        out_specs=[VMEM] + [ANY] * 3,
-        scratch_shapes=[
-            pltpu.VMEM((rows, LANES), F32),
-            pltpu.VMEM((rows, LANES), F32),
-            pltpu.VMEM((4, rows, LANES), F32),
-            pltpu.SemaphoreType.DMA((3,)),
-        ],
+        out_specs=[VMEM] * 2,
         compiler_params=PARAMS,
         name="edges",
     )(s, e, n, d, m)
 
 
-def corner_kernel(ra, rbc, pc_in, pd_in, own_in, pc, pd, own, PC, PD, OWN, sem):
-    del pc_in, pd_in, own_in
-    height = pc.shape[0]
-    cols = ra.shape[1]
+def corner_kernel(ra, rbc, own, pc, pd, ends):
+    rows, cols = own.shape[1], ra.shape[1]
     even, lon_even = is_even("lat"), is_even("lon")
-    top = height - HALO
-    starts = (jnp.where(even, top, 0), jnp.where(even, 0, top))
-    sends = []
     lane = lane_index()
-    for side, row in enumerate(starts):
+    for side, above in enumerate((jnp.where(even, 1, 0), jnp.where(even, 0, 1))):
         for r in range(0, HALO, SUB):
             if side == 0:
                 mine = [
@@ -281,34 +261,29 @@
                     for tile in (pair, pltpu.roll(pair, LANES // 2, 1)):
                         mine.append(jnp.where(lane < 2 * HALO, tile, 0.0))
             for f in range(4):
-                OWN[side, f, r : r + SUB, :] = mine[f]
-            PC[side, r : r + SUB, :], PD[side, r : r + SUB, :] = pack_columns(mine, lon_even)
-        at = pl.ds(pl.multiple_of(row, SUB), HALO)
-        for f, (src, dst) in enumerate(
-            ((PC.at[side], pc.at[at, :]), (PD.at[side], pd.at[at, :]), (OWN.at[side], own.at[:, at, :]))
-        ):
-            copy = pltpu.make_async_copy(src, dst, sem.at[side, f])
-            copy.start()
-            sends.append(copy)
-    wait_all(sends)
-
-
-def corners(ra, rbc, pc, pd, own):
+                ends[above, f, r : r + SUB, :] = mine[f]
+            at = pl.ds(pl.multiple_of(above * (rows + HALO) + r, SUB), SUB)
+            pc[at, :], pd[at, :] = pack_columns(mine, lon_even)
+
+    def pack(r):
+        at = pl.ds(r - SUB + HALO, SUB)
+        mine = [own[f, pl.ds(r - SUB, SUB), :] for f in range(4)]
+        pc[at, :], pd[at, :] = pack_columns(mine, lon_even)
+
+    loop_rows(rows // SUB, pack, 8)
+
+
+def corners(ra, rbc, own):
+    rows = own.shape[1]
+    wide = jax.ShapeDtypeStruct((rows + 2 * HALO, LANES), F32)
     return pl.pallas_call(
         corner_kernel,
-        out_shape=[jax.ShapeDtypeStruct(x.shape, F32) for x in (pc, pd, own)],
-        in_specs=[VMEM] * 2 + [ANY] * 3,
-        out_specs=[ANY] * 3,
-        scratch_shapes=[
-            pltpu.VMEM((2, HALO, LANES), F32),
-            pltpu.VMEM((2, HALO, LANES), F32),
-            pltpu.VMEM((2, 4, HALO, LANES), F32),
-            pltpu.SemaphoreType.DMA((2, 3)),
-        ],
-        input_output_aliases={2: 0, 3: 1, 4: 2},
+        out_shape=[wide, wide, jax.ShapeDtypeStruct((2, 4, HALO, LANES), F32)],
+        in_specs=[VMEM] * 3,
+        out_specs=[VMEM] * 3,
         compiler_params=PARAMS,
         name="corners",
-    )(ra, rbc, pc, pd, own)
+    )(ra, rbc, own)
 
 
 def interior_kernel(s, e, n, d, m, S, E, N, u, Q, W, isem):
@@ -381,7 +356,12 @@
     )(s, e, n, d, m)
 
 
-def strip_kernel(s, e, n, d, m, ra, rb, u, si, ei, ni, so, eo, no, v, x, S, E, N, Q, W, osem):
+def border_kernel(
+    s, e, n, d, m, ra, rb, u, si, ei, ni, rc, rd, own, ends, active, so, eo, no, grad,
+    S, E, N, Q, W, S1, E1, N1, Q1, W1, X, A, sem, osem,
+):
+    fetch = pltpu.make_async_copy(active, A, sem.at[0])
+    fetch.start()
     rows, cols = s.shape
     tiles = cols // LANES
     refs = (S, E, N, Q, W)
@@ -421,11 +401,10 @@
     for step in range(STEPS):
         loop_rows(count // SUB, lambda r: flux_rows(refs, r, tiles), 12)
         loop_rows(count // SUB, lambda r: surface_rows(refs, r, tiles, step == 0), 12)
-    for f, (src, dst) in enumerate(((S, so), (E, eo), (N, no))):
-        for side, (frm, to) in enumerate(((SUB + HALO, 0), (SUB + STRIP + keep - SUB, rows - SUB))):
+    for src, dst in ((S, so), (E, eo), (N, no)):
+        for frm, to in ((SUB + HALO, 0), (SUB + STRIP + keep - SUB, rows - SUB)):
             for c in range(tiles):
                 if c in (0, tiles - 1):
-                    x[f, min(c, 1), side] = src[c, frm : frm + SUB, :]
                     continue
                 copy = pltpu.make_async_copy(
                     src.at[c, frm : frm + SUB, :],
@@ -458,79 +437,52 @@
     for c in range(tiles):
         piece = jnp.where(lane < reach, product[c * points : (c + 1) * points], 0.0)
         total = total + pltpu.roll(piece, (c * (LANES // SPACING) - 2) % LANES, 1)
-    v[...] = total
-    wait_all(sends)
-
-
-def strips(s, e, n, d, m, ra, rb, u, si, ei, ni):
-    rows, cols = s.shape
-    tiles = cols // LANES
-    field = jax.ShapeDtypeStruct((rows, cols), F32)
-    return pl.pallas_call(
-        strip_kernel,
-        out_shape=[field] * 3
-        + [
-            jax.ShapeDtypeStruct((rows // SPACING, LANES), F32),
-            jax.ShapeDtypeStruct((3, 2, 2, SUB, LANES), F32),
-        ],
-        in_specs=[VMEM] * 8 + [ANY] * 3,
-        out_specs=[ANY] * 3 + [VMEM] * 2,
-        scratch_shapes=[pltpu.VMEM((tiles, 2 * STRIP + 2 * SUB, LANES), F32)] * 5
-        + [pltpu.SemaphoreType.DMA((1,))],
-        cost_estimate=pl.CostEstimate(flops=20 * rows * cols, bytes_accessed=16 * rows * cols, transcendentals=0),
-        compiler_params=PARAMS,
-        name="strips",
-    )(s, e, n, d, m, ra, rb, u, si, ei, ni)
-
-
-def column_kernel(
-    rc, rd, own, v, si, ei, ni, xs, active, so_in, eo_in, no_in, so, eo, no, grad, S, E, N, Q, W, X, A, sem, osem
-):
-    del so_in, eo_in, no_in
-    rows, cols = so.shape
+
     height = rows + 2 * HALO
-    refs = (S, E, N, Q, W)
+    refs = column = (S1, E1, N1, Q1, W1)
     even = is_even("lon")
-    fetch = pltpu.make_async_copy(active, A, sem.at[0])
-    fetch.start()
-    zero_borders((S, N), height, 1)
+    zero_borders((S1, N1), height, 1)
     group = lax.div(lane_index(), HALO)
 
     def unpack(r):
         at = pl.ds(r - SUB, SUB)
         c, d = rc[at, :], rd[at, :]
         right, left = jnp.where(even, c, d), jnp.where(even, d, c)
-        for f, dst in enumerate((S, E, N, Q)):
+        for f, dst in enumerate((S1, E1, N1, Q1)):
             a, b = right, left
             if f:
                 a, b = pltpu.roll(a, LANES - f * HALO, 1), pltpu.roll(b, LANES - f * HALO, 1)
-            tile = jnp.where(group == 2, a, jnp.where(group == 3, b, own[f, at, :]))
+            t = r - SUB
+            if t < HALO:
+                middle = ends[0, f, t : t + SUB, :]
+            elif t < HALO + rows:
+                middle = own[f, t - HALO : t - HALO + SUB, :]
+            else:
+                middle = ends[1, f, t - HALO - rows : t - HALO - rows + SUB, :]
+            tile = jnp.where(group == 2, a, jnp.where(group == 3, b, middle))
             dst[0, pl.ds(r, SUB), :] = tile
             if f == 3:
-                W[0, pl.ds(r, SUB), :] = jnp.where(tile > 0.0, COURANT, 0.0)
-
-    loop_rows(height // SUB, unpack, 40)
+                W1[0, pl.ds(r, SUB), :] = jnp.where(tile > 0.0, COURANT, 0.0)
+
+    loop_rows(height // SUB, unpack, height)
     lane = lane_index()
-    sends = []
 
     def merge(fields):
         def body(r, i=None):
             at = pl.ds(r - SUB, SUB)
             for f in fields:
-                tile = (S, E, N)[f][0, pl.ds(r + HALO, SUB), :]
-                xi, tiles = (si, ei, ni)[f], cols // LANES
-                first, last = (
-                    xi[end * (tiles - 1), pl.ds(r, SUB), :] if i is None else xs[f, end, i] for end in range(2)
-                )
+                tile = column[f][0, pl.ds(r + HALO, SUB), :]
+                src, row = ((si, ei, ni)[f], r) if i is None else ((S, E, N)[f], i)
+                first, last = (src[end * (tiles - 1), pl.ds(row, SUB), :] for end in range(2))
                 X[f, 0, at, :] = jnp.where(lane < EDGE, tile, first)
                 X[f, 1, at, :] = jnp.where(lane >= LANES - EDGE, pltpu.roll(tile, LANES // 2, 1), last)
 
         loop_rows(rows // SUB, body, 32)
-        body(SUB, 0)
-        body(rows, 1)
+        body(SUB, SUB + HALO)
+        body(rows, SUB + STRIP + keep - SUB)
         for f in fields:
             for end, col in enumerate((0, cols - LANES)):
-                copy = pltpu.make_async_copy(X.at[f, end], (so, eo, no)[f].at[:, col : col + LANES], osem.at[f, end])
+                copy = pltpu.make_async_copy(X.at[f, end], (so, eo, no)[f].at[:, col : col + LANES], osem.at[0])
                 copy.start()
                 sends.append(copy)
 
@@ -543,37 +495,38 @@
     points, across = grad.shape
     cell = lax.broadcasted_iota(jnp.int32, (points, height), 1) - HALO
     table = spline_of(cell, lax.broadcasted_iota(jnp.int32, (points, height), 0))
-    part = dot(table, S[0, SUB : SUB + height, :])
+    part = dot(table, S1[0, SUB : SUB + height, :])
     index = lax.broadcasted_iota(jnp.int32, (LANES, across), 0)
     col = jnp.where(index < HALO, index, jnp.where(index < 3 * HALO, index + (cols - 2 * HALO), index - LANES))
     weights = spline_of(col, lax.broadcasted_iota(jnp.int32, (LANES, across), 1))
     weights = jnp.where((col < EDGE) | (col >= cols - EDGE), weights, 0.0)
-    sums = v[:, 0:across] + dot(part, weights)
+    sums = total[:, 0:across] + dot(part, weights)
     fetch.wait()
     grad[...] = sums * A[...].astype(F32) / SPACING
     wait_all(sends)
 
 
-def columns(rc, rd, own, v, si, ei, ni, xs, active, so, eo, no):
-    rows, cols = so.shape
-    height = rows + 2 * HALO
+def borders(s, e, n, d, m, ra, rb, u, si, ei, ni, rc, rd, own, ends, active):
+    rows, cols = s.shape
+    tiles = cols // LANES
     field = jax.ShapeDtypeStruct((rows, cols), F32)
     return pl.pallas_call(
-        column_kernel,
+        border_kernel,
         out_shape=[field] * 3 + [jax.ShapeDtypeStruct(active.shape, F32)],
-        in_specs=[VMEM] * 8 + [ANY] * 4,
+        in_specs=[VMEM] * 15 + [ANY],
         out_specs=[ANY] * 3 + [VMEM],
-        scratch_shapes=[pltpu.VMEM((1, height + 2 * SUB, LANES), F32)] * 5
+        scratch_shapes=[pltpu.VMEM((tiles, 2 * STRIP + 2 * SUB, LANES), F32)] * 5
+        + [pltpu.VMEM((1, rows + 2 * HALO + 2 * SUB, LANES), F32)] * 5
         + [
             pltpu.VMEM((3, 2, rows, LANES), F32),
             pltpu.VMEM(active.shape, jnp.int32),
             pltpu.SemaphoreType.DMA((1,)),
-            pltpu.SemaphoreType.DMA((3, 2)),
+            pltpu.SemaphoreType.DMA((1,)),
         ],
-        input_output_aliases={9: 0, 10: 1, 11: 2},
+        cost_estimate=pl.CostEstimate(flops=20 * rows * cols, bytes_accessed=16 * rows * cols, transcendentals=0),
         compiler_params=PARAMS,
-        name="columns",
-    )(rc, rd, own, v, si, ei, ni, xs, in_hbm(active), so, eo, no)
+        name="borders",
+    )(s, e, n, d, m, ra, rb, u, si, ei, ni, rc, rd, own, ends, in_hbm(active))
 
 
 def swap(array, axis, offset):
@@ -591,14 +544,13 @@
     pa, pbc = pack_first(*fields)
     ra = swap(pa, "lat", 0)
     rbc = swap(pbc, "lat", 1)
-    pb, pc, pd, own = edges(*fields)
+    pb, own = edges(*fields)
     rb = swap(pb, "lat", 1)
-    pc, pd, own = corners(ra, rbc, pc, pd, own)
+    pc, pd, ends = corners(ra, rbc, own)
     rc = swap(pc, "lon", 0)
     rd = swap(pd, "lon", 1)
     si, ei, ni, u = interior(*fields)
-    so, eo, no, v, xs = strips(*fields, ra, rb, u, si, ei, ni)
-    return columns(rc, rd, own, v, si, ei, ni, xs, control_active, so, eo, no)
+    return borders(*fields, ra, rb, u, si, ei, ni, rc, rd, own, ends, control_active)
 
 
 def solution(mesh):

time: 31.6 us -> 30 us (0.949)
  the two profiles are of different devices: /device:TPU:6 before, /device:TPU:10 now
where the time goes in v5:
time: 30 us; the launch traced here: 29.8 us
  Pallas kernels  11.5 us (38%)
  starting transfers between devices  9.51 us (32%)
  waiting for transfers between devices  6.8 us (23%)
  local copies, waits for them, and re-layouts  1.29 us (4%)
  between operations  0.76 us (3%)
    ppermute x5, starting transfers between devices, swap(): return lax.ppermute(array, axis, pairs)  9.51 us
    ppermute x5, waiting for transfers between devices, swap(): return lax.ppermute(array, axis, pairs)  6.8 us
    pallas_call x1, Pallas kernels, borders(): pl.pallas_call(border_kernel, out_shape=[field] * 3 + [jax.ShapeDtypeStru...  4.8 us
    pallas_call x1, Pallas kernels, interior(): pl.pallas_call(interior_kernel, out_shape=[jax.ShapeDtypeStruct(field, F3...  4.26 us
    pallas_call x1, Pallas kernels, pack_first(): pl.pallas_call(pack_first_kernel, out_shape=[jax.ShapeDtypeStruct((4 * HA...  1.43 us
    unnamed x10, local copies, waits for them, and re-layouts  1.29 us
  transfers between devices with their start and end apart: 5, of which 2 were waited for; matrix products, arithmetic and copies ran while one was open for 0% of the time, Pallas kernels for 18%

profile of v5, /device:TPU:10, one launch (start us, length us, event | category | flops | bytes accessed | tf_op | source)
XLA Modules:
  0.0 29.8 jit_solution(13932742943144361787)
XLA Ops:
  0.6 0.0 copy-start.4
  0.6 0.0 copy-start.3
  0.7 0.0 copy-start.2
  0.7 0.0 copy-start.1
  0.7 0.0 copy-start
  0.7 1.4 %pack_first.1 = (f32[128,1024]{1,0:T(8,128)S(1)}, f32[64,128]{1,0:T(8,128)S(1)}) custom-call(f32[256,1024]{1,0:T(8,128)} %s.7, f32[256,1024]{1,0:T(8,128)} %e.7, f32[256,1024]{1,0:T(8,128)} %n.7, f32[256,1024]{1,0:T(8,128)} %d.7, s32[256,1024]{1,0:T(8,128)} %m.7), custom_call_target="tpu_custom_call" | custom-call | tf_op jit(solution)/shard_map/pack_first/pallas_call | solution.py:171
  2.1 0.1 collective-permute-start
  2.2 0.0 copy-done.4
  2.2 0.3 %copy-done.3 = f32[256,1024]{1,0:T(8,128)S(1)} copy-done((f32[256,1024]{1,0:T(8,128)S(1)}, f32[256,1024]{1,0:T(8,128)}, u32[]{:S(2)}) %copy-start.3) | copy-done | bytes 1048600
  2.5 0.3 %copy-done.2 = f32[256,1024]{1,0:T(8,128)S(1)} copy-done((f32[256,1024]{1,0:T(8,128)S(1)}, f32[256,1024]{1,0:T(8,128)}, u32[]{:S(2)}) %copy-start.2) | copy-done | bytes 1048600
  2.8 0.3 %copy-done.1 = f32[256,1024]{1,0:T(8,128)S(1)} copy-done((f32[256,1024]{1,0:T(8,128)S(1)}, f32[256,1024]{1,0:T(8,128)}, u32[]{:S(2)}) %copy-start.1) | copy-done | bytes 1048600
  3.2 0.3 %copy-done = f32[256,1024]{1,0:T(8,128)S(1)} copy-done((f32[256,1024]{1,0:T(8,128)S(1)}, f32[256,1024]{1,0:T(8,128)}, u32[]{:S(2)}) %copy-start) | copy-done | bytes 1048600
  3.5 0.5 %edges.1 = (f32[128,1024]{1,0:T(8,128)S(1)}, f32[4,256,128]{2,1,0:T(8,128)S(1)}) custom-call(f32[256,1024]{1,0:T(8,128)S(1)} %copy-done, f32[256,1024]{1,0:T(8,128)S(1)} %copy-done.1, f32[256,1024]{1,0:T(8,128)S(1)} %copy-done.2, f32[256,1024]{1,0:T(8,128)S(1)} %copy-done.3, s32[256,1024]{1,0:T(8,128)S(1)} %copy-done.4), custom_call_target="tpu_custom_call" | custom-call | tf_op jit(solution)/shard_map/edges/pallas_call | solution.py:230
  3.9 1.9 %collective-permute-start.1 = (f32[128,1024]{1,0:T(8,128)S(1)}, f32[128,1024]{1,0:T(8,128)S(1)}, u32[]{:S(2)}, u32[]{:S(2)}) collective-permute-start(f32[128,1024]{1,0:T(8,128)S(1)} %get-tuple-element.16), channel_id=1, source_target_pairs={{1,2},{2,1},{5,6},{6,5},{9,10},{10,9},{13,14},{14,13},{17,18},{18,... | collective-permute-start | bytes 1572872 | tf_op jit(solution)/shard_map/ppermute | solution.py:539
  5.9 3.6 %collective-permute-start.2 = (f32[64,128]{1,0:T(8,128)S(1)}, f32[64,128]{1,0:T(8,128)S(1)}, u32[]{:S(2)}, u32[]{:S(2)}) collective-permute-start(f32[64,128]{1,0:T(8,128)S(1)} %get-tuple-element.21), channel_id=1, source_target_pairs={{1,2},{2,1},{5,6},{6,5},{9,10},{10,9},{13,14},{14,13},{17,18},{18,... | collective-permute-start | bytes 98312 | tf_op jit(solution)/shard_map/ppermute | solution.py:539
  9.5 5.3 %collective-permute-done.2.rbc = f32[64,128]{1,0:T(8,128)S(1)} collective-permute-done((f32[64,128]{1,0:T(8,128)S(1)}, f32[64,128]{1,0:T(8,128)S(1)}, u32[]{:S(2)}, u32[]{:S(2)}) %collective-permute-start.2) | collective-permute-done | bytes 32800 | tf_op jit(solution)/shard_map/ppermute | solution.py:539
  14.8 0.0 collective-permute-done.ra
  14.8 0.5 %corners.1 = (f32[320,128]{1,0:T(8,128)S(1)}, f32[320,128]{1,0:T(8,128)S(1)}, f32[2,4,32,128]{3,2,1,0:T(8,128)S(1)}) custom-call(f32[128,1024]{1,0:T(8,128)S(1)} %collective-permute-done.ra, f32[64,128]{1,0:T(8,128)S(1)} %collective-permute-done.2.rbc, f32[4,256,128]{2,1,0:T(8,128)S(1)} %get-tuple-element.22.own), custom_call_target="tpu_custom_call" | custom-call | tf_op jit(solution)/shard_map/corners/pallas_call | solution.py:279
  15.3 1.6 %collective-permute-start.3 = (f32[320,128]{1,0:T(8,128)S(1)}, f32[320,128]{1,0:T(8,128)S(1)}, u32[]{:S(2)}, u32[]{:S(2)}) collective-permute-start(f32[320,128]{1,0:T(8,128)S(1)} %get-tuple-element.23), channel_id=1, source_target_pairs={{0,4},{4,0},{8,12},{12,8},{16,20},{20,16},{24,28},{28,24},{1,5},{5... | collective-permute-start | bytes 491528 | tf_op jit(solution)/shard_map/ppermute | solution.py:539
  16.9 2.3 %collective-permute-start.4 = (f32[320,128]{1,0:T(8,128)S(1)}, f32[320,128]{1,0:T(8,128)S(1)}, u32[]{:S(2)}, u32[]{:S(2)}) collective-permute-start(f32[320,128]{1,0:T(8,128)S(1)} %get-tuple-element.24), channel_id=1, source_target_pairs={{4,8},{8,4},{12,16},{16,12},{20,24},{24,20},{5,9},{9,5},{13,17},{1... | collective-permute-start | bytes 491528 | tf_op jit(solution)/shard_map/ppermute | solution.py:539
  19.2 4.3 %interior.1 = (f32[8,272,128]{2,1,0:T(8,128)S(1)}, f32[8,272,128]{2,1,0:T(8,128)S(1)}, f32[8,272,128]{2,1,0:T(8,128)S(1)}, f32[16,1024]{1,0:T(8,128)S(1)}) custom-call(f32[256,1024]{1,0:T(8,128)S(1)} %copy-done, f32[256,1024]{1,0:T(8,128)S(1)} %copy-done.1, f32[256,1024]{1,0:T(8,128)S(1)} %copy-done.2, f32[256,1024]{1,0:T(8,128)S(1)} %copy-done.3, ...), custom_call_target="tpu_custom_call" | custom-call | flops 10485760 | bytes 8388608 | tf_op jit(solution)/shard_map/interior/pallas_call | solution.py:347
  23.5 0.0 collective-permute-done.1.rb
  23.5 0.0 collective-permute-done.3.rc
  23.5 1.5 %collective-permute-done.4.rd = f32[320,128]{1,0:T(8,128)S(1)} collective-permute-done((f32[320,128]{1,0:T(8,128)S(1)}, f32[320,128]{1,0:T(8,128)S(1)}, u32[]{:S(2)}, u32[]{:S(2)}) %collective-permute-start.4) | collective-permute-done | bytes 163872 | tf_op jit(solution)/shard_map/ppermute | solution.py:539
  25.0 4.8 %borders.1 = (f32[256,1024]{1,0:T(8,128)}, f32[256,1024]{1,0:T(8,128)}, f32[256,1024]{1,0:T(8,128)}, f32[16,64]{1,0:T(8,128)}) custom-call(f32[256,1024]{1,0:T(8,128)S(1)} %copy-done, f32[256,1024]{1,0:T(8,128)S(1)} %copy-done.1, f32[256,1024]{1,0:T(8,128)S(1)} %copy-done.2, f32[256,1024]{1,0:T(8,128)S(1)} %copy-done.3, s32[256,1024]{1,0:T(8,128)S(1)} %copy-done.4, ...), custom_call_target="tpu_custom_call" | custom-call | flops 5242880 | bytes 4194304 | tf_op jit(solution)/shard_map/borders/pallas_call | solution.py:513
Async XLA Ops:
  0.6 1.6 %copy-start.4 = (s32[256,1024]{1,0:T(8,128)S(1)}, s32[256,1024]{1,0:T(8,128)}, u32[]{:S(2)}) copy-start(s32[256,1024]{1,0:T(8,128)} %m.7) | copy-start | bytes 3145732
  0.6 1.9 %copy-start.3 = (f32[256,1024]{1,0:T(8,128)S(1)}, f32[256,1024]{1,0:T(8,128)}, u32[]{:S(2)}) copy-start(f32[256,1024]{1,0:T(8,128)} %d.7) | copy-start | bytes 3145732
  0.7 2.2 %copy-start.2 = (f32[256,1024]{1,0:T(8,128)S(1)}, f32[256,1024]{1,0:T(8,128)}, u32[]{:S(2)}) copy-start(f32[256,1024]{1,0:T(8,128)} %n.7) | copy-start | bytes 3145732
  0.7 2.5 %copy-start.1 = (f32[256,1024]{1,0:T(8,128)S(1)}, f32[256,1024]{1,0:T(8,128)}, u32[]{:S(2)}) copy-start(f32[256,1024]{1,0:T(8,128)} %e.7) | copy-start | bytes 3145732
  0.7 2.8 %copy-start = (f32[256,1024]{1,0:T(8,128)S(1)}, f32[256,1024]{1,0:T(8,128)}, u32[]{:S(2)}) copy-start(f32[256,1024]{1,0:T(8,128)} %s.7) | copy-start | bytes 3145732
  2.1 12.7 %collective-permute-start = (f32[128,1024]{1,0:T(8,128)S(1)}, f32[128,1024]{1,0:T(8,128)S(1)}, u32[]{:S(2)}, u32[]{:S(2)}) collective-permute-start(f32[128,1024]{1,0:T(8,128)S(1)} %get-tuple-element.15), channel_id=1, source_target_pairs={{0,1},{1,0},{2,3},{3,2},{4,5},{5,4},{6,7},{7,6},{8,9},{9,8},{10,11... | collective-permute-start | bytes 1572872 | tf_op jit(solution)/shard_map/ppermute | solution.py:539
  3.9 19.6 %collective-permute-start.1 = (f32[128,1024]{1,0:T(8,128)S(1)}, f32[128,1024]{1,0:T(8,128)S(1)}, u32[]{:S(2)}, u32[]{:S(2)}) collective-permute-start(f32[128,1024]{1,0:T(8,128)S(1)} %get-tuple-element.16), channel_id=1, source_target_pairs={{1,2},{2,1},{5,6},{6,5},{9,10},{10,9},{13,14},{14,13},{17,18},{18,... | collective-permute-start | bytes 1572872 | tf_op jit(solution)/shard_map/ppermute | solution.py:539
  5.9 8.9 %collective-permute-start.2 = (f32[64,128]{1,0:T(8,128)S(1)}, f32[64,128]{1,0:T(8,128)S(1)}, u32[]{:S(2)}, u32[]{:S(2)}) collective-permute-start(f32[64,128]{1,0:T(8,128)S(1)} %get-tuple-element.21), channel_id=1, source_target_pairs={{1,2},{2,1},{5,6},{6,5},{9,10},{10,9},{13,14},{14,13},{17,18},{18,... | collective-permute-start | bytes 98312 | tf_op jit(solution)/shard_map/ppermute | solution.py:539
  15.3 8.2 %collective-permute-start.3 = (f32[320,128]{1,0:T(8,128)S(1)}, f32[320,128]{1,0:T(8,128)S(1)}, u32[]{:S(2)}, u32[]{:S(2)}) collective-permute-start(f32[320,128]{1,0:T(8,128)S(1)} %get-tuple-element.23), channel_id=1, source_target_pairs={{0,4},{4,0},{8,12},{12,8},{16,20},{20,16},{24,28},{28,24},{1,5},{5... | collective-permute-start | bytes 491528 | tf_op jit(solution)/shard_map/ppermute | solution.py:539
  16.9 8.1 %collective-permute-start.4 = (f32[320,128]{1,0:T(8,128)S(1)}, f32[320,128]{1,0:T(8,128)S(1)}, u32[]{:S(2)}, u32[]{:S(2)}) collective-permute-start(f32[320,128]{1,0:T(8,128)S(1)} %get-tuple-element.24), channel_id=1, source_target_pairs={{4,8},{8,4},{12,16},{16,12},{20,24},{24,20},{5,9},{9,5},{13,17},{1... | collective-permute-start | bytes 491528 | tf_op jit(solution)/shard_map/ppermute | solution.py:539

commit v6 on v5

--- a/solution.py
+++ b/solution.py
@@ -63,6 +63,42 @@
         if first:
             s = s * (hw + hw)
         S[c, pl.ds(r, SUB), :] = s + hw * (de[c] + (rows_at(N, c, r + 1) - rows_at(N, c, r - 1)))
+
+
+def turned(tiles, by):
+    n, lane = len(tiles), lane_index()
+    moved = [pltpu.roll(t, -by % LANES, 1) for t in tiles]
+    if n == 1:
+        return moved
+    beyond = lane >= LANES - by if by > 0 else lane < -by
+    step = 1 if by > 0 else -1
+    return [jnp.where(beyond, moved[(c + step) % n], moved[c]) for c in range(n)]
+
+
+def ahead_flux_rows(refs, r, tiles):
+    S, E, N, Q, T, _ = refs
+    here = [rows_at(S, c, r) for c in range(tiles)]
+    ahead = turned(here, 2)
+    for c in range(tiles):
+        E[c, pl.ds(r, SUB), :] = rows_at(E, c, r) + rows_at(T, c, r) * (ahead[c] - here[c])
+        north = rows_at(S, c, r + 1) - rows_at(S, c, r - 1)
+        N[c, pl.ds(r, SUB), :] = rows_at(N, c, r) + rows_at(Q, c, r) * north
+
+
+def ahead_surface_rows(refs, r, tiles, step):
+    S, E, N, _, _, W = refs
+    here = [rows_at(E, c, r) for c in range(tiles)]
+    behind = turned(here, -2)
+    for c in range(tiles):
+        hw = rows_at(W, c, r)
+        s = rows_at(S, c, r)
+        if step == 0:
+            s = s * (hw + hw)
+        north = rows_at(N, c, r + 1) - rows_at(N, c, r - 1)
+        S[c, pl.ds(r, SUB), :] = s + hw * ((here[c] - behind[c]) + north)
+    if step == STEPS - 1:
+        for c, value in enumerate(turned(here, -1)):
+            E[c, pl.ds(r, SUB), :] = value
 
 
 def loop_rows(count, body, unroll=64):
@@ -286,11 +322,11 @@
     )(ra, rbc, own)
 
 
-def interior_kernel(s, e, n, d, m, S, E, N, u, Q, W, isem):
+def interior_kernel(s, e, n, d, m, S, E, N, u, Q, T, W, isem):
     rows, cols = e.shape
     tiles = cols // LANES
     chunks = rows // CHUNK
-    refs = (S, E, N, Q, W)
+    refs = (S, E, N, Q, T, W)
     loads = []
     for k in range(chunks):
         loads.append([])
@@ -305,8 +341,10 @@
     zero_borders((S, N), rows, tiles)
 
     def first_flux(r):
-        ds = east_minus_west([rows_at(S, c, r) for c in range(tiles)])
         at = pl.ds(r - SUB, SUB)
+        here = [rows_at(S, c, r) for c in range(tiles)]
+        ahead = turned(here, 2)
+        flux, factor = [], []
         for c in range(tiles):
             to = slice(c * LANES, (c + 1) * LANES)
             wet = m[at, to].astype(F32)
@@ -314,8 +352,13 @@
             q = d[at, to] * hw
             W[c, pl.ds(r, SUB), :] = hw
             Q[c, pl.ds(r, SUB), :] = q
-            E[c, pl.ds(r, SUB), :] = e[at, to] * wet + q * ds[c]
-            N[c, pl.ds(r, SUB), :] = n[at, to] * wet + q * (rows_at(S, c, r + 1) - rows_at(S, c, r - 1))
+            north = rows_at(S, c, r + 1) - rows_at(S, c, r - 1)
+            N[c, pl.ds(r, SUB), :] = n[at, to] * wet + q * north
+            flux.append(e[at, to] * wet)
+            factor.append(q)
+        for c, (e1, q1) in enumerate(zip(turned(flux, 1), turned(factor, 1))):
+            T[c, pl.ds(r, SUB), :] = q1
+            E[c, pl.ds(r, SUB), :] = e1 + q1 * (ahead[c] - here[c])
 
     def over_chunk(k, body):
         def shifted(r):
@@ -328,10 +371,10 @@
         if k + 1 < chunks:
             wait_all(loads[k + 1])
         over_chunk(k, first_flux)
-    loop_rows(rows // SUB, lambda r: surface_rows(refs, r, tiles, True))
-    for _ in range(1, STEPS):
-        loop_rows(rows // SUB, lambda r: flux_rows(refs, r, tiles))
-        loop_rows(rows // SUB, lambda r: surface_rows(refs, r, tiles, False))
+    loop_rows(rows // SUB, lambda r: ahead_surface_rows(refs, r, tiles, 0))
+    for step in range(1, STEPS):
+        loop_rows(rows // SUB, lambda r: ahead_flux_rows(refs, r, tiles))
+        loop_rows(rows // SUB, lambda r: ahead_surface_rows(refs, r, tiles, step))
     points = rows // SPACING
     cell = lax.broadcasted_iota(jnp.int32, (points, rows), 1)
     table = spline_of(cell, lax.broadcasted_iota(jnp.int32, (points, rows), 0))
@@ -349,7 +392,7 @@
         out_shape=[jax.ShapeDtypeStruct(field, F32)] * 3 + [jax.ShapeDtypeStruct((rows // SPACING, cols), F32)],
         in_specs=[ANY] + [VMEM] * 4,
         out_specs=[VMEM] * 4,
-        scratch_shapes=[pltpu.VMEM(field, F32)] * 2 + [pltpu.SemaphoreType.DMA((rows // CHUNK,))],
+        scratch_shapes=[pltpu.VMEM(field, F32)] * 3 + [pltpu.SemaphoreType.DMA((rows // CHUNK,))],
         cost_estimate=pl.CostEstimate(flops=40 * rows * cols, bytes_accessed=32 * rows * cols, transcendentals=0),
         compiler_params=PARAMS,
         name="interior",
@@ -398,9 +441,63 @@
                     value = src[f * HALO + r : f * HALO + r + SUB, c * LANES : (c + 1) * LANES]
                     dst[c, here, :] = value
                 W[c, here, :] = jnp.where(value > 0.0, COURANT, 0.0)
+
+    height = rows + 2 * HALO
+    column = (S1, E1, N1, Q1, W1)
+    lon_even = is_even("lon")
+    zero_borders((S1, N1), height, 1)
+    group = lax.div(lane_index(), HALO)
+
+    def unpack(r):
+        at = pl.ds(r - SUB, SUB)
+        c, d = rc[at, :], rd[at, :]
+        right, left = jnp.where(lon_even, c, d), jnp.where(lon_even, d, c)
+        for f, dst in enumerate((S1, E1, N1, Q1)):
+            a, b = right, left
+            if f:
+                a, b = pltpu.roll(a, LANES - f * HALO, 1), pltpu.roll(b, LANES - f * HALO, 1)
+            t = r - SUB
+            if t < HALO:
+                middle = ends[0, f, t : t + SUB, :]
+            elif t < HALO + rows:
+                middle = own[f, t - HALO : t - HALO + SUB, :]
+            else:
+                middle = ends[1, f, t - HALO - rows : t - HALO - rows + SUB, :]
+            tile = jnp.where(group == 2, a, jnp.where(group == 3, b, middle))
+            dst[0, pl.ds(r, SUB), :] = tile
+            if f == 3:
+                W1[0, pl.ds(r, SUB), :] = jnp.where(tile > 0.0, COURANT, 0.0)
+
+    loop_rows(height // SUB, unpack, height)
+    lane = lane_index()
+
+    def merge(fields):
+        def body(r, i=None):
+            at = pl.ds(r - SUB, SUB)
+            for f in fields:
+                tile = column[f][0, pl.ds(r + HALO, SUB), :]
+                src, row = ((si, ei, ni)[f], r) if i is None else ((S, E, N)[f], i)
+                first, last = (src[end * (tiles - 1), pl.ds(row, SUB), :] for end in range(2))
+                X[f, 0, at, :] = jnp.where(lane < EDGE, tile, first)
+                X[f, 1, at, :] = jnp.where(lane >= LANES - EDGE, pltpu.roll(tile, LANES // 2, 1), last)
+
+        loop_rows(rows // SUB, body, 32)
+        body(SUB, SUB + HALO)
+        body(rows, SUB + STRIP + keep - SUB)
+        for f in fields:
+            for end, col in enumerate((0, cols - LANES)):
+                copy = pltpu.make_async_copy(X.at[f, end], (so, eo, no)[f].at[:, col : col + LANES], osem.at[0])
+                copy.start()
+                sends.append(copy)
+
     for step in range(STEPS):
-        loop_rows(count // SUB, lambda r: flux_rows(refs, r, tiles), 12)
-        loop_rows(count // SUB, lambda r: surface_rows(refs, r, tiles, step == 0), 12)
+        loop_rows(count // SUB, lambda r: flux_rows(refs, r, tiles))
+        loop_rows(height // SUB, lambda r: flux_rows(column, r, 1))
+        if step == STEPS - 1:
+            merge((1, 2))
+        loop_rows(count // SUB, lambda r: surface_rows(refs, r, tiles, step == 0))
+        loop_rows(height // SUB, lambda r: surface_rows(column, r, 1, step == 0))
+    merge((0,))
     for src, dst in ((S, so), (E, eo), (N, no)):
         for frm, to in ((SUB + HALO, 0), (SUB + STRIP + keep - SUB, rows - SUB)):
             for c in range(tiles):
@@ -437,61 +534,6 @@
     for c in range(tiles):
         piece = jnp.where(lane < reach, product[c * points : (c + 1) * points], 0.0)
         total = total + pltpu.roll(piece, (c * (LANES // SPACING) - 2) % LANES, 1)
-
-    height = rows + 2 * HALO
-    refs = column = (S1, E1, N1, Q1, W1)
-    even = is_even("lon")
-    zero_borders((S1, N1), height, 1)
-    group = lax.div(lane_index(), HALO)
-
-    def unpack(r):
-        at = pl.ds(r - SUB, SUB)
-        c, d = rc[at, :], rd[at, :]
-        right, left = jnp.where(even, c, d), jnp.where(even, d, c)
-        for f, dst in enumerate((S1, E1, N1, Q1)):
-            a, b = right, left
-            if f:
-                a, b = pltpu.roll(a, LANES - f * HALO, 1), pltpu.roll(b, LANES - f * HALO, 1)
-            t = r - SUB
-            if t < HALO:
-                middle = ends[0, f, t : t + SUB, :]
-            elif t < HALO + rows:
-                middle = own[f, t - HALO : t - HALO + SUB, :]
-            else:
-                middle = ends[1, f, t - HALO - rows : t - HALO - rows + SUB, :]
-            tile = jnp.where(group == 2, a, jnp.where(group == 3, b, middle))
-            dst[0, pl.ds(r, SUB), :] = tile
-            if f == 3:
-                W1[0, pl.ds(r, SUB), :] = jnp.where(tile > 0.0, COURANT, 0.0)
-
-    loop_rows(height // SUB, unpack, height)
-    lane = lane_index()
-
-    def merge(fields):
-        def body(r, i=None):
-            at = pl.ds(r - SUB, SUB)
-            for f in fields:
-                tile = column[f][0, pl.ds(r + HALO, SUB), :]
-                src, row = ((si, ei, ni)[f], r) if i is None else ((S, E, N)[f], i)
-                first, last = (src[end * (tiles - 1), pl.ds(row, SUB), :] for end in range(2))
-                X[f, 0, at, :] = jnp.where(lane < EDGE, tile, first)
-                X[f, 1, at, :] = jnp.where(lane >= LANES - EDGE, pltpu.roll(tile, LANES // 2, 1), last)
-
-        loop_rows(rows // SUB, body, 32)
-        body(SUB, SUB + HALO)
-        body(rows, SUB + STRIP + keep - SUB)
-        for f in fields:
-            for end, col in enumerate((0, cols - LANES)):
-                copy = pltpu.make_async_copy(X.at[f, end], (so, eo, no)[f].at[:, col : col + LANES], osem.at[0])
-                copy.start()
-                sends.append(copy)
-
-    for step in range(STEPS):
-        loop_rows(height // SUB, lambda r: flux_rows(refs, r, 1), 40)
-        if step == STEPS - 1:
-            merge((1, 2))
-        loop_rows(height // SUB, lambda r: surface_rows(refs, r, 1, step == 0), 40)
-    merge((0,))
     points, across = grad.shape
     cell = lax.broadcasted_iota(jnp.int32, (points, height), 1) - HALO
     table = spline_of(cell, lax.broadcasted_iota(jnp.int32, (points, height), 0))

time: 30 us -> 29.8 us (level)
  Pallas kernels: 11.5 us -> 10.7 us
  waiting for transfers between devices: 6.8 us -> 7.35 us
    ppermute x5, waiting for transfers between devices: 6.8 us -> 7.35 us  [swap(): return lax.ppermute(array, axis, pairs)]
    pallas_call x1, Pallas kernels: 4.26 us -> 3.71 us  [interior(): pl.pallas_call(interior_kernel, out_shape=[jax.ShapeDtypeStruct(field, F3...]
  transfers between devices with their start and end apart: 5 -> 5, of which waited for: 2 -> 2; matrix products, arithmetic and copies ran while one was open for 0% -> 0% of each run, Pallas kernels for 18% -> 16%
where the time goes in v6:
time: 29.8 us; the launch traced here: 29.6 us
  Pallas kernels  10.7 us (36%)
  starting transfers between devices  9.51 us (32%)
  waiting for transfers between devices  7.35 us (25%)
  local copies, waits for them, and re-layouts  1.29 us (4%)
  between operations  0.76 us (3%)
    ppermute x5, starting transfers between devices, swap(): return lax.ppermute(array, axis, pairs)  9.51 us
    ppermute x5, waiting for transfers between devices, swap(): return lax.ppermute(array, axis, pairs)  7.35 us
    pallas_call x1, Pallas kernels, borders(): pl.pallas_call(border_kernel, out_shape=[field] * 3 + [jax.ShapeDtypeStru...  4.58 us
    pallas_call x1, Pallas kernels, interior(): pl.pallas_call(interior_kernel, out_shape=[jax.ShapeDtypeStruct(field, F3...  3.71 us
    pallas_call x1, Pallas kernels, pack_first(): pl.pallas_call(pack_first_kernel, out_shape=[jax.ShapeDtypeStruct((4 * HA...  1.43 us
    unnamed x10, local copies, waits for them, and re-layouts  1.29 us
  transfers between devices with their start and end apart: 5, of which 2 were waited for; matrix products, arithmetic and copies ran while one was open for 0% of the time, Pallas kernels for 16%

profile of v6, /device:TPU:10, one launch (start us, length us, event | category | flops | bytes accessed | tf_op | source)
XLA Modules:
  0.0 29.6 jit_solution(7368183445009835833)
XLA Ops:
  0.6 0.0 copy-start.4
  0.6 0.0 copy-start.3
  0.7 0.0 copy-start.2
  0.7 0.0 copy-start.1
  0.7 0.0 copy-start
  0.7 1.4 %pack_first.1 = (f32[128,1024]{1,0:T(8,128)S(1)}, f32[64,128]{1,0:T(8,128)S(1)}) custom-call(f32[256,1024]{1,0:T(8,128)} %s.7, f32[256,1024]{1,0:T(8,128)} %e.7, f32[256,1024]{1,0:T(8,128)} %n.7, f32[256,1024]{1,0:T(8,128)} %d.7, s32[256,1024]{1,0:T(8,128)} %m.7), custom_call_target="tpu_custom_call" | custom-call | tf_op jit(solution)/shard_map/pack_first/pallas_call | solution.py:207
  2.1 0.1 collective-permute-start
  2.2 0.0 copy-done.4
  2.2 0.3 %copy-done.3 = f32[256,1024]{1,0:T(8,128)S(1)} copy-done((f32[256,1024]{1,0:T(8,128)S(1)}, f32[256,1024]{1,0:T(8,128)}, u32[]{:S(2)}) %copy-start.3) | copy-done | bytes 1048600
  2.5 0.3 %copy-done.2 = f32[256,1024]{1,0:T(8,128)S(1)} copy-done((f32[256,1024]{1,0:T(8,128)S(1)}, f32[256,1024]{1,0:T(8,128)}, u32[]{:S(2)}) %copy-start.2) | copy-done | bytes 1048600
  2.8 0.3 %copy-done.1 = f32[256,1024]{1,0:T(8,128)S(1)} copy-done((f32[256,1024]{1,0:T(8,128)S(1)}, f32[256,1024]{1,0:T(8,128)}, u32[]{:S(2)}) %copy-start.1) | copy-done | bytes 1048600
  3.2 0.3 %copy-done = f32[256,1024]{1,0:T(8,128)S(1)} copy-done((f32[256,1024]{1,0:T(8,128)S(1)}, f32[256,1024]{1,0:T(8,128)}, u32[]{:S(2)}) %copy-start) | copy-done | bytes 1048600
  3.5 0.5 %edges.1 = (f32[128,1024]{1,0:T(8,128)S(1)}, f32[4,256,128]{2,1,0:T(8,128)S(1)}) custom-call(f32[256,1024]{1,0:T(8,128)S(1)} %copy-done, f32[256,1024]{1,0:T(8,128)S(1)} %copy-done.1, f32[256,1024]{1,0:T(8,128)S(1)} %copy-done.2, f32[256,1024]{1,0:T(8,128)S(1)} %copy-done.3, s32[256,1024]{1,0:T(8,128)S(1)} %copy-done.4), custom_call_target="tpu_custom_call" | custom-call | tf_op jit(solution)/shard_map/edges/pallas_call | solution.py:266
  3.9 1.9 %collective-permute-start.1 = (f32[128,1024]{1,0:T(8,128)S(1)}, f32[128,1024]{1,0:T(8,128)S(1)}, u32[]{:S(2)}, u32[]{:S(2)}) collective-permute-start(f32[128,1024]{1,0:T(8,128)S(1)} %get-tuple-element.16), channel_id=1, source_target_pairs={{1,2},{2,1},{5,6},{6,5},{9,10},{10,9},{13,14},{14,13},{17,18},{18,... | collective-permute-start | bytes 1572872 | tf_op jit(solution)/shard_map/ppermute | solution.py:581
  5.9 3.6 %collective-permute-start.2 = (f32[64,128]{1,0:T(8,128)S(1)}, f32[64,128]{1,0:T(8,128)S(1)}, u32[]{:S(2)}, u32[]{:S(2)}) collective-permute-start(f32[64,128]{1,0:T(8,128)S(1)} %get-tuple-element.21), channel_id=1, source_target_pairs={{1,2},{2,1},{5,6},{6,5},{9,10},{10,9},{13,14},{14,13},{17,18},{18,... | collective-permute-start | bytes 98312 | tf_op jit(solution)/shard_map/ppermute | solution.py:581
  9.5 5.3 %collective-permute-done.2.rbc = f32[64,128]{1,0:T(8,128)S(1)} collective-permute-done((f32[64,128]{1,0:T(8,128)S(1)}, f32[64,128]{1,0:T(8,128)S(1)}, u32[]{:S(2)}, u32[]{:S(2)}) %collective-permute-start.2) | collective-permute-done | bytes 32800 | tf_op jit(solution)/shard_map/ppermute | solution.py:581
  14.8 0.0 collective-permute-done.ra
  14.8 0.5 %corners.1 = (f32[320,128]{1,0:T(8,128)S(1)}, f32[320,128]{1,0:T(8,128)S(1)}, f32[2,4,32,128]{3,2,1,0:T(8,128)S(1)}) custom-call(f32[128,1024]{1,0:T(8,128)S(1)} %collective-permute-done.ra, f32[64,128]{1,0:T(8,128)S(1)} %collective-permute-done.2.rbc, f32[4,256,128]{2,1,0:T(8,128)S(1)} %get-tuple-element.22.own), custom_call_target="tpu_custom_call" | custom-call | tf_op jit(solution)/shard_map/corners/pallas_call | solution.py:315
  15.3 1.6 %collective-permute-start.3 = (f32[320,128]{1,0:T(8,128)S(1)}, f32[320,128]{1,0:T(8,128)S(1)}, u32[]{:S(2)}, u32[]{:S(2)}) collective-permute-start(f32[320,128]{1,0:T(8,128)S(1)} %get-tuple-element.23), channel_id=1, source_target_pairs={{0,4},{4,0},{8,12},{12,8},{16,20},{20,16},{24,28},{28,24},{1,5},{5... | collective-permute-start | bytes 491528 | tf_op jit(solution)/shard_map/ppermute | solution.py:581
  16.9 2.3 %collective-permute-start.4 = (f32[320,128]{1,0:T(8,128)S(1)}, f32[320,128]{1,0:T(8,128)S(1)}, u32[]{:S(2)}, u32[]{:S(2)}) collective-permute-start(f32[320,128]{1,0:T(8,128)S(1)} %get-tuple-element.24), channel_id=1, source_target_pairs={{4,8},{8,4},{12,16},{16,12},{20,24},{24,20},{5,9},{9,5},{13,17},{1... | collective-permute-start | bytes 491528 | tf_op jit(solution)/shard_map/ppermute | solution.py:581
  19.2 3.7 %interior.1 = (f32[8,272,128]{2,1,0:T(8,128)S(1)}, f32[8,272,128]{2,1,0:T(8,128)S(1)}, f32[8,272,128]{2,1,0:T(8,128)S(1)}, f32[16,1024]{1,0:T(8,128)S(1)}) custom-call(f32[256,1024]{1,0:T(8,128)S(1)} %copy-done, f32[256,1024]{1,0:T(8,128)S(1)} %copy-done.1, f32[256,1024]{1,0:T(8,128)S(1)} %copy-done.2, f32[256,1024]{1,0:T(8,128)S(1)} %copy-done.3, ...), custom_call_target="tpu_custom_call" | custom-call | flops 10485760 | bytes 8388608 | tf_op jit(solution)/shard_map/interior/pallas_call | solution.py:390
  22.9 0.0 collective-permute-done.1.rb
  22.9 0.0 collective-permute-done.3.rc
  23.0 2.1 %collective-permute-done.4.rd = f32[320,128]{1,0:T(8,128)S(1)} collective-permute-done((f32[320,128]{1,0:T(8,128)S(1)}, f32[320,128]{1,0:T(8,128)S(1)}, u32[]{:S(2)}, u32[]{:S(2)}) %collective-permute-start.4) | collective-permute-done | bytes 163872 | tf_op jit(solution)/shard_map/ppermute | solution.py:581
  25.0 4.6 %borders.1 = (f32[256,1024]{1,0:T(8,128)}, f32[256,1024]{1,0:T(8,128)}, f32[256,1024]{1,0:T(8,128)}, f32[16,64]{1,0:T(8,128)}) custom-call(f32[256,1024]{1,0:T(8,128)S(1)} %copy-done, f32[256,1024]{1,0:T(8,128)S(1)} %copy-done.1, f32[256,1024]{1,0:T(8,128)S(1)} %copy-done.2, f32[256,1024]{1,0:T(8,128)S(1)} %copy-done.3, s32[256,1024]{1,0:T(8,128)S(1)} %copy-done.4, ...), custom_call_target="tpu_custom_call" | custom-call | flops 5242880 | bytes 4194304 | tf_op jit(solution)/shard_map/borders/pallas_call | solution.py:555
Async XLA Ops:
  0.6 1.6 %copy-start.4 = (s32[256,1024]{1,0:T(8,128)S(1)}, s32[256,1024]{1,0:T(8,128)}, u32[]{:S(2)}) copy-start(s32[256,1024]{1,0:T(8,128)} %m.7) | copy-start | bytes 3145732
  0.6 1.9 %copy-start.3 = (f32[256,1024]{1,0:T(8,128)S(1)}, f32[256,1024]{1,0:T(8,128)}, u32[]{:S(2)}) copy-start(f32[256,1024]{1,0:T(8,128)} %d.7) | copy-start | bytes 3145732
  0.7 2.2 %copy-start.2 = (f32[256,1024]{1,0:T(8,128)S(1)}, f32[256,1024]{1,0:T(8,128)}, u32[]{:S(2)}) copy-start(f32[256,1024]{1,0:T(8,128)} %n.7) | copy-start | bytes 3145732
  0.7 2.5 %copy-start.1 = (f32[256,1024]{1,0:T(8,128)S(1)}, f32[256,1024]{1,0:T(8,128)}, u32[]{:S(2)}) copy-start(f32[256,1024]{1,0:T(8,128)} %e.7) | copy-start | bytes 3145732
  0.7 2.8 %copy-start = (f32[256,1024]{1,0:T(8,128)S(1)}, f32[256,1024]{1,0:T(8,128)}, u32[]{:S(2)}) copy-start(f32[256,1024]{1,0:T(8,128)} %s.7) | copy-start | bytes 3145732
  2.1 12.7 %collective-permute-start = (f32[128,1024]{1,0:T(8,128)S(1)}, f32[128,1024]{1,0:T(8,128)S(1)}, u32[]{:S(2)}, u32[]{:S(2)}) collective-permute-start(f32[128,1024]{1,0:T(8,128)S(1)} %get-tuple-element.15), channel_id=1, source_target_pairs={{0,1},{1,0},{2,3},{3,2},{4,5},{5,4},{6,7},{7,6},{8,9},{9,8},{10,11... | collective-permute-start | bytes 1572872 | tf_op jit(solution)/shard_map/ppermute | solution.py:581
  3.9 19.0 %collective-permute-start.1 = (f32[128,1024]{1,0:T(8,128)S(1)}, f32[128,1024]{1,0:T(8,128)S(1)}, u32[]{:S(2)}, u32[]{:S(2)}) collective-permute-start(f32[128,1024]{1,0:T(8,128)S(1)} %get-tuple-element.16), channel_id=1, source_target_pairs={{1,2},{2,1},{5,6},{6,5},{9,10},{10,9},{13,14},{14,13},{17,18},{18,... | collective-permute-start | bytes 1572872 | tf_op jit(solution)/shard_map/ppermute | solution.py:581
  5.9 8.9 %collective-permute-start.2 = (f32[64,128]{1,0:T(8,128)S(1)}, f32[64,128]{1,0:T(8,128)S(1)}, u32[]{:S(2)}, u32[]{:S(2)}) collective-permute-start(f32[64,128]{1,0:T(8,128)S(1)} %get-tuple-element.21), channel_id=1, source_target_pairs={{1,2},{2,1},{5,6},{6,5},{9,10},{10,9},{13,14},{14,13},{17,18},{18,... | collective-permute-start | bytes 98312 | tf_op jit(solution)/shard_map/ppermute | solution.py:581
  15.3 7.6 %collective-permute-start.3 = (f32[320,128]{1,0:T(8,128)S(1)}, f32[320,128]{1,0:T(8,128)S(1)}, u32[]{:S(2)}, u32[]{:S(2)}) collective-permute-start(f32[320,128]{1,0:T(8,128)S(1)} %get-tuple-element.23), channel_id=1, source_target_pairs={{0,4},{4,0},{8,12},{12,8},{16,20},{20,16},{24,28},{28,24},{1,5},{5... | collective-permute-start | bytes 491528 | tf_op jit(solution)/shard_map/ppermute | solution.py:581
  16.9 8.1 %collective-permute-start.4 = (f32[320,128]{1,0:T(8,128)S(1)}, f32[320,128]{1,0:T(8,128)S(1)}, u32[]{:S(2)}, u32[]{:S(2)}) collective-permute-start(f32[320,128]{1,0:T(8,128)S(1)} %get-tuple-element.24), channel_id=1, source_target_pairs={{4,8},{8,4},{12,16},{16,12},{20,24},{24,20},{5,9},{9,5},{13,17},{1... | collective-permute-start | bytes 491528 | tf_op jit(solution)/shard_map/ppermute | solution.py:581
